TPU v7x, 256 devices: a whole 4x4x8 slice. The times are simulated.
256 devices in a mesh: space: 64 (over x, y, z_lo), load: 4 (over z_hi, core).
Axes of the slice: x: 4, y: 4, z: 8 (z_hi: 2, z_lo: 4; z = z_hi * 4 + z_lo), core: 2. Of those that a mesh axis runs over, the one named last changes fastest.
Arguments:
- load_force: float32 [4, 3, 512, 16, 256], P('load', None, 'space'), may hold values from -6 to 6
- stiffness: float32 [512, 16, 256], P('space'), may hold values from 0.5 to 4
- material: int32 [64, 2], P('space'), may hold values from 0 to 2
- face_src: int32 [64, 64, 256], P('space'), may hold values from 0 to 32767
- face_count: int32 [64, 64], P('space'), may hold values from 0 to 256, as said below
- face_dst: int32 [64, 64, 256], P('space'), may hold values from 0 to 4095
Outputs:
- displacement: float32 [4, 3, 512, 16, 256], P('load', None, 'space')
- sensitivity: float32 [3, 512, 16, 256], P(None, 'space', 'load')
Inputs may be any that keep to these rules, and one draw needn't show every extreme that they name: face_count[s, o] counts the live first slots from slab s to owner o; in every row one owner gets all 256.
All inputs are finite; a program needn't handle non-finite values.
Results may differ from a plain program's by a relative error of at most 0.0001.
Values sent between devices are 32-bit elements; how exact they have to be, the bound alone decides.
No kernel may reach another device: no remote copies, remote signals or barrier semaphores. Data moves between devices by JAX's collectives and lax.ppermute only.
A program may use at most 192 MiB of HBM per device.

v0:
```python
import jax
import jax.numpy as jnp
from jax import lax
from jax.sharding import PartitionSpec as P

NY = 16
BY = 8
SLOTS = 256
FINE_STEPS = 3
COARSE_STEPS = 4


UPPER_EDGE = 2.1
LOWER_EDGE = 0.15
COUPLING = 0.1
MODULI = (1.0, 0.55, 0.25)


def extended(block, sides, width):
    for axis, dim in sides:
        count = lax.axis_size(axis)
        forward = [(i, i + 1) for i in range(count - 1)]
        backward = [(target, source) for source, target in forward]
        low = lax.ppermute(
            lax.slice_in_dim(block, block.shape[dim] - width, None, axis=dim), axis, forward
        )
        high = lax.ppermute(lax.slice_in_dim(block, 0, width, axis=dim), axis, backward)
        block = jnp.concatenate([low, block, high], axis=dim)
    return block


def neighbour_list():
    entries = []
    for shift_x in (-1, 0, 1):
        for shift_y in (-1, 0, 1):
            for shift_z in (-1, 0, 1):
                reach_len = abs(shift_x) + abs(shift_y) + abs(shift_z)
                if reach_len > 0:
                    entries.append(
                        (shift_x, shift_y, shift_z, (1.0, 0.5, 0.25)[reach_len - 1] / 14.0)
                    )
    return entries


def window(padded, shift_x, shift_y, shift_z, inner_shape):
    size_x, size_y, size_z = inner_shape
    return padded[
        :,
        1 + shift_x : 1 + shift_x + size_x,
        1 + shift_y : 1 + shift_y + size_y,
        1 + shift_z : 1 + shift_z + size_z,
    ]


def operate(padded_field, padded_coef):
    inner_shape = (padded_field.shape[1] - 2, padded_field.shape[2] - 2, padded_field.shape[3] - 2)
    centre = window(padded_field, 0, 0, 0, inner_shape)
    coef_mid = window(padded_coef, 0, 0, 0, inner_shape)
    result = jnp.zeros_like(centre)
    for shift_x, shift_y, shift_z, weight in neighbour_list():
        face_coef = 0.5 * (coef_mid + window(padded_coef, shift_x, shift_y, shift_z, inner_shape))
        result = result + weight * face_coef * (
            centre - window(padded_field, shift_x, shift_y, shift_z, inner_shape)
        )
    pieces = []
    for component in range(3):
        mixed_term = jnp.zeros_like(coef_mid[0])
        for partner in range(3):
            if partner != component:
                for sign_a in (1, -1):
                    for sign_b in (1, -1):
                        offset = [0, 0, 0]
                        offset[component] += sign_a
                        offset[partner] += sign_b
                        mixed_term = (
                            mixed_term
                            + 0.25
                            * sign_a
                            * sign_b
                            * window(
                                padded_field[partner : partner + 1],
                                offset[0],
                                offset[1],
                                offset[2],
                                inner_shape,
                            )[0]
                        )
        pieces.append(result[component] - COUPLING * coef_mid[0] * mixed_term)
    return jnp.stack(pieces)


def diagonal_of(padded_coef):
    inner_shape = (padded_coef.shape[1] - 2, padded_coef.shape[2] - 2, padded_coef.shape[3] - 2)
    coef_mid = window(padded_coef, 0, 0, 0, inner_shape)
    total_sum = jnp.zeros_like(coef_mid)
    for shift_x, shift_y, shift_z, weight in neighbour_list():
        total_sum = total_sum + weight * 0.5 * (
            coef_mid + window(padded_coef, shift_x, shift_y, shift_z, inner_shape)
        )
    return total_sum


def pad_sides(grid_field):
    return jnp.pad(grid_field, ((0, 0), (0, 0), (1, 1), (1, 1)))


def chebyshev(source, padded_coef, diagonal, sweep_count, widen):
    midpoint = (UPPER_EDGE + LOWER_EDGE) / 2.0
    halfwidth = (UPPER_EDGE - LOWER_EDGE) / 2.0
    spread_ratio = midpoint / halfwidth
    rho_old = 1.0 / spread_ratio
    update = source / (midpoint * diagonal)
    solution = update
    for sweep_idx in range(1, sweep_count):
        residual = source - operate(widen(solution), padded_coef)
        rho_new = 1.0 / (2.0 * spread_ratio - rho_old)
        update = rho_new * rho_old * update + 2.0 * rho_new / halfwidth * residual / diagonal
        solution = solution + update
        rho_old = rho_new
    return solution


def coarsen(grid_field):
    comps, size_x, size_y, size_z = grid_field.shape
    return grid_field.reshape(comps, size_x // 2, 2, size_y // 2, 2, size_z // 2, 2).mean(
        axis=(2, 4, 6)
    )


def refine(grid_field):
    return jnp.repeat(jnp.repeat(jnp.repeat(grid_field, 2, axis=1), 2, axis=2), 2, axis=3)


def modulus_rows(material, brick_rows):
    onehot = (material[..., None] == jnp.arange(len(MODULI), dtype=jnp.int32)).astype(jnp.float32)
    values = jnp.sum(onehot * jnp.array(MODULI, jnp.float32), axis=-1)
    return jnp.repeat(values, brick_rows, axis=-1)


def widen_fine(grid_field):
    planes = extended(grid_field, (("space", 1),), 1)
    return pad_sides(planes)


def body(load_force, stiffness, material, face_src, face_count, face_dst):
    own_cells = modulus_rows(material, BY)[0][None, :, None]
    coef = stiffness * own_cells
    padded_coef = widen_fine(coef[None])
    diag_fine = diagonal_of(padded_coef)
    coarse_coef = coarsen(coef[None])

    def widen_coarse(grid_field):
        planes = extended(grid_field, (("space", 1),), 1)
        return pad_sides(planes)

    padded_coarse = widen_coarse(coarse_coef)
    diag_coarse = diagonal_of(padded_coarse)
    live_mask = (jnp.arange(SLOTS, dtype=jnp.int32)[None, :] < face_count[0][:, None]).astype(
        jnp.float32
    )
    source = load_force[0]
    smooth = chebyshev(source, padded_coef, diag_fine, FINE_STEPS, widen_fine)
    smooth, residual = (smooth, source - operate(widen_fine(smooth), padded_coef))
    coarse_source = 4.0 * coarsen(residual)
    picked = residual.reshape(3, -1)[:, face_src[0]] * live_mask[None]
    arrived = lax.all_to_all(picked, "space", split_axis=1, concat_axis=1, tiled=True)
    coarse_source = (
        coarse_source.reshape(3, -1).at[:, face_dst[0]].add(arrived).reshape(coarse_source.shape)
    )
    displaced = smooth + refine(
        chebyshev(coarse_source, padded_coarse, diag_coarse, COARSE_STEPS, widen_coarse)
    )
    image = operate(widen_fine(displaced), padded_coef)
    energy = jnp.sum(displaced * image, axis=0)
    outputs = [displaced]
    rows_part = NY // lax.axis_size("load")
    start_row = lax.axis_index("load") * rows_part
    total_sum = lax.psum(energy, "load")
    energy_part = lax.dynamic_slice_in_dim(total_sum, start_row, rows_part, 1)
    own_part = lax.dynamic_slice_in_dim(own_cells, start_row, rows_part, 1)[None]
    moduli = jnp.array(MODULI, jnp.float32)[:, None, None, None]
    sensitivity = (moduli - own_part) / own_part * energy_part[None]
    return (jnp.stack(outputs), sensitivity)


def solution(mesh):
    return jax.shard_map(
        body,
        mesh=mesh,
        in_specs=(
            P("load", None, "space", None, None),
            P("space", None, None),
            P("space", None),
            P("space", None, None),
            P("space", None),
            P("space", None, None),
        ),
        out_specs=(P("load", None, "space", None, None), P(None, "space", "load", None)),
        check_vma=False,
    )
```

profile of v0, /device:TPU:1, one launch (start us, length us, event | category | flops | bytes accessed | tf_op | source)
XLA Modules:
  0.0 533.6 jit_solution(4295424980780647665)
XLA Ops:
  10.5 5.0 collective-permute-start
  16.5 9.8 %reshape_broadcast_in_dim.3 = f32[4,2,8,2,128,2]{5,4,3,2,1,0:T(8,128)} reshape(f32[8,16,256]{2,1,0:T(8,128)S(1)} %broadcast_multiply_fusion.1) | data formatting | bytes 262144 | tf_op jit(solution)/shard_map/reshape;broadcast_in_dim | solution.py:125
  26.3 4.1 reduce_sum.38
  31.7 4.2 collective-permute-start.8
  37.3 26.5 %squeeze.11 = f32[3,4,2,8,2,128,2]{6,5,4,3,2,1,0:T(8,128)} reshape(f32[1,3,8,16,256]{4,3,2,1,0:T(8,128)S(1)} %copy-done) | data formatting | bytes 786432 | tf_op jit(solution)/shard_map/squeeze | solution.py:161
  63.9 8.6 %copy.310 = f32[1,3,8,16,256]{1,4,3,2,0:T(8,128)} copy(f32[1,3,8,16,256]{4,3,2,1,0:T(8,128)S(1)} %copy-done) | data formatting | bytes 786432 | tf_op args[0]
  76.2 4.2 collective-permute-start.2
  86.1 6.7 %collective-permute-start.4 = (f32[3,1,16,256]{3,2,1,0:T(8,128)S(1)}, f32[3,1,16,256]{3,2,1,0:T(8,128)S(1)}, u32[]{:S(2)}, u32[]{:S(2)}) collective-permute-start(f32[3,1,16,256]{3,2,1,0:T(8,128)S(1)} %get-tuple-element.56), channel_id=1, source_target_pairs={{0,4},{4,8},{8,12},{12,16},{16,20},{20,24},{24,28},{28,32},{32,36}... | collective-permute-start | bytes 147464 | tf_op jit(solution)/shard_map/ppermute | solution.py:24
  98.7 6.9 %collective-permute-start.6 = (f32[3,1,16,256]{3,2,1,0:T(8,128)S(1)}, f32[3,1,16,256]{3,2,1,0:T(8,128)S(1)}, u32[]{:S(2)}, u32[]{:S(2)}) collective-permute-start(f32[3,1,16,256]{3,2,1,0:T(8,128)S(1)} %get-tuple-element.54), channel_id=1, source_target_pairs={{0,4},{4,8},{8,12},{12,16},{16,20},{20,24},{24,28},{28,32},{32,36}... | collective-permute-start | bytes 147464 | tf_op jit(solution)/shard_map/ppermute | solution.py:24
  109.9 9.7 %stack.91 = f32[1,4,2,8,2,128,2]{6,5,4,3,2,1,0:T(8,128)} reshape(f32[1,8,16,256]{3,2,1,0:T(8,128)S(1)} %fusion.270) | data formatting | bytes 262144 | tf_op jit(solution)/shard_map/stack | solution.py:89
  119.6 9.7 %stack.90 = f32[1,4,2,8,2,128,2]{6,5,4,3,2,1,0:T(8,128)} reshape(f32[1,8,16,256]{3,2,1,0:T(8,128)S(1)} %get-tuple-element.23) | data formatting | bytes 262144 | tf_op jit(solution)/shard_map/stack | solution.py:89
  129.4 9.7 %stack.89 = f32[1,4,2,8,2,128,2]{6,5,4,3,2,1,0:T(8,128)} reshape(f32[1,8,16,256]{3,2,1,0:T(8,128)S(1)} %get-tuple-element.22) | data formatting | bytes 262144 | tf_op jit(solution)/shard_map/stack | solution.py:89
  139.9 8.6 %copy.311 = f32[3,32768]{0,1:T(8,128)} copy(f32[3,32768]{1,0:T(4,128)S(1)} %pad_maximum_fusion) | data formatting | bytes 786432 | tf_op jit(solution)/shard_map/stack | solution.py:89
  148.5 17.8 %bitcast_subtract_fusion = f32[3,32768]{0,1:T(8,128)} fusion(f32[3,32768]{0,1:T(8,128)} %copy.311, f32[1,3,8,16,256]{1,4,3,2,0:T(8,128)} %copy.310), kind=kLoop, calls=%fused_computation.4 | loop fusion | flops 98304 | bytes 1179648 | tf_op jit(solution)/shard_map/sub | solution.py:163
  166.3 60.5 %gather_fusion = f32[16384,3]{1,0:T(8,128)} fusion(f32[3,32768]{0,1:T(8,128)} %bitcast_subtract_fusion, s32[16384]{0:T(1024)S(1)} %copy-done.77), kind=kCustom, calls=%fused_computation | custom fusion | bytes 458752 | tf_op jit(solution)/shard_map/gather | solution.py:165
  226.8 5.4 %copy.312 = f32[64,256,3]{1,2,0:T(4,128)S(1)} copy(f32[64,256,3]{2,1,0:T(8,128)} %bitcast.288) | data formatting | bytes 393216 | tf_op jit(solution)/shard_map/gather | solution.py:165
  233.0 30.9 %all-to-all-start = ((f32[3,64,256]{2,0,1:T(4,128)}), f32[3,64,256]{2,0,1:T(4,128)S(1)}, u32[]{:S(2)}, u32[]{:S(2)}) async-start(f32[3,64,256]{2,0,1:T(4,128)} %multiply_bitcast_fusion), calls=%async_computation | async-start | bytes 524288 | tf_op jit(solution)/shard_map/all_to_all | solution.py:166
  263.9 16.1 %fusion = f32[3,4,8,128]{3,2,1,0:T(8,128)S(1)} fusion(f32[3,4,2,8,2,128,2]{6,5,4,3,2,1,0:T(8,128)} %squeeze.11, f32[1,4,2,8,2,128,2]{6,5,4,3,2,1,0:T(8,128)} %stack.91, f32[1,4,2,8,2,128,2]{6,5,4,3,2,1,0:T(8,128)} %stack.90, f32[1,4,2,8,2,128,2]{6,5,4,3,2,1,0:T(8,128)} %stack.89), kind=kLoop, calls=%fused_computation.3 | loop fusion | flops 380928 | bytes 835584 | tf_op jit(solution)/shard_map/reduce_sum | solution.py:125
  280.7 5.1 copy.313
  285.8 88.6 %scatter_fusion = f32[3,4096]{0,1:T(8,128)S(1)} fusion(f32[3,4096]{0,1:T(8,128)S(1)} %bitcast.286, s32[16384]{0:T(1024)S(1)} %bitcast.312, f32[16384,3]{1,0:T(8,128)} %copy.313), kind=kCustom, calls=%fused_computation.1 | custom fusion | flops 49152 | bytes 655360 | tf_op jit(solution)/shard_map/scatter-add | solution.py:168
  383.8 4.2 collective-permute-start.12
  390.9 4.2 collective-permute-start.14
  406.1 5.8 %collective-permute-start.16 = (f32[3,1,16,256]{3,2,1,0:T(8,128)}, f32[3,1,16,256]{3,2,1,0:T(8,128)}, u32[]{:S(2)}, u32[]{:S(2)}) collective-permute-start(f32[3,1,16,256]{3,2,1,0:T(8,128)} %get-tuple-element.52), channel_id=1, source_target_pairs={{0,4},{4,8},{8,12},{12,16},{16,20},{20,24},{24,28},{28,32},{32,36}... | collective-permute-start | bytes 147464 | tf_op jit(solution)/shard_map/ppermute | solution.py:24
  422.9 101.1 %all-reduce.11.cloned.1.call-done = f32[8,16,256]{1,0,2:T(8,128)} async-done(((f32[8,16,256]{1,0,2:T(8,128)}), f32[8,16,256]{1,0,2:T(8,128)}) %all-reduce.11.cloned.1.call-update) | async-done | bytes 131088 | tf_op jit(solution)/shard_map/psum | solution.py:178
  (309 shorter events, 64.0 us)
Async XLA Ops:
  8.2 75.9 %copy-start.79 = (f32[16]{0:T(128)}, f32[16]{0:T(128)S(1)}, u32[]{:S(2)}) copy-start(f32[16]{0:T(128)S(1)} %broadcast_in_dim.30) | copy-start | bytes 196
  9.2 64.1 %collective-permute-start.1 = (f32[1,1,16,256]{3,2,1,0:T(8,128)S(1)}, f32[1,1,16,256]{3,2,1,0:T(8,128)S(1)}, u32[]{:S(2)}, u32[]{:S(2)}) collective-permute-start(f32[1,1,16,256]{3,2,1,0:T(8,128)S(1)} %get-tuple-element.69), channel_id=1, source_target_pairs={{4,0},{8,4},{12,8},{16,12},{20,16},{24,20},{28,24},{32,28},{36,32}... | collective-permute-start | bytes 49160 | tf_op jit(solution)/shard_map/ppermute | solution.py:27
  10.5 62.8 %collective-permute-start = (f32[1,1,16,256]{3,2,1,0:T(8,128)S(1)}, f32[1,1,16,256]{3,2,1,0:T(8,128)S(1)}, u32[]{:S(2)}, u32[]{:S(2)}) collective-permute-start(f32[1,1,16,256]{3,2,1,0:T(8,128)S(1)} %get-tuple-element.68), channel_id=1, source_target_pairs={{0,4},{4,8},{8,12},{12,16},{16,20},{20,24},{24,28},{28,32},{32,36}... | collective-permute-start | bytes 49160 | tf_op jit(solution)/shard_map/ppermute | solution.py:24
  30.4 42.7 %collective-permute-start.9 = (f32[1,1,8,128]{3,2,1,0:T(8,128)S(1)}, f32[1,1,8,128]{3,2,1,0:T(8,128)S(1)}, u32[]{:S(2)}, u32[]{:S(2)}) collective-permute-start(f32[1,1,8,128]{3,2,1,0:T(8,128)S(1)} %get-tuple-element.103), channel_id=1, source_target_pairs={{4,0},{8,4},{12,8},{16,12},{20,16},{24,20},{28,24},{32,28},{36,32}... | collective-permute-start | bytes 12296 | tf_op jit(solution)/shard_map/ppermute | solution.py:27
  31.7 41.4 %collective-permute-start.8 = (f32[1,1,8,128]{3,2,1,0:T(8,128)S(1)}, f32[1,1,8,128]{3,2,1,0:T(8,128)S(1)}, u32[]{:S(2)}, u32[]{:S(2)}) collective-permute-start(f32[1,1,8,128]{3,2,1,0:T(8,128)S(1)} %get-tuple-element.102), channel_id=1, source_target_pairs={{0,4},{4,8},{8,12},{12,16},{16,20},{20,24},{24,28},{28,32},{32,36}... | collective-permute-start | bytes 12296 | tf_op jit(solution)/shard_map/ppermute | solution.py:24
  74.0 32.9 %copy-start.15 = (f32[8,16,256]{2,1,0:T(8,128)}, f32[8,16,256]{2,1,0:T(8,128)S(1)}, u32[]{:S(2)}) copy-start(f32[8,16,256]{2,1,0:T(8,128)S(1)} %get-tuple-element.28) | copy-start | bytes 393220
  74.0 32.9 %copy-start.17 = (f32[8,16,256]{2,1,0:T(8,128)}, f32[8,16,256]{2,1,0:T(8,128)S(1)}, u32[]{:S(2)}) copy-start(f32[8,16,256]{2,1,0:T(8,128)S(1)} %get-tuple-element.29) | copy-start | bytes 393220
  74.0 32.9 %copy-start.19 = (f32[8,16,256]{2,1,0:T(8,128)}, f32[8,16,256]{2,1,0:T(8,128)S(1)}, u32[]{:S(2)}) copy-start(f32[8,16,256]{2,1,0:T(8,128)S(1)} %get-tuple-element.30) | copy-start | bytes 393220
  74.9 5.8 %collective-permute-start.3 = (f32[3,1,16,256]{3,2,1,0:T(8,128)S(1)}, f32[3,1,16,256]{3,2,1,0:T(8,128)S(1)}, u32[]{:S(2)}, u32[]{:S(2)}) collective-permute-start(f32[3,1,16,256]{3,2,1,0:T(8,128)S(1)} %get-tuple-element.59), channel_id=1, source_target_pairs={{4,0},{8,4},{12,8},{16,12},{20,16},{24,20},{28,24},{32,28},{36,32}... | collective-permute-start | bytes 147464 | tf_op jit(solution)/shard_map/ppermute | solution.py:27
  76.2 5.3 %collective-permute-start.2 = (f32[3,1,16,256]{3,2,1,0:T(8,128)S(1)}, f32[3,1,16,256]{3,2,1,0:T(8,128)S(1)}, u32[]{:S(2)}, u32[]{:S(2)}) collective-permute-start(f32[3,1,16,256]{3,2,1,0:T(8,128)S(1)} %get-tuple-element.58), channel_id=1, source_target_pairs={{0,4},{4,8},{8,12},{12,16},{16,20},{20,24},{24,28},{28,32},{32,36}... | collective-permute-start | bytes 147464 | tf_op jit(solution)/shard_map/ppermute | solution.py:24
  84.8 8.8 %collective-permute-start.5 = (f32[3,1,16,256]{3,2,1,0:T(8,128)S(1)}, f32[3,1,16,256]{3,2,1,0:T(8,128)S(1)}, u32[]{:S(2)}, u32[]{:S(2)}) collective-permute-start(f32[3,1,16,256]{3,2,1,0:T(8,128)S(1)} %get-tuple-element.57), channel_id=1, source_target_pairs={{4,0},{8,4},{12,8},{16,12},{20,16},{24,20},{28,24},{32,28},{36,32}... | collective-permute-start | bytes 147464 | tf_op jit(solution)/shard_map/ppermute | solution.py:27
  86.1 7.9 %collective-permute-start.4 = (f32[3,1,16,256]{3,2,1,0:T(8,128)S(1)}, f32[3,1,16,256]{3,2,1,0:T(8,128)S(1)}, u32[]{:S(2)}, u32[]{:S(2)}) collective-permute-start(f32[3,1,16,256]{3,2,1,0:T(8,128)S(1)} %get-tuple-element.56), channel_id=1, source_target_pairs={{0,4},{4,8},{8,12},{12,16},{16,20},{20,24},{24,28},{28,32},{32,36}... | collective-permute-start | bytes 147464 | tf_op jit(solution)/shard_map/ppermute | solution.py:24
  97.4 8.9 %collective-permute-start.7 = (f32[3,1,16,256]{3,2,1,0:T(8,128)S(1)}, f32[3,1,16,256]{3,2,1,0:T(8,128)S(1)}, u32[]{:S(2)}, u32[]{:S(2)}) collective-permute-start(f32[3,1,16,256]{3,2,1,0:T(8,128)S(1)} %get-tuple-element.55), channel_id=1, source_target_pairs={{4,0},{8,4},{12,8},{16,12},{20,16},{24,20},{28,24},{32,28},{36,32}... | collective-permute-start | bytes 147464 | tf_op jit(solution)/shard_map/ppermute | solution.py:27
  98.7 7.9 %collective-permute-start.6 = (f32[3,1,16,256]{3,2,1,0:T(8,128)S(1)}, f32[3,1,16,256]{3,2,1,0:T(8,128)S(1)}, u32[]{:S(2)}, u32[]{:S(2)}) collective-permute-start(f32[3,1,16,256]{3,2,1,0:T(8,128)S(1)} %get-tuple-element.54), channel_id=1, source_target_pairs={{0,4},{4,8},{8,12},{12,16},{16,20},{20,24},{24,28},{28,32},{32,36}... | collective-permute-start | bytes 147464 | tf_op jit(solution)/shard_map/ppermute | solution.py:24
  233.0 47.7 %all-to-all-start = ((f32[3,64,256]{2,0,1:T(4,128)}), f32[3,64,256]{2,0,1:T(4,128)S(1)}, u32[]{:S(2)}, u32[]{:S(2)}) async-start(f32[3,64,256]{2,0,1:T(4,128)} %multiply_bitcast_fusion), calls=%async_computation | async-start | bytes 524288 | tf_op jit(solution)/shard_map/all_to_all | solution.py:166
  263.9 260.2 %all-reduce.11.cloned.1.call-start = ((), (), s32[]{:S(2)}) async-start(), calls=%async_computation.1 | async-start | bytes 2097152 | tf_op jit(solution)/shard_map/psum | solution.py:178
  375.3 5.4 %collective-permute-start.11 = (f32[3,1,8,128]{3,2,1,0:T(8,128)S(1)}, f32[3,1,8,128]{3,2,1,0:T(8,128)S(1)}, u32[]{:S(2)}, u32[]{:S(2)}) collective-permute-start(f32[3,1,8,128]{3,2,1,0:T(8,128)S(1)} %get-tuple-element.99), channel_id=1, source_target_pairs={{4,0},{8,4},{12,8},{16,12},{20,16},{24,20},{28,24},{32,28},{36,32}... | collective-permute-start | bytes 36872 | tf_op jit(solution)/shard_map/ppermute | solution.py:27
  376.6 4.8 collective-permute-start.10
  382.5 5.6 %collective-permute-start.13 = (f32[3,1,8,128]{3,2,1,0:T(8,128)S(1)}, f32[3,1,8,128]{3,2,1,0:T(8,128)S(1)}, u32[]{:S(2)}, u32[]{:S(2)}) collective-permute-start(f32[3,1,8,128]{3,2,1,0:T(8,128)S(1)} %get-tuple-element.97), channel_id=1, source_target_pairs={{4,0},{8,4},{12,8},{16,12},{20,16},{24,20},{28,24},{32,28},{36,32}... | collective-permute-start | bytes 36872 | tf_op jit(solution)/shard_map/ppermute | solution.py:27
  383.8 5.1 collective-permute-start.12
  389.6 6.2 %collective-permute-start.15 = (f32[3,1,8,128]{3,2,1,0:T(8,128)S(1)}, f32[3,1,8,128]{3,2,1,0:T(8,128)S(1)}, u32[]{:S(2)}, u32[]{:S(2)}) collective-permute-start(f32[3,1,8,128]{3,2,1,0:T(8,128)S(1)} %get-tuple-element.95), channel_id=1, source_target_pairs={{4,0},{8,4},{12,8},{16,12},{20,16},{24,20},{28,24},{32,28},{36,32}... | collective-permute-start | bytes 36872 | tf_op jit(solution)/shard_map/ppermute | solution.py:27
  390.9 5.1 collective-permute-start.14
  404.8 9.0 %collective-permute-start.17 = (f32[3,1,16,256]{3,2,1,0:T(8,128)}, f32[3,1,16,256]{3,2,1,0:T(8,128)}, u32[]{:S(2)}, u32[]{:S(2)}) collective-permute-start(f32[3,1,16,256]{3,2,1,0:T(8,128)} %get-tuple-element.53), channel_id=1, source_target_pairs={{4,0},{8,4},{12,8},{16,12},{20,16},{24,20},{28,24},{32,28},{36,32}... | collective-permute-start | bytes 147464 | tf_op jit(solution)/shard_map/ppermute | solution.py:27
  406.1 7.7 %collective-permute-start.16 = (f32[3,1,16,256]{3,2,1,0:T(8,128)}, f32[3,1,16,256]{3,2,1,0:T(8,128)}, u32[]{:S(2)}, u32[]{:S(2)}) collective-permute-start(f32[3,1,16,256]{3,2,1,0:T(8,128)} %get-tuple-element.52), channel_id=1, source_target_pairs={{0,4},{4,8},{8,12},{12,16},{16,20},{20,24},{24,28},{28,32},{32,36}... | collective-permute-start | bytes 147464 | tf_op jit(solution)/shard_map/ppermute | solution.py:24
  (91 other events, 1095.7 us)
Sparse Core Ops, SparseCore 0:
  423.0 101.0 all-reduce.10
where the time goes:
time: 535 us; the launch traced here: 534 us
  local copies, waits for them, and re-layouts  170 us (32%)
  other arithmetic  156 us (29%)
  waiting for transfers between devices  104 us (19%)
  starting transfers between devices  87.7 us (16%)
  between operations  16 us (3%)
    psum x1, waiting for transfers between devices, body(): total_sum = lax.psum(energy, 'load')  101 us
    scatter-add x1, other arithmetic, body(): coarse_source.reshape(3, -1).at[:, face_dst[0]].add(arrived)  88.6 us
    gather x2, local copies, waits for them, and re-layouts, body(): picked = residual.reshape(3, -1)[:, face_src[0]] * live_mask[None]  65.9 us
    ppermute x9, starting transfers between devices, extended(): lax.ppermute(lax.slice_in_dim(block, block.shape[dim] - width, None, axis...  45.2 us
    another operation x4, local copies, waits for them, and re-layouts, operate(): return jnp.stack(pieces)  37.8 us
    all_to_all x1, starting transfers between devices, body(): lax.all_to_all(picked, 'space', split_axis=1, concat_axis=1, tiled=True)  30.9 us
    squeeze x1, local copies, waits for them, and re-layouts, body(): source = load_force[0]  26.5 us
    reduce_sum x2, other arithmetic, coarsen(): grid_field.reshape(comps, size_x // 2, 2, size_y // 2, 2, size_z // 2, 2)  20.2 us
  transfers between devices with their start and end apart: 20, of which 7 were waited for; matrix products, arithmetic and copies ran while one was open for 14% of the time, Pallas kernels for 0%

commit v1 on v0

v1 whole, which is shorter than its diff:
```python
import jax
import jax.numpy as jnp
import numpy as np
from jax import lax
from jax.experimental import pallas as pl
from jax.experimental.pallas import tpu as pltpu
from jax.sharding import PartitionSpec as P

CX = 8
NY = 16
NZ = 256
BY = 8
SLOTS = 256
FINE_STEPS = 3
COARSE_STEPS = 4

UPPER_EDGE = 2.1
LOWER_EDGE = 0.15
COUPLING = 0.1
MODULI = (1.0, 0.55, 0.25)

MIDPOINT = (UPPER_EDGE + LOWER_EDGE) / 2.0
HALFWIDTH = (UPPER_EDGE - LOWER_EDGE) / 2.0

HX, HY, HZ = CX // 2, NY // 2, NZ // 2
FINE_PLANES = CX + 6
COEF_PLANES = CX + 8
PACK = 3 * 3 + 4 + 1
F32 = jnp.float32
BF16 = jnp.bfloat16
HIGHEST = lax.Precision.HIGHEST


def step_factors(count):
    ratio = MIDPOINT / HALFWIDTH
    rho_old = 1.0 / ratio
    factors = []
    for _ in range(1, count):
        rho_new = 1.0 / (2.0 * ratio - rho_old)
        factors.append((rho_new * rho_old, 2.0 * rho_new / HALFWIDTH))
        rho_old = rho_new
    return factors


class Shifts:
    def __init__(self, shape):
        self.nd = len(shape)
        self.shape = shape
        y = lax.broadcasted_iota(jnp.int32, shape, self.nd - 2)
        z = lax.broadcasted_iota(jnp.int32, shape, self.nd - 1)
        self.edge = {
            self.nd - 2: (y == 0, y == shape[-2] - 1),
            self.nd - 1: (z == 0, z == shape[-1] - 1),
        }

    def pair(self, x, axis):
        first, last = self.edge[axis]
        size = self.shape[axis]
        below = jnp.where(first, 0.0, pltpu.roll(x, 1, axis))
        above = jnp.where(last, 0.0, pltpu.roll(x, size - 1, axis))
        return below, above

    def diff(self, x, axis):
        below, above = self.pair(x, axis)
        return above - below

    def dy(self, x):
        return self.diff(x, self.nd - 2)

    def dz(self, x):
        return self.diff(x, self.nd - 1)

    def spread(self, x):
        for axis in (self.nd - 2, self.nd - 1):
            below, above = self.pair(x, axis)
            x = x + 0.5 * (below + above)
        return x


def diagonal(sh, k_below, k_mid, k_above):
    return (3.0 / 7.0) * k_mid + (1.0 / 14.0) * sh.spread(k_mid + 0.5 * (k_below + k_above))


def operate(sh, below, mid, above, k_below, k_mid, k_above, diag):
    centre = diag + (1.0 / 7.0) * k_mid
    slope = [above[c] - below[c] for c in range(3)]
    mixed = (
        sh.dy(slope[1]) + sh.dz(slope[2]),
        sh.dy(slope[0] + sh.dz(mid[2])),
        sh.dz(slope[0] + sh.dy(mid[1])),
    )
    result = []
    for c in range(3):
        plain = sh.spread(mid[c] + 0.5 * (below[c] + above[c]))
        scaled = sh.spread(k_mid * mid[c] + 0.5 * (k_below * below[c] + k_above * above[c]))
        result.append(
            centre * mid[c]
            - (1.0 / 14.0) * (k_mid * plain + scaled)
            - (0.25 * COUPLING) * (k_mid * mixed[c])
        )
    return result


def modulus(material_ref, brick):
    ident = material_ref[0, brick]
    return jnp.where(ident == 0, MODULI[0], jnp.where(ident == 1, MODULI[1], MODULI[2])).astype(F32)


def own_plane(material_ref):
    row = lax.broadcasted_iota(jnp.int32, (NY, NZ), 0)
    return jnp.where(row < BY, modulus(material_ref, 0), modulus(material_ref, 1))


def pair_columns():
    fine = lax.broadcasted_iota(jnp.int32, (NZ, HZ), 0)
    coarse = lax.broadcasted_iota(jnp.int32, (NZ, HZ), 1)
    return (lax.shift_right_logical(fine, 1) == coarse).astype(F32)


def coarse_sum(planes, narrow_ref):
    narrow_ref[...] = jnp.dot(
        planes, pair_columns(), precision=HIGHEST, preferred_element_type=F32
    )
    rows = narrow_ref.shape[0] // 2
    return narrow_ref[pl.ds(0, rows, stride=2), :] + narrow_ref[pl.ds(1, rows, stride=2), :]


def pack_kernel(material_ref, force_ref, stiff_ref, low_ref, high_ref, coarse_ref, sums):
    own = own_plane(material_ref)
    for c in range(3):
        for p in range(3):
            low_ref[3 * c + p] = force_ref[0, c, p]
            high_ref[3 * c + p] = force_ref[0, c, CX - 3 + p]
    coef = [stiff_ref[p] * own for p in range(CX)]
    for p in range(4):
        low_ref[9 + p] = coef[p]
        high_ref[9 + p] = coef[CX - 4 + p]
    pairs = jnp.concatenate([coef[2 * p] + coef[2 * p + 1] for p in range(HX)], axis=0)
    coarse = (0.125 * coarse_sum(pairs, sums)).reshape(HX, HY, HZ)
    coarse_ref[...] = coarse
    for p in range(HX):
        y, z = (p // 2) * HY, (p % 2) * HZ
        low_ref[13, y : y + HY, z : z + HZ] = coarse[p]
        high_ref[13, y : y + HY, z : z + HZ] = coarse[p]


def unpack_coarse(plane_ref):
    return [
        plane_ref[0, (p // 2) * HY : (p // 2) * HY + HY, (p % 2) * HZ : (p % 2) * HZ + HZ]
        for p in range(HX)
    ]


def fine_kernel(
    material_ref,
    count_ref,
    force_ref,
    stiff_ref,
    below_ref,
    above_ref,
    index_ref,
    smooth_ref,
    coef_out_ref,
    diag_out_ref,
    coarse_ref,
    picked_ref,
    coef,
    diag,
    inverse,
    force,
    first,
    second,
    table,
    sums,
    residual,
):
    slab = lax.axis_index("space")
    slabs = lax.axis_size("space")
    sh = Shifts((NY, NZ))
    own = own_plane(material_ref)
    has_below = slab > 0
    has_above = slab < slabs - 1
    for p in range(CX):
        coef[4 + p] = stiff_ref[p] * own
    for p in range(4):
        coef[p] = jnp.where(has_below, below_ref[9 + p], 0.0)
        coef[4 + CX + p] = jnp.where(has_above, above_ref[9 + p], 0.0)
    for c in range(3):
        for p in range(3):
            force[c, p] = below_ref[3 * c + p]
            force[c, 3 + CX + p] = above_ref[3 * c + p]
        for p in range(CX):
            force[c, 3 + p] = force_ref[0, c, p]

    @pl.loop(0, FINE_PLANES)
    def _(p):
        d = diagonal(sh, coef[p], coef[p + 1], coef[p + 2])
        where = slab * CX + p - 3
        valid = jnp.logical_and(where >= 0, where < slabs * CX)
        inv = jnp.where(valid, 1.0 / d, 0.0)
        diag[p] = d
        inverse[p] = inv
        for c in range(3):
            first[c, p] = force[c, p] * inv * (1.0 / MIDPOINT)

    def remainder(src, p, base):
        planes = [[src[c, p + o - base] for c in range(3)] for o in (-1, 0, 1)]
        image = operate(sh, *planes, coef[p], coef[p + 1], coef[p + 2], diag[p])
        return planes[1], [force[c, p] - image[c] for c in range(3)]

    (keep_2, gain_2), (keep_3, gain_3) = step_factors(FINE_STEPS)

    @pl.loop(1, FINE_PLANES - 1)
    def _(p):
        value, left = remainder(first, p, 0)
        for c in range(3):
            second[c, p] = (1.0 + keep_2) * value[c] + gain_2 * (left[c] * inverse[p])

    @pl.loop(2, FINE_PLANES - 2)
    def _(p):
        value, left = remainder(second, p, 0)
        for c in range(3):
            step = keep_3 * (value[c] - first[c, p]) + gain_3 * (left[c] * inverse[p])
            smooth_ref[c, p - 2] = value[c] + step

    @pl.loop(3, FINE_PLANES - 3)
    def _(p):
        _, left = remainder(smooth_ref, p, 2)
        for c in range(3):
            row = pl.multiple_of(c * (CX * NY) + (p - 3) * NY, NY)
            residual[pl.ds(row, NY), :] = left[c]
            head = left[c].astype(BF16)
            table[pl.ds(row, NY), 0:NZ] = head
            table[pl.ds(row, NY), NZ : 2 * NZ] = (left[c] - head.astype(F32)).astype(BF16)

    for p in range(CX + 2):
        coef_out_ref[p] = coef[p + 3]
    for p in range(CX):
        diag_out_ref[p] = diag[p + 3]

    planes = residual[...].reshape(3 * HX, 2, NY, NZ)
    pairs = (planes[:, 0] + planes[:, 1]).reshape(3 * HX * NY, NZ)
    coarse_ref[...] = 0.5 * coarse_sum(pairs, sums)

    plane_rows = CX * NY
    column = lax.broadcasted_iota(jnp.int32, (NZ, SLOTS), 0)
    line = lax.broadcasted_iota(jnp.int32, (plane_rows, SLOTS), 0)
    slot = lax.broadcasted_iota(jnp.int32, (1, SLOTS), 1)

    @pl.loop(0, slabs)
    def _(o):
        index = index_ref[0, pl.ds(o, 1), :]
        hot = (column == (index & (NZ - 1))).astype(BF16)
        both = jnp.dot(table[:, 0:NZ], hot, preferred_element_type=F32) + jnp.dot(
            table[:, NZ : 2 * NZ], hot, preferred_element_type=F32
        )
        chosen = line == lax.shift_right_logical(index, 8)
        live = slot < count_ref[0, o]
        for c in range(3):
            part = jnp.where(chosen, both[c * plane_rows : (c + 1) * plane_rows, :], 0.0)
            value = jnp.sum(part, axis=0, keepdims=True)
            picked_ref[pl.ds(o, 1), c * SLOTS : (c + 1) * SLOTS] = jnp.where(live, value, 0.0)


def coarse_extent(below_pack_ref, coarse_ref, above_pack_ref, slab, slabs):
    low = [jnp.where(slab > 0, x, 0.0) for x in unpack_coarse(below_pack_ref)]
    high = [jnp.where(slab < slabs - 1, x, 0.0) for x in unpack_coarse(above_pack_ref)]
    return low + [coarse_ref[p] for p in range(HX)] + high


def gather_kernel(
    arrived_ref,
    target_ref,
    local_ref,
    coef_below_ref,
    coef_ref,
    coef_above_ref,
    source_ref,
    low_ref,
    high_ref,
    total,
    rows,
):
    slab = lax.axis_index("space")
    slabs = lax.axis_size("space")
    half_rows = HX * HY * HZ // SLOTS
    column = lax.broadcasted_iota(jnp.int32, (SLOTS, SLOTS), 0)
    line = lax.broadcasted_iota(jnp.int32, (half_rows, SLOTS), 0)
    total[...] = jnp.zeros_like(total)

    @pl.loop(0, slabs)
    def _(s):
        index = target_ref[0, pl.ds(s, 1), :]
        hot = (column == (index & (SLOTS - 1))).astype(BF16)
        chosen = line == lax.shift_right_logical(index, 8)
        parts = [
            jnp.where(chosen, arrived_ref[pl.ds(s, 1), c * SLOTS : (c + 1) * SLOTS], 0.0)
            for c in range(3)
        ]
        values = jnp.concatenate(parts, axis=0)
        head = values.astype(BF16)
        tail = (values - head.astype(F32)).astype(BF16)
        total[...] += lax.dot_general(
            jnp.concatenate([head, tail], axis=0),
            hot,
            (((1,), (1,)), ((), ())),
            preferred_element_type=F32,
        )

    count = 3 * half_rows
    joined = total[0:count, :] + total[count : 2 * count, :]
    rows[pl.ds(0, count, stride=2), :] = joined[:, 0:HZ]
    rows[pl.ds(1, count, stride=2), :] = joined[:, HZ:]
    source = (rows[...] + local_ref[...]).reshape(3, HX, HY, HZ)
    source_ref[...] = source
    low_ref[...] = source
    high_ref[...] = source
    coef = coarse_extent(coef_below_ref, coef_ref, coef_above_ref, slab, slabs)
    sh = Shifts((HY, HZ))
    for ref, p in ((high_ref, 0), (low_ref, HX - 1)):
        d = diagonal(sh, coef[HX + p - 1], coef[HX + p], coef[HX + p + 1])
        scale = (1.0 / MIDPOINT) / d
        for c in range(3):
            ref[c, p] = source[c, p] * scale


def coarse_kernel(
    source_ref,
    below_ref,
    above_ref,
    coef_below_ref,
    coarse_coef_ref,
    coef_above_ref,
    smooth_ref,
    coef_ref,
    diag_ref,
    moved_ref,
    kept_ref,
    sent_1_ref,
    sent_2_ref,
    sent_3_ref,
    rows,
    field,
    energy,
):
    slab = lax.axis_index("space")
    slabs = lax.axis_size("space")
    mine = lax.axis_index("load")
    coef = jnp.stack(coarse_extent(coef_below_ref, coarse_coef_ref, coef_above_ref, slab, slabs))
    source = [
        jnp.concatenate([below_ref[c], source_ref[c], above_ref[c]], axis=0) for c in range(3)
    ]
    count = 3 * HX - 2
    place = lax.broadcasted_iota(jnp.int32, (count, HY, HZ), 0) + (slab * HX - HX + 1)
    valid = jnp.logical_and(place >= 0, place < slabs * HX)
    diag = diagonal(Shifts((count, HY, HZ)), coef[:-2], coef[1:-1], coef[2:])
    inverse = jnp.where(valid, 1.0 / diag, 0.0)
    older = None
    value = []
    for c in range(3):
        low = jnp.where(slab > 0, source[c][:1], 0.0)
        high = jnp.where(slab < slabs - 1, source[c][-1:], 0.0)
        inner = source[c][1:-1] * inverse * (1.0 / MIDPOINT)
        value.append(jnp.concatenate([low, inner, high], axis=0))
    for number, (keep, gain) in enumerate(step_factors(COARSE_STEPS)):
        size = count - 2 * number
        inside = slice(number, number + size)
        window = slice(number + 1, number + 1 + size)
        image = operate(
            Shifts((size, HY, HZ)),
            [v[:-2] for v in value],
            [v[1:-1] for v in value],
            [v[2:] for v in value],
            coef[number : number + size],
            coef[window],
            coef[number + 2 : number + 2 + size],
            diag[inside],
        )
        newer = []
        for c in range(3):
            mid = value[c][1:-1]
            change = mid if older is None else mid - older[c][2:-2]
            left = source[c][window] - image[c]
            newer.append(mid + keep * change + gain * (left * inverse[inside]))
        older, value = value, newer

    planes = HX + 2
    flat = jnp.concatenate([v.reshape(planes * HY, HZ) for v in value], axis=0)
    fine = lax.broadcasted_iota(jnp.int32, (HZ, NZ), 1)
    half = lax.broadcasted_iota(jnp.int32, (HZ, NZ), 0)
    repeat = (lax.shift_right_logical(fine, 1) == half).astype(F32)
    amount = 3 * planes * HY
    rows[pl.ds(0, amount, stride=2), :] = flat
    rows[pl.ds(1, amount, stride=2), :] = flat
    wide = jnp.dot(rows[...], repeat, precision=HIGHEST, preferred_element_type=F32)
    for c in range(3):
        for p in range(CX + 2):
            at = (c * planes + (p + 1) // 2) * NY
            moved = smooth_ref[c, p] + wide[at : at + NY, :]
            field[c, p] = moved
            if 0 < p <= CX:
                moved_ref[0, c, p - 1] = moved

    sh = Shifts((NY, NZ))

    @pl.loop(1, CX + 1)
    def _(p):
        planes = [[field[c, p + o] for c in range(3)] for o in (-1, 0, 1)]
        image = operate(
            sh, *planes, coef_ref[p - 1], coef_ref[p], coef_ref[p + 1], diag_ref[p - 1]
        )
        mid = planes[1]
        energy[p - 1] = mid[0] * image[0] + mid[1] * image[1] + mid[2] * image[2]

    part = NY // 4
    for q in range(4):

        @pl.when(mine == q)
        def _():
            for k, ref in enumerate((kept_ref, sent_1_ref, sent_2_ref, sent_3_ref)):
                y = ((q + k) % 4) * part
                ref[...] = energy[:, y : y + part, :]


def close_kernel(material_ref, kept_ref, got_1_ref, got_2_ref, got_3_ref, out_ref):
    mine = lax.axis_index("load")
    ident = jnp.where(mine < 2, material_ref[0, 0], material_ref[0, 1])
    total = kept_ref[...] + got_1_ref[...] + got_2_ref[...] + got_3_ref[...]
    base = np.array(MODULI, np.float32)
    for m in range(3):
        factor = [float((base[m] - base[i]) / base[i]) for i in range(3)]
        scale = jnp.where(ident == 0, factor[0], jnp.where(ident == 1, factor[1], factor[2]))
        out_ref[m] = total * scale.astype(F32)


VMEM = pl.BlockSpec(memory_space=pltpu.VMEM)
SMEM = pl.BlockSpec(memory_space=pltpu.SMEM)
PARAMS = pltpu.CompilerParams(vmem_limit_bytes=32 << 20)


def shaped(*shape):
    return jax.ShapeDtypeStruct(shape, F32)


def body(load_force, stiffness, material, face_src, face_count, face_dst):
    slabs = lax.axis_size("space")
    forward = [(i, (i + 1) % slabs) for i in range(slabs)]
    backward = [(target, origin) for origin, target in forward]
    pack_low, pack_high, coarse_coef = pl.pallas_call(
        pack_kernel,
        out_shape=(shaped(PACK, NY, NZ), shaped(PACK, NY, NZ), shaped(HX, HY, HZ)),
        in_specs=[SMEM, VMEM, VMEM],
        out_specs=(VMEM, VMEM, VMEM),
        scratch_shapes=[pltpu.VMEM((HX * NY, HZ), F32)],
        compiler_params=PARAMS,
        name="pack",
    )(material, load_force, stiffness)
    below = lax.ppermute(pack_high, "space", forward)
    above = lax.ppermute(pack_low, "space", backward)

    smooth, coef, diag, local, picked = pl.pallas_call(
        fine_kernel,
        out_shape=(
            shaped(3, CX + 2, NY, NZ),
            shaped(CX + 2, NY, NZ),
            shaped(CX, NY, NZ),
            shaped(3 * HX * HY, HZ),
            shaped(slabs, 3 * SLOTS),
        ),
        in_specs=[SMEM, SMEM, VMEM, VMEM, VMEM, VMEM, VMEM],
        out_specs=(VMEM, VMEM, VMEM, VMEM, VMEM),
        scratch_shapes=[
            pltpu.VMEM((COEF_PLANES, NY, NZ), F32),
            pltpu.VMEM((FINE_PLANES, NY, NZ), F32),
            pltpu.VMEM((FINE_PLANES, NY, NZ), F32),
            pltpu.VMEM((3, FINE_PLANES, NY, NZ), F32),
            pltpu.VMEM((3, FINE_PLANES, NY, NZ), F32),
            pltpu.VMEM((3, FINE_PLANES, NY, NZ), F32),
            pltpu.VMEM((3 * CX * NY, 2 * NZ), BF16),
            pltpu.VMEM((3 * HX * NY, HZ), F32),
            pltpu.VMEM((3 * CX * NY, NZ), F32),
        ],
        compiler_params=PARAMS,
        name="fine",
    )(material, face_count, load_force, stiffness, below, above, face_src)

    arrived = lax.all_to_all(picked, "space", split_axis=0, concat_axis=0, tiled=True)

    tail = pl.BlockSpec((1, NY, NZ), lambda i: (PACK - 1, 0, 0))

    def whole(*shape):
        return pl.BlockSpec(shape, lambda i: (0,) * len(shape))

    grid_shape = (3, HX, HY, HZ)
    source, send_low, send_high = pl.pallas_call(
        gather_kernel,
        grid=(1,),
        out_shape=(shaped(*grid_shape), shaped(*grid_shape), shaped(*grid_shape)),
        in_specs=[
            whole(slabs, 3 * SLOTS),
            whole(1, slabs, SLOTS),
            whole(3 * HX * HY, HZ),
            tail,
            whole(HX, HY, HZ),
            tail,
        ],
        out_specs=(whole(*grid_shape), whole(*grid_shape), whole(*grid_shape)),
        scratch_shapes=[
            pltpu.VMEM((6 * HX * HY * HZ // SLOTS, SLOTS), F32),
            pltpu.VMEM((3 * HX * HY, HZ), F32),
        ],
        compiler_params=PARAMS,
        name="reflux",
    )(arrived, face_dst, local, below, coarse_coef, above)
    source_below = lax.ppermute(send_high, "space", forward)
    source_above = lax.ppermute(send_low, "space", backward)

    part = (CX, NY // 4, NZ)
    moved, kept, sent_1, sent_2, sent_3 = pl.pallas_call(
        coarse_kernel,
        grid=(1,),
        out_shape=(shaped(1, 3, CX, NY, NZ),) + (shaped(*part),) * 4,
        in_specs=[
            whole(*grid_shape),
            whole(*grid_shape),
            whole(*grid_shape),
            tail,
            whole(HX, HY, HZ),
            tail,
            whole(3, CX + 2, NY, NZ),
            whole(CX + 2, NY, NZ),
            whole(CX, NY, NZ),
        ],
        out_specs=(whole(1, 3, CX, NY, NZ),) + (whole(*part),) * 4,
        scratch_shapes=[
            pltpu.VMEM((3 * (HX + 2) * NY, HZ), F32),
            pltpu.VMEM((3, CX + 2, NY, NZ), F32),
            pltpu.VMEM((CX, NY, NZ), F32),
        ],
        compiler_params=PARAMS,
        name="coarse",
    )(source, source_below, source_above, below, coarse_coef, above, smooth, coef, diag)
    got = [
        lax.ppermute(piece, "load", [(i, (i + k) % 4) for i in range(4)])
        for k, piece in ((1, sent_1), (2, sent_2), (3, sent_3))
    ]
    sensitivity = pl.pallas_call(
        close_kernel,
        out_shape=shaped(3, *part),
        in_specs=[SMEM, VMEM, VMEM, VMEM, VMEM],
        out_specs=VMEM,
        name="close",
    )(material, kept, *got)
    return moved, sensitivity


def solution(mesh):
    return jax.shard_map(
        body,
        mesh=mesh,
        in_specs=(
            P("load", None, "space", None, None),
            P("space", None, None),
            P("space", None),
            P("space", None, None),
            P("space", None),
            P("space", None, None),
        ),
        out_specs=(P("load", None, "space", None, None), P(None, "space", "load", None)),
        check_vma=False,
    )
```

time: 535 us -> 109 us (0.20)
  local copies, waits for them, and re-layouts: 170 us -> 4.82 us
  other arithmetic: 156 us -> 0 us
  waiting for transfers between devices: 104 us -> 13.1 us
  starting transfers between devices: 87.7 us -> 27.8 us
  Pallas kernels: 0 us -> 43.2 us
  blocking collectives: 0 us -> 19.1 us
  between operations: 16 us -> 0.7 us
    psum x1 -> x0, waiting for transfers between devices: 101 us -> none  [body(): total_sum = lax.psum(energy, 'load')]
    scatter-add x1 -> x0, other arithmetic: 88.6 us -> none  [body(): coarse_source.reshape(3, -1).at[:, face_dst[0]].add(arrived)]
    gather x2 -> x0, local copies, waits for them, and re-layouts: 65.9 us -> none  [body(): picked = residual.reshape(3, -1)[:, face_src[0]] * live_mask[None]]
    another operation x5 -> x0, local copies, waits for them, and re-layouts: 47.6 us -> none  [the longest x4 37.8 us: operate(): return jnp.stack(pieces)]
    pallas_call x0 -> x5, Pallas kernels: none -> 43.2 us  [the longest x1 25.1 us: body(): pl.pallas_call(fine_kernel, out_shape=(shaped(3, CX + 2, NY, NZ), shaped(...]
    all_to_all x1 -> x0, starting transfers between devices: 30.9 us -> none  [body(): lax.all_to_all(picked, 'space', split_axis=1, concat_axis=1, tiled=True)]
    ppermute x18 -> x7, starting transfers between devices: 56.8 us -> 27.8 us  [the longest x3 10.2 us: body(): lax.ppermute(piece, 'load', [(i, (i + k) % 4) for i in range(4)])]
    squeeze x1 -> x0, local copies, waits for them, and re-layouts: 26.5 us -> none  [body(): source = load_force[0]]
  transfers between devices with their start and end apart: 20 -> 7, of which waited for: 7 -> 5; matrix products, arithmetic and copies ran while one was open for 14% -> 0% of each run, Pallas kernels for 0% -> 0%
where the time goes in v1:
time: 109 us
  Pallas kernels  43.2 us (40%)
  starting transfers between devices  27.8 us (26%)
  blocking collectives  19.1 us (18%)
  waiting for transfers between devices  13.1 us (12%)
  local copies, waits for them, and re-layouts  4.82 us (4%)
    pallas_call x1, Pallas kernels, body(): pl.pallas_call(fine_kernel, out_shape=(shaped(3, CX + 2, NY, NZ), shaped(...  25.1 us
    all_to_all x1, blocking collectives, body(): lax.all_to_all(picked, 'space', split_axis=0, concat_axis=0, tiled=True)  19.1 us
    pallas_call x1, Pallas kernels, body(): pl.pallas_call(gather_kernel, grid=(1,), out_shape=(shaped(*grid_shape),...  12.7 us
    ppermute x3, starting transfers between devices, body(): lax.ppermute(piece, 'load', [(i, (i + k) % 4) for i in range(4)])  10.2 us
    ppermute x1, starting transfers between devices, body(): above = lax.ppermute(pack_low, 'space', backward)  7.44 us
    ppermute x1, starting transfers between devices, body(): source_above = lax.ppermute(send_low, 'space', backward)  7.07 us
    ppermute x3, waiting for transfers between devices, body(): lax.ppermute(piece, 'load', [(i, (i + k) % 4) for i in range(4)])  6.89 us
    ppermute x1, waiting for transfers between devices, body(): below = lax.ppermute(pack_high, 'space', forward)  4.71 us
  transfers between devices with their start and end apart: 7, of which 5 were waited for; matrix products, arithmetic and copies ran while one was open for 0% of the time, Pallas kernels for 0%

profile of v1, /device:TPU:1, one launch (start us, length us, event | category | flops | bytes accessed | tf_op | source)
XLA Modules:
  0.0 108.7 jit_solution(1381003576623289881)
XLA Ops:
  0.6 1.0 copy-done
  1.6 0.9 copy-done.1
  2.5 0.7 copy-done.5
  3.2 0.8 pack.1
  4.0 2.5 %collective-permute-start = (f32[14,16,256]{2,1,0:T(8,128)S(1)}, f32[14,16,256]{2,1,0:T(8,128)S(1)}, u32[]{:S(2)}, u32[]{:S(2)}) collective-permute-start(f32[14,16,256]{2,1,0:T(8,128)S(1)} %get-tuple-element.18), channel_id=1, source_target_pairs={{0,4},{4,8},{8,12},{12,16},{16,20},{20,24},{24,28},{28,32},{32,36}... | collective-permute-start | bytes 688136 | tf_op jit(solution)/shard_map/ppermute | solution.py:458
  6.5 7.4 %collective-permute-start.1 = (f32[14,16,256]{2,1,0:T(8,128)S(1)}, f32[14,16,256]{2,1,0:T(8,128)S(1)}, u32[]{:S(2)}, u32[]{:S(2)}) collective-permute-start(f32[14,16,256]{2,1,0:T(8,128)S(1)} %get-tuple-element.19), channel_id=1, source_target_pairs={{4,0},{8,4},{12,8},{16,12},{20,16},{24,20},{28,24},{32,28},{36,32}... | collective-permute-start | bytes 688136 | tf_op jit(solution)/shard_map/ppermute | solution.py:459
  14.0 4.7 %collective-permute-done.below_ref.coef_below_ref = f32[14,16,256]{2,1,0:T(8,128)S(1)} collective-permute-done((f32[14,16,256]{2,1,0:T(8,128)S(1)}, f32[14,16,256]{2,1,0:T(8,128)S(1)}, u32[]{:S(2)}, u32[]{:S(2)}) %collective-permute-start) | collective-permute-done | bytes 229408 | tf_op jit(solution)/shard_map/ppermute | solution.py:458
  18.7 25.1 %fine.1 = (f32[3,10,16,256]{3,2,1,0:T(8,128)S(1)}, f32[10,16,256]{2,1,0:T(8,128)S(1)}, f32[8,16,256]{2,1,0:T(8,128)S(1)}, f32[96,128]{1,0:T(8,128)S(1)}, f32[64,768]{1,0:T(8,128)S(1)}) custom-call(s32[1,2]{1,0:T(1,128)S(1)} %copy-done.5, s32[1,64]{1,0:T(1,128)S(1)} %copy-done.6, f32[1,3,8,16,256]{4,3,2,1,0:T(8,128)S(1)} %copy-done, ...), custom_call_target="tpu_custom_call" | custom-call | tf_op jit(solution)/shard_map/fine/pallas_call | solution.py:461
  44.0 19.1 %all_to_all.11 = f32[64,1,768]{2,1,0:T(1,128)S(1)} all-to-all(f32[64,1,768]{2,1,0:T(1,128)S(1)} %copy.8), channel_id=1, replica_groups=mesh['space'=64,'load'=4] {'space'}, dimensions={0} | all-to-all | bytes 393216 | tf_op jit(solution)/shard_map/all_to_all | solution.py:487
  63.2 0.8 copy-done.3
  64.0 12.7 %reflux.1 = (f32[3,4,8,128]{3,2,1,0:T(8,128)S(1)}, f32[3,4,8,128]{3,2,1,0:T(8,128)S(1)}, f32[3,4,8,128]{3,2,1,0:T(8,128)S(1)}) custom-call(f32[64,768]{1,0:T(8,128)S(1)} %bitcast.4, s32[1,64,256]{2,1,0:T(8,128)S(1)} %copy-done.3, f32[96,128]{1,0:T(8,128)S(1)} %get-tuple-element.21.local_ref, ...), custom_call_target="tpu_custom_call" | custom-call | tf_op jit(solution)/shard_map/reflux/pallas_call | solution.py:495
  76.8 0.5 collective-permute-start.2
  77.2 7.1 %collective-permute-start.3 = (f32[3,4,8,128]{3,2,1,0:T(8,128)S(1)}, f32[3,4,8,128]{3,2,1,0:T(8,128)S(1)}, u32[]{:S(2)}, u32[]{:S(2)}) collective-permute-start(f32[3,4,8,128]{3,2,1,0:T(8,128)S(1)} %get-tuple-element.25), channel_id=1, source_target_pairs={{4,0},{8,4},{12,8},{16,12},{20,16},{24,20},{28,24},{32,28},{36,32}... | collective-permute-start | bytes 147464 | tf_op jit(solution)/shard_map/ppermute | solution.py:516
  84.3 1.5 %collective-permute-done.2.below_ref = f32[3,4,8,128]{3,2,1,0:T(8,128)S(1)} collective-permute-done((f32[3,4,8,128]{3,2,1,0:T(8,128)S(1)}, f32[3,4,8,128]{3,2,1,0:T(8,128)S(1)}, u32[]{:S(2)}, u32[]{:S(2)}) %collective-permute-start.2) | collective-permute-done | bytes 49184 | tf_op jit(solution)/shard_map/ppermute | solution.py:515
  85.8 3.1 %coarse.1 = (f32[1,3,8,16,256]{4,3,2,1,0:T(8,128)}, f32[8,4,256]{2,1,0:T(4,128)S(1)}, f32[8,4,256]{2,1,0:T(4,128)S(1)}, f32[8,4,256]{2,1,0:T(4,128)S(1)}, f32[8,4,256]{2,1,0:T(4,128)S(1)}) custom-call(f32[3,4,8,128]{3,2,1,0:T(8,128)S(1)} %get-tuple-element.23.source_ref, f32[3,4,8,128]{3,2,1,0:T(8,128)S(1)} %collective-permute-done.2.below_ref, ...), custom_call_target="tpu_custom_call" | custom-call | tf_op jit(solution)/shard_map/coarse/pallas_call | solution.py:519
  88.9 0.6 copy-done.4
  89.5 9.8 %collective-permute-start.4 = (f32[8,4,256]{2,1,0:T(4,128)S(1)}, f32[8,4,256]{2,1,0:T(4,128)S(1)}, u32[]{:S(2)}, u32[]{:S(2)}) collective-permute-start(f32[8,4,256]{2,1,0:T(4,128)S(1)} %get-tuple-element.31), channel_id=1, source_target_pairs={{0,1},{1,2},{2,3},{3,0},{4,5},{5,6},{6,7},{7,4},{8,9},{9,10},{10,1... | collective-permute-start | bytes 98312 | tf_op jit(solution)/shard_map/ppermute | solution.py:544
  99.3 0.3 collective-permute-start.6
  99.7 0.6 collective-permute-done.4.got_1_ref
  100.3 5.9 %collective-permute-done.5.got_2_ref = f32[8,4,256]{2,1,0:T(4,128)S(1)} collective-permute-done((f32[8,4,256]{2,1,0:T(4,128)S(1)}, f32[8,4,256]{2,1,0:T(4,128)S(1)}, u32[]{:S(2)}, u32[]{:S(2)}) %collective-permute-start.5) | collective-permute-done | bytes 32800 | tf_op jit(solution)/shard_map/ppermute | solution.py:544
  106.2 0.4 collective-permute-done.6.got_3_ref
  106.6 0.2 copy-done.8
  106.8 0.4 copy-done.9
  107.2 1.5 %close.1 = f32[3,8,4,256]{3,2,1,0:T(4,128)} custom-call(s32[1,2]{1,0:T(1,128)} %material_ref.5, f32[8,4,256]{2,1,0:T(4,128)} %copy-done.4, f32[8,4,256]{2,1,0:T(4,128)} %copy-done.7, f32[8,4,256]{2,1,0:T(4,128)} %copy-done.8, f32[8,4,256]{2,1,0:T(4,128)} %copy-done.9), custom_call_target="tpu_custom_call" | custom-call | tf_op jit(solution)/shard_map/close/pallas_call | solution.py:547
  (18 shorter events, 0.3 us)
Async XLA Ops:
  0.6 1.0 copy-start
  1.6 0.9 copy-start.1
  2.5 0.7 copy-start.5
  3.2 15.5 %copy-start.2 = (s32[1,64,256]{2,1,0:T(8,128)S(1)}, s32[1,64,256]{2,1,0:T(8,128)}, u32[]{:S(2)}) copy-start(s32[1,64,256]{2,1,0:T(8,128)} %index_ref.1) | copy-start | bytes 196612
  4.0 14.7 %copy-start.6 = (s32[1,64]{1,0:T(1,128)S(1)}, s32[1,64]{1,0:T(1,128)}, u32[]{:S(2)}) copy-start(s32[1,64]{1,0:T(1,128)} %count_ref.1) | copy-start | bytes 772
  4.0 14.7 %collective-permute-start = (f32[14,16,256]{2,1,0:T(8,128)S(1)}, f32[14,16,256]{2,1,0:T(8,128)S(1)}, u32[]{:S(2)}, u32[]{:S(2)}) collective-permute-start(f32[14,16,256]{2,1,0:T(8,128)S(1)} %get-tuple-element.18), channel_id=1, source_target_pairs={{0,4},{4,8},{8,12},{12,16},{16,20},{20,24},{24,28},{28,32},{32,36}... | collective-permute-start | bytes 688136 | tf_op jit(solution)/shard_map/ppermute | solution.py:458
  6.5 12.2 %collective-permute-start.1 = (f32[14,16,256]{2,1,0:T(8,128)S(1)}, f32[14,16,256]{2,1,0:T(8,128)S(1)}, u32[]{:S(2)}, u32[]{:S(2)}) collective-permute-start(f32[14,16,256]{2,1,0:T(8,128)S(1)} %get-tuple-element.19), channel_id=1, source_target_pairs={{4,0},{8,4},{12,8},{16,12},{20,16},{24,20},{28,24},{32,28},{36,32}... | collective-permute-start | bytes 688136 | tf_op jit(solution)/shard_map/ppermute | solution.py:459
  63.2 0.8 copy-start.3
  76.8 9.0 %collective-permute-start.2 = (f32[3,4,8,128]{3,2,1,0:T(8,128)S(1)}, f32[3,4,8,128]{3,2,1,0:T(8,128)S(1)}, u32[]{:S(2)}, u32[]{:S(2)}) collective-permute-start(f32[3,4,8,128]{3,2,1,0:T(8,128)S(1)} %get-tuple-element.24), channel_id=1, source_target_pairs={{0,4},{4,8},{8,12},{12,16},{16,20},{20,24},{24,28},{28,32},{32,36}... | collective-permute-start | bytes 147464 | tf_op jit(solution)/shard_map/ppermute | solution.py:515
  77.2 8.5 %collective-permute-start.3 = (f32[3,4,8,128]{3,2,1,0:T(8,128)S(1)}, f32[3,4,8,128]{3,2,1,0:T(8,128)S(1)}, u32[]{:S(2)}, u32[]{:S(2)}) collective-permute-start(f32[3,4,8,128]{3,2,1,0:T(8,128)S(1)} %get-tuple-element.25), channel_id=1, source_target_pairs={{4,0},{8,4},{12,8},{16,12},{20,16},{24,20},{28,24},{32,28},{36,32}... | collective-permute-start | bytes 147464 | tf_op jit(solution)/shard_map/ppermute | solution.py:516
  88.9 0.6 copy-start.4
  89.5 10.8 %collective-permute-start.4 = (f32[8,4,256]{2,1,0:T(4,128)S(1)}, f32[8,4,256]{2,1,0:T(4,128)S(1)}, u32[]{:S(2)}, u32[]{:S(2)}) collective-permute-start(f32[8,4,256]{2,1,0:T(4,128)S(1)} %get-tuple-element.31), channel_id=1, source_target_pairs={{0,1},{1,2},{2,3},{3,0},{4,5},{5,6},{6,7},{7,4},{8,9},{9,10},{10,1... | collective-permute-start | bytes 98312 | tf_op jit(solution)/shard_map/ppermute | solution.py:544
  99.3 6.9 %collective-permute-start.5 = (f32[8,4,256]{2,1,0:T(4,128)S(1)}, f32[8,4,256]{2,1,0:T(4,128)S(1)}, u32[]{:S(2)}, u32[]{:S(2)}) collective-permute-start(f32[8,4,256]{2,1,0:T(4,128)S(1)} %get-tuple-element.32), channel_id=1, source_target_pairs={{0,2},{1,3},{2,0},{3,1},{4,6},{5,7},{6,4},{7,5},{8,10},{9,11},{10,... | collective-permute-start | bytes 98312 | tf_op jit(solution)/shard_map/ppermute | solution.py:544
  99.3 7.2 %collective-permute-start.6 = (f32[8,4,256]{2,1,0:T(4,128)S(1)}, f32[8,4,256]{2,1,0:T(4,128)S(1)}, u32[]{:S(2)}, u32[]{:S(2)}) collective-permute-start(f32[8,4,256]{2,1,0:T(4,128)S(1)} %get-tuple-element.33), channel_id=1, source_target_pairs={{0,3},{1,0},{2,1},{3,2},{4,7},{5,4},{6,5},{7,6},{8,11},{9,8},{10,9... | collective-permute-start | bytes 98312 | tf_op jit(solution)/shard_map/ppermute | solution.py:544
  100.3 6.3 %copy-start.7 = (f32[8,4,256]{2,1,0:T(4,128)}, f32[8,4,256]{2,1,0:T(4,128)S(1)}, u32[]{:S(2)}) copy-start(f32[8,4,256]{2,1,0:T(4,128)S(1)} %collective-permute-done.4.got_1_ref) | copy-start | bytes 98308
  106.2 0.6 copy-start.8
  106.6 0.6 copy-start.9

commit v2 on v1

--- a/solution.py
+++ b/solution.py
@@ -24,8 +24,8 @@
 
 HX, HY, HZ = CX // 2, NY // 2, NZ // 2
 FINE_PLANES = CX + 6
-COEF_PLANES = CX + 8
-PACK = 3 * 3 + 4 + 1
+COEF_PLANES = CX + 6
+PACK = 3 * 3 + 3 + 1
 F32 = jnp.float32
 BF16 = jnp.bfloat16
 HIGHEST = lax.Precision.HIGHEST
@@ -125,23 +125,63 @@
     return narrow_ref[pl.ds(0, rows, stride=2), :] + narrow_ref[pl.ds(1, rows, stride=2), :]
 
 
-def pack_kernel(material_ref, force_ref, stiff_ref, low_ref, high_ref, coarse_ref, sums):
-    own = own_plane(material_ref)
+def pack_kernel(
+    material_hbm, force_hbm, stiff_hbm, low_ref, high_ref, coarse_ref, material, stiff, sums, sems
+):
+    copies = [
+        pltpu.make_async_copy(stiff_hbm, stiff, sems.at[0]),
+        pltpu.make_async_copy(material_hbm, material, sems.at[1]),
+    ]
     for c in range(3):
-        for p in range(3):
-            low_ref[3 * c + p] = force_ref[0, c, p]
-            high_ref[3 * c + p] = force_ref[0, c, CX - 3 + p]
-    coef = [stiff_ref[p] * own for p in range(CX)]
-    for p in range(4):
+        rows = pl.ds(3 * c, 3)
+        copies += [
+            pltpu.make_async_copy(force_hbm.at[0, c, pl.ds(0, 3)], low_ref.at[rows], sems.at[2 + c]),
+            pltpu.make_async_copy(
+                force_hbm.at[0, c, pl.ds(CX - 3, 3)], high_ref.at[rows], sems.at[5 + c]
+            ),
+        ]
+    for copy in copies:
+        copy.start()
+    for copy in copies:
+        copy.wait()
+    own = own_plane(material)
+    sh = Shifts((NY, NZ))
+    coef = [stiff[p] * own for p in range(CX)]
+    for p in range(3):
         low_ref[9 + p] = coef[p]
-        high_ref[9 + p] = coef[CX - 4 + p]
+        high_ref[9 + p] = coef[CX - 3 + p]
+    for ref, p, slot in ((low_ref, 2, 2), (high_ref, CX - 3, 0)):
+        scale = (1.0 / MIDPOINT) / diagonal(sh, coef[p - 1], coef[p], coef[p + 1])
+        for c in range(3):
+            ref[3 * c + slot] = ref[3 * c + slot] * scale
     pairs = jnp.concatenate([coef[2 * p] + coef[2 * p + 1] for p in range(HX)], axis=0)
     coarse = (0.125 * coarse_sum(pairs, sums)).reshape(HX, HY, HZ)
     coarse_ref[...] = coarse
     for p in range(HX):
         y, z = (p // 2) * HY, (p % 2) * HZ
-        low_ref[13, y : y + HY, z : z + HZ] = coarse[p]
-        high_ref[13, y : y + HY, z : z + HZ] = coarse[p]
+        low_ref[PACK - 1, y : y + HY, z : z + HZ] = coarse[p]
+        high_ref[PACK - 1, y : y + HY, z : z + HZ] = coarse[p]
+
+
+def plan_kernel(count_ref, source_ref, target_ref, line_ref, column_ref, where_ref, index_ref):
+    slabs = count_ref.shape[1]
+    lane = lax.broadcasted_iota(jnp.int32, (1, SLOTS), 1)
+    cells = target_ref[0]
+    line_ref[...] = lax.shift_right_logical(cells, 7).astype(F32)
+    column_ref[...] = (cells & (HZ - 1)).astype(F32)
+
+    def place(o, at):
+        where_ref[o] = at
+        tile = lax.shift_right_logical(at, 8)
+        offset = at & (SLOTS - 1)
+        turned = pltpu.roll(source_ref[0, pl.ds(o, 1), :], offset, 1)
+        index_ref[pl.ds(tile, 1), :] = jnp.where(
+            lane >= offset, turned, index_ref[pl.ds(tile, 1), :]
+        )
+        index_ref[pl.ds(tile + 1, 1), :] = turned
+        return at + count_ref[0, o]
+
+    where_ref[slabs] = lax.fori_loop(0, slabs, place, jnp.int32(0))
 
 
 def unpack_coarse(plane_ref):
@@ -154,6 +194,7 @@
 def fine_kernel(
     material_ref,
     count_ref,
+    where_ref,
     force_ref,
     stiff_ref,
     below_ref,
@@ -173,6 +214,7 @@
     table,
     sums,
     residual,
+    found,
 ):
     slab = lax.axis_index("space")
     slabs = lax.axis_size("space")
@@ -181,22 +223,24 @@
     has_below = slab > 0
     has_above = slab < slabs - 1
     for p in range(CX):
-        coef[4 + p] = stiff_ref[p] * own
-    for p in range(4):
+        coef[3 + p] = stiff_ref[p] * own
+    for p in range(3):
         coef[p] = jnp.where(has_below, below_ref[9 + p], 0.0)
-        coef[4 + CX + p] = jnp.where(has_above, above_ref[9 + p], 0.0)
+        coef[3 + CX + p] = jnp.where(has_above, above_ref[9 + p], 0.0)
     for c in range(3):
-        for p in range(3):
-            force[c, p] = below_ref[3 * c + p]
+        first[c, 0] = jnp.where(has_below, below_ref[3 * c], 0.0)
+        first[c, FINE_PLANES - 1] = jnp.where(has_above, above_ref[3 * c + 2], 0.0)
+        for p in range(2):
+            force[c, 1 + p] = below_ref[3 * c + 1 + p]
             force[c, 3 + CX + p] = above_ref[3 * c + p]
         for p in range(CX):
             force[c, 3 + p] = force_ref[0, c, p]
 
-    @pl.loop(0, FINE_PLANES)
+    @pl.loop(1, FINE_PLANES - 1)
     def _(p):
-        d = diagonal(sh, coef[p], coef[p + 1], coef[p + 2])
-        where = slab * CX + p - 3
-        valid = jnp.logical_and(where >= 0, where < slabs * CX)
+        d = diagonal(sh, coef[p - 1], coef[p], coef[p + 1])
+        place = slab * CX + p - 3
+        valid = jnp.logical_and(place >= 0, place < slabs * CX)
         inv = jnp.where(valid, 1.0 / d, 0.0)
         diag[p] = d
         inverse[p] = inv
@@ -205,7 +249,7 @@
 
     def remainder(src, p, base):
         planes = [[src[c, p + o - base] for c in range(3)] for o in (-1, 0, 1)]
-        image = operate(sh, *planes, coef[p], coef[p + 1], coef[p + 2], diag[p])
+        image = operate(sh, *planes, coef[p - 1], coef[p], coef[p + 1], diag[p])
         return planes[1], [force[c, p] - image[c] for c in range(3)]
 
     (keep_2, gain_2), (keep_3, gain_3) = step_factors(FINE_STEPS)
@@ -234,7 +278,7 @@
             table[pl.ds(row, NY), NZ : 2 * NZ] = (left[c] - head.astype(F32)).astype(BF16)
 
     for p in range(CX + 2):
-        coef_out_ref[p] = coef[p + 3]
+        coef_out_ref[p] = coef[p + 2]
     for p in range(CX):
         diag_out_ref[p] = diag[p + 3]
 
@@ -243,23 +287,43 @@
     coarse_ref[...] = 0.5 * coarse_sum(pairs, sums)
 
     plane_rows = CX * NY
-    column = lax.broadcasted_iota(jnp.int32, (NZ, SLOTS), 0)
-    line = lax.broadcasted_iota(jnp.int32, (plane_rows, SLOTS), 0)
-    slot = lax.broadcasted_iota(jnp.int32, (1, SLOTS), 1)
-
-    @pl.loop(0, slabs)
-    def _(o):
-        index = index_ref[0, pl.ds(o, 1), :]
-        hot = (column == (index & (NZ - 1))).astype(BF16)
+    groups = plane_rows // 8
+    column = lax.broadcasted_iota(jnp.int32, (NZ, SLOTS), 0).astype(F32).astype(BF16)
+    line = lax.broadcasted_iota(jnp.int32, (8, SLOTS), 0)
+    lane = lax.broadcasted_iota(jnp.int32, (8, SLOTS), 1)
+    one = jnp.ones((), BF16)
+    zero = jnp.zeros((), BF16)
+
+    def pick(t):
+        index = index_ref[pl.ds(t, 1), :]
+        group = lax.shift_right_logical(index, 11)
+        inner = line == (lax.shift_right_logical(index, 8) & 7)
+        hot = jnp.where(column == (index & (NZ - 1)).astype(F32).astype(BF16), one, zero)
         both = jnp.dot(table[:, 0:NZ], hot, preferred_element_type=F32) + jnp.dot(
             table[:, NZ : 2 * NZ], hot, preferred_element_type=F32
         )
-        chosen = line == lax.shift_right_logical(index, 8)
-        live = slot < count_ref[0, o]
-        for c in range(3):
-            part = jnp.where(chosen, both[c * plane_rows : (c + 1) * plane_rows, :], 0.0)
-            value = jnp.sum(part, axis=0, keepdims=True)
-            picked_ref[pl.ds(o, 1), c * SLOTS : (c + 1) * SLOTS] = jnp.where(live, value, 0.0)
+        for c in range(3):
+            held = both[c * plane_rows : c * plane_rows + 8, :]
+            for g in range(1, groups):
+                at = c * plane_rows + 8 * g
+                held = jnp.where(group == g, both[at : at + 8, :], held)
+            found[t, c : c + 1, :] = jnp.sum(jnp.where(inner, held, 0.0), axis=0, keepdims=True)
+
+    @pl.loop(0, lax.shift_right_logical(where_ref[slabs] + 2 * SLOTS - 1, 9))
+    def _(pair):
+        pick(2 * pair)
+        pick(2 * pair + 1)
+
+    @pl.loop(0, slabs, unroll=4)
+    def _(o):
+        at = where_ref[o]
+        tile = lax.shift_right_logical(at, 8)
+        offset = at & (SLOTS - 1)
+        joined = jnp.where(lane >= offset, found[tile], found[tile + 1])
+        turned = pltpu.roll(joined, SLOTS - offset, 1)
+        turned = jnp.where(lane < count_ref[0, o], turned, 0.0)
+        for c in range(3):
+            picked_ref[pl.ds(o, 1), c * SLOTS : (c + 1) * SLOTS] = turned[c : c + 1, :]
 
 
 def coarse_extent(below_pack_ref, coarse_ref, above_pack_ref, slab, slabs):
@@ -270,7 +334,8 @@
 
 def gather_kernel(
     arrived_ref,
-    target_ref,
+    line_ref,
+    column_ref,
     local_ref,
     coef_below_ref,
     coef_ref,
@@ -279,39 +344,40 @@
     low_ref,
     high_ref,
     total,
-    rows,
 ):
     slab = lax.axis_index("space")
     slabs = lax.axis_size("space")
-    half_rows = HX * HY * HZ // SLOTS
-    column = lax.broadcasted_iota(jnp.int32, (SLOTS, SLOTS), 0)
-    line = lax.broadcasted_iota(jnp.int32, (half_rows, SLOTS), 0)
+    lines = HX * HY
+    column = lax.broadcasted_iota(jnp.int32, (HZ, SLOTS), 0).astype(F32).astype(BF16)
+    line = lax.broadcasted_iota(jnp.int32, (lines, SLOTS), 0).astype(F32).astype(BF16)
     total[...] = jnp.zeros_like(total)
-
-    @pl.loop(0, slabs)
+    one = jnp.ones((), BF16)
+    zero = jnp.zeros((), BF16)
+
+    @pl.loop(0, slabs, step=4)
     def _(s):
-        index = target_ref[0, pl.ds(s, 1), :]
-        hot = (column == (index & (SLOTS - 1))).astype(BF16)
-        chosen = line == lax.shift_right_logical(index, 8)
-        parts = [
-            jnp.where(chosen, arrived_ref[pl.ds(s, 1), c * SLOTS : (c + 1) * SLOTS], 0.0)
-            for c in range(3)
-        ]
-        values = jnp.concatenate(parts, axis=0)
-        head = values.astype(BF16)
-        tail = (values - head.astype(F32)).astype(BF16)
-        total[...] += lax.dot_general(
-            jnp.concatenate([head, tail], axis=0),
-            hot,
-            (((1,), (1,)), ((), ())),
-            preferred_element_type=F32,
-        )
-
-    count = 3 * half_rows
-    joined = total[0:count, :] + total[count : 2 * count, :]
-    rows[pl.ds(0, count, stride=2), :] = joined[:, 0:HZ]
-    rows[pl.ds(1, count, stride=2), :] = joined[:, HZ:]
-    source = (rows[...] + local_ref[...]).reshape(3, HX, HY, HZ)
+        add = None
+        for u in range(4):
+            hot = jnp.where(column == column_ref[pl.ds(s + u, 1), :].astype(BF16), one, zero)
+            chosen = line == line_ref[pl.ds(s + u, 1), :].astype(BF16)
+            heads, tails = [], []
+            for c in range(3):
+                value = arrived_ref[pl.ds(s + u, 1), c * SLOTS : (c + 1) * SLOTS]
+                head = value.astype(BF16)
+                tail = (value - head.astype(F32)).astype(BF16)
+                heads.append(jnp.where(chosen, head, zero))
+                tails.append(jnp.where(chosen, tail, zero))
+            part = lax.dot_general(
+                jnp.concatenate(heads + tails, axis=0),
+                hot,
+                (((1,), (1,)), ((), ())),
+                preferred_element_type=F32,
+            )
+            add = part if add is None else add + part
+        total[...] += add
+
+    count = 3 * lines
+    source = (total[0:count, :] + total[count : 2 * count, :] + local_ref[...]).reshape(3, HX, HY, HZ)
     source_ref[...] = source
     low_ref[...] = source
     high_ref[...] = source
@@ -422,18 +488,8 @@
                 ref[...] = energy[:, y : y + part, :]
 
 
-def close_kernel(material_ref, kept_ref, got_1_ref, got_2_ref, got_3_ref, out_ref):
-    mine = lax.axis_index("load")
-    ident = jnp.where(mine < 2, material_ref[0, 0], material_ref[0, 1])
-    total = kept_ref[...] + got_1_ref[...] + got_2_ref[...] + got_3_ref[...]
-    base = np.array(MODULI, np.float32)
-    for m in range(3):
-        factor = [float((base[m] - base[i]) / base[i]) for i in range(3)]
-        scale = jnp.where(ident == 0, factor[0], jnp.where(ident == 1, factor[1], factor[2]))
-        out_ref[m] = total * scale.astype(F32)
-
-
 VMEM = pl.BlockSpec(memory_space=pltpu.VMEM)
+HBM = pl.BlockSpec(memory_space=pltpu.HBM)
 SMEM = pl.BlockSpec(memory_space=pltpu.SMEM)
 PARAMS = pltpu.CompilerParams(vmem_limit_bytes=32 << 20)
 
@@ -449,14 +505,34 @@
     pack_low, pack_high, coarse_coef = pl.pallas_call(
         pack_kernel,
         out_shape=(shaped(PACK, NY, NZ), shaped(PACK, NY, NZ), shaped(HX, HY, HZ)),
-        in_specs=[SMEM, VMEM, VMEM],
+        in_specs=[HBM, HBM, HBM],
         out_specs=(VMEM, VMEM, VMEM),
-        scratch_shapes=[pltpu.VMEM((HX * NY, HZ), F32)],
+        scratch_shapes=[
+            pltpu.SMEM((1, NY // BY), jnp.int32),
+            pltpu.VMEM((CX, NY, NZ), F32),
+            pltpu.VMEM((HX * NY, HZ), F32),
+            pltpu.SemaphoreType.DMA((8,)),
+        ],
         compiler_params=PARAMS,
         name="pack",
     )(material, load_force, stiffness)
     below = lax.ppermute(pack_high, "space", forward)
     above = lax.ppermute(pack_low, "space", backward)
+
+    rows_kept = slabs + 8
+    line, column, where, index = pl.pallas_call(
+        plan_kernel,
+        out_shape=(
+            shaped(slabs, SLOTS),
+            shaped(slabs, SLOTS),
+            jax.ShapeDtypeStruct((slabs + 1,), jnp.int32),
+            jax.ShapeDtypeStruct((rows_kept, SLOTS), jnp.int32),
+        ),
+        in_specs=[SMEM, VMEM, VMEM],
+        out_specs=(VMEM, VMEM, SMEM, VMEM),
+        compiler_params=PARAMS,
+        name="plan",
+    )(face_count, face_src, face_dst)
 
     smooth, coef, diag, local, picked = pl.pallas_call(
         fine_kernel,
@@ -467,7 +543,7 @@
             shaped(3 * HX * HY, HZ),
             shaped(slabs, 3 * SLOTS),
         ),
-        in_specs=[SMEM, SMEM, VMEM, VMEM, VMEM, VMEM, VMEM],
+        in_specs=[SMEM, SMEM, SMEM, VMEM, VMEM, VMEM, VMEM, VMEM],
         out_specs=(VMEM, VMEM, VMEM, VMEM, VMEM),
         scratch_shapes=[
             pltpu.VMEM((COEF_PLANES, NY, NZ), F32),
@@ -479,10 +555,11 @@
             pltpu.VMEM((3 * CX * NY, 2 * NZ), BF16),
             pltpu.VMEM((3 * HX * NY, HZ), F32),
             pltpu.VMEM((3 * CX * NY, NZ), F32),
+            pltpu.VMEM((rows_kept, 8, SLOTS), F32),
         ],
         compiler_params=PARAMS,
         name="fine",
-    )(material, face_count, load_force, stiffness, below, above, face_src)
+    )(material, face_count, where, load_force, stiffness, below, above, index)
 
     arrived = lax.all_to_all(picked, "space", split_axis=0, concat_axis=0, tiled=True)
 
@@ -498,7 +575,8 @@
         out_shape=(shaped(*grid_shape), shaped(*grid_shape), shaped(*grid_shape)),
         in_specs=[
             whole(slabs, 3 * SLOTS),
-            whole(1, slabs, SLOTS),
+            whole(slabs, SLOTS),
+            whole(slabs, SLOTS),
             whole(3 * HX * HY, HZ),
             tail,
             whole(HX, HY, HZ),
@@ -506,12 +584,11 @@
         ],
         out_specs=(whole(*grid_shape), whole(*grid_shape), whole(*grid_shape)),
         scratch_shapes=[
-            pltpu.VMEM((6 * HX * HY * HZ // SLOTS, SLOTS), F32),
-            pltpu.VMEM((3 * HX * HY, HZ), F32),
+            pltpu.VMEM((6 * HX * HY, HZ), F32),
         ],
         compiler_params=PARAMS,
         name="reflux",
-    )(arrived, face_dst, local, below, coarse_coef, above)
+    )(arrived, line, column, local, below, coarse_coef, above)
     source_below = lax.ppermute(send_high, "space", forward)
     source_above = lax.ppermute(send_low, "space", backward)
 
@@ -544,13 +621,13 @@
         lax.ppermute(piece, "load", [(i, (i + k) % 4) for i in range(4)])
         for k, piece in ((1, sent_1), (2, sent_2), (3, sent_3))
     ]
-    sensitivity = pl.pallas_call(
-        close_kernel,
-        out_shape=shaped(3, *part),
-        in_specs=[SMEM, VMEM, VMEM, VMEM, VMEM],
-        out_specs=VMEM,
-        name="close",
-    )(material, kept, *got)
+    mine = lax.axis_index("load")
+    ident = jnp.where(mine < 2, material[0, 0], material[0, 1])
+    base = np.array(MODULI, np.float32)
+    factors = jnp.asarray((base[None, :] - base[:, None]) / base[:, None])
+    scale = jnp.where(ident == 0, factors[0], jnp.where(ident == 1, factors[1], factors[2]))
+    total = kept + got[0] + got[1] + got[2]
+    sensitivity = scale[:, None, None, None] * total[None]
     return moved, sensitivity
 
 

time: 109 us -> 86.4 us (0.79)
  Pallas kernels: 43.2 us -> 27.1 us
  waiting for transfers between devices: 13.1 us -> 6.89 us
  between operations: 0.7 us -> 2.07 us
  blocking collectives: 19.1 us -> 17.8 us
    pallas_call x1, Pallas kernels: 25.1 us -> 12.3 us  [body(): pl.pallas_call(fine_kernel, out_shape=(shaped(3, CX + 2, NY, NZ), shaped(...]
    pallas_call x1, Pallas kernels: 12.7 us -> 4.61 us  [body(): pl.pallas_call(gather_kernel, grid=(1,), out_shape=(shaped(*grid_shape),...]
    ppermute x1, waiting for transfers between devices: 4.71 us -> 0.01 us  [body(): below = lax.ppermute(pack_high, 'space', forward)]
    pallas_call x1, Pallas kernels: 1.47 us -> 6.06 us  [body(): pl.pallas_call(plan_kernel, out_shape=(shaped(slabs, SLOTS), shaped(slabs...]
    ppermute x1, waiting for transfers between devices: 1.47 us -> 0.01 us  [body(): source_below = lax.ppermute(send_high, 'space', forward)]
    all_to_all x1, blocking collectives: 19.1 us -> 17.8 us  [body(): lax.all_to_all(picked, 'space', split_axis=0, concat_axis=0, tiled=True)]
    unnamed x21 -> x23, local copies, waits for them, and re-layouts: 4.61 us -> 3.7 us
  transfers between devices with their start and end apart: 7 -> 7, of which waited for: 5 -> 2; matrix products, arithmetic and copies ran while one was open for 0% -> 1% of each run, Pallas kernels for 0% -> 7%
where the time goes in v2:
time: 86.4 us
  starting transfers between devices  27.3 us (32%)
  Pallas kernels  27.1 us (31%)
  blocking collectives  17.8 us (21%)
  waiting for transfers between devices  6.89 us (8%)
  local copies, waits for them, and re-layouts  4.49 us (5%)
  between operations  2.07 us (2%)
    all_to_all x1, blocking collectives, body(): lax.all_to_all(picked, 'space', split_axis=0, concat_axis=0, tiled=True)  17.8 us
    pallas_call x1, Pallas kernels, body(): pl.pallas_call(fine_kernel, out_shape=(shaped(3, CX + 2, NY, NZ), shaped(...  12.3 us
    ppermute x3, starting transfers between devices, body(): lax.ppermute(piece, 'load', [(i, (i + k) % 4) for i in range(4)])  9.74 us
    ppermute x1, starting transfers between devices, body(): above = lax.ppermute(pack_low, 'space', backward)  7.44 us
    ppermute x1, starting transfers between devices, body(): source_above = lax.ppermute(send_low, 'space', backward)  7.07 us
    ppermute x3, waiting for transfers between devices, body(): lax.ppermute(piece, 'load', [(i, (i + k) % 4) for i in range(4)])  6.88 us
    pallas_call x1, Pallas kernels, body(): pl.pallas_call(plan_kernel, out_shape=(shaped(slabs, SLOTS), shaped(slabs...  6.06 us
    pallas_call x1, Pallas kernels, body(): pl.pallas_call(gather_kernel, grid=(1,), out_shape=(shaped(*grid_shape),...  4.61 us
  transfers between devices with their start and end apart: 7, of which 2 were waited for; matrix products, arithmetic and copies ran while one was open for 1% of the time, Pallas kernels for 7%

profile of v2, /device:TPU:1, one launch (start us, length us, event | category | flops | bytes accessed | tf_op | source)
XLA Modules:
  0.0 86.4 jit_solution(11943747888695143996)
XLA Ops:
  0.6 1.0 %copy-done = f32[1,3,8,16,256]{4,3,2,1,0:T(8,128)S(1)} copy-done((f32[1,3,8,16,256]{4,3,2,1,0:T(8,128)S(1)}, f32[1,3,8,16,256]{4,3,2,1,0:T(8,128)}, u32[]{:S(2)}) %copy-start) | copy-done | bytes 393240
  1.6 0.9 %copy-done.2 = f32[8,16,256]{2,1,0:T(8,128)S(1)} copy-done((f32[8,16,256]{2,1,0:T(8,128)S(1)}, f32[8,16,256]{2,1,0:T(8,128)}, u32[]{:S(2)}) %copy-start.2) | copy-done | bytes 131096
  2.5 0.7 copy-done.5
  3.2 1.0 %pack.1 = (f32[13,16,256]{2,1,0:T(8,128)S(1)}, f32[13,16,256]{2,1,0:T(8,128)S(1)}, f32[4,8,128]{2,1,0:T(8,128)S(1)}) custom-call(s32[1,2]{1,0:T(1,128)S(1)} %copy-done.5, f32[1,3,8,16,256]{4,3,2,1,0:T(8,128)S(1)} %copy-done, f32[8,16,256]{2,1,0:T(8,128)S(1)} %copy-done.2), custom_call_target="tpu_custom_call" | custom-call | tf_op jit(solution)/shard_map/pack/pallas_call | solution.py:505
  4.2 2.5 %collective-permute-start = (f32[13,16,256]{2,1,0:T(8,128)S(1)}, f32[13,16,256]{2,1,0:T(8,128)S(1)}, u32[]{:S(2)}, u32[]{:S(2)}) collective-permute-start(f32[13,16,256]{2,1,0:T(8,128)S(1)} %get-tuple-element.23), channel_id=1, source_target_pairs={{0,4},{4,8},{8,12},{12,16},{16,20},{20,24},{24,28},{28,32},{32,36}... | collective-permute-start | bytes 638984 | tf_op jit(solution)/shard_map/ppermute | solution.py:519
  6.8 7.4 %collective-permute-start.1 = (f32[13,16,256]{2,1,0:T(8,128)S(1)}, f32[13,16,256]{2,1,0:T(8,128)S(1)}, u32[]{:S(2)}, u32[]{:S(2)}) collective-permute-start(f32[13,16,256]{2,1,0:T(8,128)S(1)} %get-tuple-element.24), channel_id=1, source_target_pairs={{4,0},{8,4},{12,8},{16,12},{20,16},{24,20},{28,24},{32,28},{36,32}... | collective-permute-start | bytes 638984 | tf_op jit(solution)/shard_map/ppermute | solution.py:520
  14.2 6.1 %plan.1 = (f32[64,256]{1,0:T(8,128)S(1)}, f32[64,256]{1,0:T(8,128)S(1)}, s32[65]{0:T(128)S(1)}, s32[72,256]{1,0:T(8,128)S(1)}) custom-call(s32[1,64]{1,0:T(1,128)S(1)} %copy-done.7, s32[1,64,256]{2,1,0:T(8,128)S(1)} %copy-done.3, s32[1,64,256]{2,1,0:T(8,128)S(1)} %copy-done.4), custom_call_target="tpu_custom_call" | custom-call | tf_op jit(solution)/shard_map/plan/pallas_call | solution.py:523
  20.3 0.6 copy-done.6
  21.0 12.3 %fine.1 = (f32[3,10,16,256]{3,2,1,0:T(8,128)S(1)}, f32[10,16,256]{2,1,0:T(8,128)S(1)}, f32[8,16,256]{2,1,0:T(8,128)S(1)}, f32[96,128]{1,0:T(8,128)S(1)}, f32[64,768]{1,0:T(8,128)S(1)}) custom-call(s32[1,2]{1,0:T(1,128)S(1)} %copy-done.6, s32[1,64]{1,0:T(1,128)S(1)} %copy-done.7, s32[65]{0:T(128)S(1)} %get-tuple-element.22.where_ref, ...), custom_call_target="tpu_custom_call" | custom-call | tf_op jit(solution)/shard_map/fine/pallas_call | solution.py:537
  33.3 0.2 copy.9
  33.5 17.8 %all_to_all.11 = f32[64,1,768]{2,1,0:T(1,128)S(1)} all-to-all(f32[64,1,768]{2,1,0:T(1,128)S(1)} %copy.9), channel_id=1, replica_groups=mesh['space'=64,'load'=4] {'space'}, dimensions={0} | all-to-all | bytes 393216 | tf_op jit(solution)/shard_map/all_to_all | solution.py:564
  51.4 4.6 %reflux.1 = (f32[3,4,8,128]{3,2,1,0:T(8,128)S(1)}, f32[3,4,8,128]{3,2,1,0:T(8,128)S(1)}, f32[3,4,8,128]{3,2,1,0:T(8,128)S(1)}) custom-call(f32[64,768]{1,0:T(8,128)S(1)} %bitcast.13, f32[64,256]{1,0:T(8,128)S(1)} %get-tuple-element.27.line_ref, f32[64,256]{1,0:T(8,128)S(1)} %get-tuple-element.28.column_ref, f32[96,128]{1,0:T(8,128)S(1)} %get-tuple-element.29.local_ref, ...), custom_call_target="tpu_custom_call" | custom-call | tf_op jit(solution)/shard_map/reflux/pallas_call | solution.py:572
  56.0 0.5 collective-permute-start.2
  56.5 7.1 %collective-permute-start.3 = (f32[3,4,8,128]{3,2,1,0:T(8,128)S(1)}, f32[3,4,8,128]{3,2,1,0:T(8,128)S(1)}, u32[]{:S(2)}, u32[]{:S(2)}) collective-permute-start(f32[3,4,8,128]{3,2,1,0:T(8,128)S(1)} %get-tuple-element.33), channel_id=1, source_target_pairs={{4,0},{8,4},{12,8},{16,12},{20,16},{24,20},{28,24},{32,28},{36,32}... | collective-permute-start | bytes 147464 | tf_op jit(solution)/shard_map/ppermute | solution.py:593
  63.6 0.6 fusion.1
  65.5 3.1 %coarse.1 = (f32[1,3,8,16,256]{4,3,2,1,0:T(8,128)}, f32[8,4,256]{2,1,0:T(4,128)S(1)}, f32[8,4,256]{2,1,0:T(4,128)S(1)}, f32[8,4,256]{2,1,0:T(4,128)S(1)}, f32[8,4,256]{2,1,0:T(4,128)S(1)}) custom-call(f32[3,4,8,128]{3,2,1,0:T(8,128)S(1)} %get-tuple-element.31.source_ref, f32[3,4,8,128]{3,2,1,0:T(8,128)S(1)} %collective-permute-done.2.below_ref, ...), custom_call_target="tpu_custom_call" | custom-call | tf_op jit(solution)/shard_map/coarse/pallas_call | solution.py:596
  68.6 9.5 %collective-permute-start.4 = (f32[8,4,256]{2,1,0:T(4,128)S(1)}, f32[8,4,256]{2,1,0:T(4,128)S(1)}, u32[]{:S(2)}, u32[]{:S(2)}) collective-permute-start(f32[8,4,256]{2,1,0:T(4,128)S(1)} %get-tuple-element.39), channel_id=1, source_target_pairs={{0,1},{1,2},{2,3},{3,0},{4,5},{5,6},{6,7},{7,4},{8,9},{9,10},{10,1... | collective-permute-start | bytes 98312 | tf_op jit(solution)/shard_map/ppermute | solution.py:621
  78.1 0.2 collective-permute-start.5
  78.3 0.4 copy-done.8
  78.8 0.0 copy-done.9
  78.8 0.0 copy-done.10
  78.8 0.7 collective-permute-done.4
  79.5 6.2 %collective-permute-done.6 = f32[8,4,256]{2,1,0:T(4,128)S(1)} collective-permute-done((f32[8,4,256]{2,1,0:T(4,128)S(1)}, f32[8,4,256]{2,1,0:T(4,128)S(1)}, u32[]{:S(2)}, u32[]{:S(2)}) %collective-permute-start.6) | collective-permute-done | bytes 32800 | tf_op jit(solution)/shard_map/ppermute | solution.py:621
  85.7 0.7 broadcast_multiply_fusion
  (24 shorter events, 0.1 us)
Async XLA Ops:
  0.6 1.0 %copy-start = (f32[1,3,8,16,256]{4,3,2,1,0:T(8,128)S(1)}, f32[1,3,8,16,256]{4,3,2,1,0:T(8,128)}, u32[]{:S(2)}) copy-start(f32[1,3,8,16,256]{4,3,2,1,0:T(8,128)} %force_ref.1) | copy-start | bytes 1179652
  1.6 0.9 %copy-start.2 = (f32[8,16,256]{2,1,0:T(8,128)S(1)}, f32[8,16,256]{2,1,0:T(8,128)}, u32[]{:S(2)}) copy-start(f32[8,16,256]{2,1,0:T(8,128)} %stiff_ref.1) | copy-start | bytes 393220
  2.5 0.7 copy-start.5
  3.2 11.0 %copy-start.3 = (s32[1,64,256]{2,1,0:T(8,128)S(1)}, s32[1,64,256]{2,1,0:T(8,128)}, u32[]{:S(2)}) copy-start(s32[1,64,256]{2,1,0:T(8,128)} %source_ref.1) | copy-start | bytes 196612
  3.2 11.0 %copy-start.4 = (s32[1,64,256]{2,1,0:T(8,128)S(1)}, s32[1,64,256]{2,1,0:T(8,128)}, u32[]{:S(2)}) copy-start(s32[1,64,256]{2,1,0:T(8,128)} %target_ref.1) | copy-start | bytes 196612
  3.2 17.1 %copy-start.1 = (f32[1,3,8,16,256]{4,3,2,1,0:T(8,128)S(1)}, f32[1,3,8,16,256]{4,3,2,1,0:T(8,128)}, u32[]{:S(2)}) copy-start(f32[1,3,8,16,256]{4,3,2,1,0:T(8,128)} %force_ref.1) | copy-start | bytes 1179652
  4.2 10.0 %copy-start.7 = (s32[1,64]{1,0:T(1,128)S(1)}, s32[1,64]{1,0:T(1,128)}, u32[]{:S(2)}) copy-start(s32[1,64]{1,0:T(1,128)} %count_ref.3) | copy-start | bytes 772
  4.2 16.1 %collective-permute-start = (f32[13,16,256]{2,1,0:T(8,128)S(1)}, f32[13,16,256]{2,1,0:T(8,128)S(1)}, u32[]{:S(2)}, u32[]{:S(2)}) collective-permute-start(f32[13,16,256]{2,1,0:T(8,128)S(1)} %get-tuple-element.23), channel_id=1, source_target_pairs={{0,4},{4,8},{8,12},{12,16},{16,20},{20,24},{24,28},{28,32},{32,36}... | collective-permute-start | bytes 638984 | tf_op jit(solution)/shard_map/ppermute | solution.py:519
  6.8 13.5 %collective-permute-start.1 = (f32[13,16,256]{2,1,0:T(8,128)S(1)}, f32[13,16,256]{2,1,0:T(8,128)S(1)}, u32[]{:S(2)}, u32[]{:S(2)}) collective-permute-start(f32[13,16,256]{2,1,0:T(8,128)S(1)} %get-tuple-element.24), channel_id=1, source_target_pairs={{4,0},{8,4},{12,8},{16,12},{20,16},{24,20},{28,24},{32,28},{36,32}... | collective-permute-start | bytes 638984 | tf_op jit(solution)/shard_map/ppermute | solution.py:520
  20.3 0.7 copy-start.6
  56.0 9.4 %collective-permute-start.2 = (f32[3,4,8,128]{3,2,1,0:T(8,128)S(1)}, f32[3,4,8,128]{3,2,1,0:T(8,128)S(1)}, u32[]{:S(2)}, u32[]{:S(2)}) collective-permute-start(f32[3,4,8,128]{3,2,1,0:T(8,128)S(1)} %get-tuple-element.32), channel_id=1, source_target_pairs={{0,4},{4,8},{8,12},{12,16},{16,20},{20,24},{24,28},{28,32},{32,36}... | collective-permute-start | bytes 147464 | tf_op jit(solution)/shard_map/ppermute | solution.py:592
  56.5 9.0 %collective-permute-start.3 = (f32[3,4,8,128]{3,2,1,0:T(8,128)S(1)}, f32[3,4,8,128]{3,2,1,0:T(8,128)S(1)}, u32[]{:S(2)}, u32[]{:S(2)}) collective-permute-start(f32[3,4,8,128]{3,2,1,0:T(8,128)S(1)} %get-tuple-element.33), channel_id=1, source_target_pairs={{4,0},{8,4},{12,8},{16,12},{20,16},{24,20},{28,24},{32,28},{36,32}... | collective-permute-start | bytes 147464 | tf_op jit(solution)/shard_map/ppermute | solution.py:593
  68.6 10.9 %collective-permute-start.4 = (f32[8,4,256]{2,1,0:T(4,128)S(1)}, f32[8,4,256]{2,1,0:T(4,128)S(1)}, u32[]{:S(2)}, u32[]{:S(2)}) collective-permute-start(f32[8,4,256]{2,1,0:T(4,128)S(1)} %get-tuple-element.39), channel_id=1, source_target_pairs={{0,1},{1,2},{2,3},{3,0},{4,5},{5,6},{6,7},{7,4},{8,9},{9,10},{10,1... | collective-permute-start | bytes 98312 | tf_op jit(solution)/shard_map/ppermute | solution.py:621
  78.1 0.7 copy-start.8
  78.1 0.7 copy-start.9
  78.1 0.7 copy-start.10
  78.1 7.6 %collective-permute-start.6 = (f32[8,4,256]{2,1,0:T(4,128)S(1)}, f32[8,4,256]{2,1,0:T(4,128)S(1)}, u32[]{:S(2)}, u32[]{:S(2)}) collective-permute-start(f32[8,4,256]{2,1,0:T(4,128)S(1)} %get-tuple-element.41), channel_id=1, source_target_pairs={{0,3},{1,0},{2,1},{3,2},{4,7},{5,4},{6,5},{7,6},{8,11},{9,8},{10,9... | collective-permute-start | bytes 98312 | tf_op jit(solution)/shard_map/ppermute | solution.py:621
  78.1 7.6 %collective-permute-start.5 = (f32[8,4,256]{2,1,0:T(4,128)S(1)}, f32[8,4,256]{2,1,0:T(4,128)S(1)}, u32[]{:S(2)}, u32[]{:S(2)}) collective-permute-start(f32[8,4,256]{2,1,0:T(4,128)S(1)} %get-tuple-element.40), channel_id=1, source_target_pairs={{0,2},{1,3},{2,0},{3,1},{4,6},{5,7},{6,4},{7,5},{8,10},{9,11},{10,... | collective-permute-start | bytes 98312 | tf_op jit(solution)/shard_map/ppermute | solution.py:621

commit v3 on v2

--- a/solution.py
+++ b/solution.py
@@ -26,6 +26,8 @@
 FINE_PLANES = CX + 6
 COEF_PLANES = CX + 6
 PACK = 3 * 3 + 3 + 1
+BATCH = 32
+UNROLL = 2
 F32 = jnp.float32
 BF16 = jnp.bfloat16
 HIGHEST = lax.Precision.HIGHEST
@@ -42,39 +44,59 @@
     return factors
 
 
+def tiles(plane):
+    return jnp.stack([plane[:HY, :HZ], plane[:HY, HZ:], plane[HY:, :HZ], plane[HY:, HZ:]])
+
+
+def plane(quarters):
+    return jnp.concatenate(
+        [
+            jnp.concatenate([quarters[0], quarters[1]], axis=1),
+            jnp.concatenate([quarters[2], quarters[3]], axis=1),
+        ],
+        axis=0,
+    )
+
+
 class Shifts:
-    def __init__(self, shape):
-        self.nd = len(shape)
-        self.shape = shape
-        y = lax.broadcasted_iota(jnp.int32, shape, self.nd - 2)
-        z = lax.broadcasted_iota(jnp.int32, shape, self.nd - 1)
-        self.edge = {
-            self.nd - 2: (y == 0, y == shape[-2] - 1),
-            self.nd - 1: (z == 0, z == shape[-1] - 1),
-        }
-
-    def pair(self, x, axis):
-        first, last = self.edge[axis]
-        size = self.shape[axis]
-        below = jnp.where(first, 0.0, pltpu.roll(x, 1, axis))
-        above = jnp.where(last, 0.0, pltpu.roll(x, size - 1, axis))
-        return below, above
-
-    def diff(self, x, axis):
-        below, above = self.pair(x, axis)
-        return above - below
-
-    def dy(self, x):
-        return self.diff(x, self.nd - 2)
-
-    def dz(self, x):
-        return self.diff(x, self.nd - 1)
+    def __init__(self, count, quarters):
+        shape = (count, HY, HZ)
+        y = lax.broadcasted_iota(jnp.int32, shape, 1)
+        z = lax.broadcasted_iota(jnp.int32, shape, 2)
+        self.quarters = quarters
+        self.first_y, self.last_y = y == 0, y == HY - 1
+        self.first_z, self.last_z = z == 0, z == HZ - 1
+
+    def fill(self, turned, order):
+        if not self.quarters:
+            return 0.0
+        zero = jnp.zeros((HY, HZ), F32)
+        return jnp.stack([zero if i is None else turned[i] for i in order])
+
+    def up_y(self, x):
+        turned = pltpu.roll(x, HY - 1, 1)
+        return jnp.where(self.last_y, self.fill(turned, (2, 3, None, None)), turned)
+
+    def down_y(self, x):
+        turned = pltpu.roll(x, 1, 1)
+        return jnp.where(self.first_y, self.fill(turned, (None, None, 0, 1)), turned)
+
+    def up_z(self, x):
+        turned = pltpu.roll(x, HZ - 1, 2)
+        return jnp.where(self.last_z, self.fill(turned, (1, None, 3, None)), turned)
+
+    def down_z(self, x):
+        turned = pltpu.roll(x, 1, 2)
+        return jnp.where(self.first_z, self.fill(turned, (None, 0, None, 2)), turned)
+
+    def spread_y(self, x):
+        return x + 0.5 * (self.up_y(x) + self.down_y(x))
+
+    def spread_z(self, x):
+        return x + 0.5 * (self.up_z(x) + self.down_z(x))
 
     def spread(self, x):
-        for axis in (self.nd - 2, self.nd - 1):
-            below, above = self.pair(x, axis)
-            x = x + 0.5 * (below + above)
-        return x
+        return self.spread_z(self.spread_y(x))
 
 
 def diagonal(sh, k_below, k_mid, k_above):
@@ -84,20 +106,27 @@
 def operate(sh, below, mid, above, k_below, k_mid, k_above, diag):
     centre = diag + (1.0 / 7.0) * k_mid
     slope = [above[c] - below[c] for c in range(3)]
-    mixed = (
-        sh.dy(slope[1]) + sh.dz(slope[2]),
-        sh.dy(slope[0] + sh.dz(mid[2])),
-        sh.dz(slope[0] + sh.dy(mid[1])),
+    cross = 0.25 * COUPLING
+    plain = [mid[c] + 0.5 * (below[c] + above[c]) for c in range(3)]
+
+    def close_y(x, skew):
+        x, skew, own = (1.0 / 28.0) * x, cross * skew, (1.0 / 14.0) * x
+        return own + sh.up_y(x + skew) + sh.down_y(x - skew)
+
+    def close_z(x, skew):
+        x, skew, own = (1.0 / 28.0) * x, cross * skew, (1.0 / 14.0) * x
+        return own + sh.up_z(x + skew) + sh.down_z(x - skew)
+
+    inner = (
+        close_z(sh.spread_y(plain[0]), slope[2])
+        + cross * (sh.up_y(slope[1]) - sh.down_y(slope[1])),
+        close_y(sh.spread_z(plain[1]), slope[0] + (sh.up_z(mid[2]) - sh.down_z(mid[2]))),
+        close_z(sh.spread_y(plain[2]), slope[0] + (sh.up_y(mid[1]) - sh.down_y(mid[1]))),
     )
     result = []
     for c in range(3):
-        plain = sh.spread(mid[c] + 0.5 * (below[c] + above[c]))
         scaled = sh.spread(k_mid * mid[c] + 0.5 * (k_below * below[c] + k_above * above[c]))
-        result.append(
-            centre * mid[c]
-            - (1.0 / 14.0) * (k_mid * plain + scaled)
-            - (0.25 * COUPLING) * (k_mid * mixed[c])
-        )
+        result.append(centre * mid[c] - k_mid * inner[c] - (1.0 / 14.0) * scaled)
     return result
 
 
@@ -126,7 +155,9 @@
 
 
 def pack_kernel(
-    material_hbm, force_hbm, stiff_hbm, low_ref, high_ref, coarse_ref, material, stiff, sums, sems
+    material_hbm, force_hbm, stiff_hbm,
+    low_ref, high_ref, coarse_ref, coef_ref,
+    material, stiff, sums, sems,
 ):
     copies = [
         pltpu.make_async_copy(stiff_hbm, stiff, sems.at[0]),
@@ -145,13 +176,16 @@
     for copy in copies:
         copy.wait()
     own = own_plane(material)
-    sh = Shifts((NY, NZ))
+    sh = Shifts(4, True)
     coef = [stiff[p] * own for p in range(CX)]
+    for p in range(CX):
+        coef_ref[p] = coef[p]
     for p in range(3):
         low_ref[9 + p] = coef[p]
         high_ref[9 + p] = coef[CX - 3 + p]
     for ref, p, slot in ((low_ref, 2, 2), (high_ref, CX - 3, 0)):
-        scale = (1.0 / MIDPOINT) / diagonal(sh, coef[p - 1], coef[p], coef[p + 1])
+        scale = (1.0 / MIDPOINT) / diagonal(sh, *[tiles(coef[p + o]) for o in (-1, 0, 1)])
+        scale = plane(scale)
         for c in range(3):
             ref[3 * c + slot] = ref[3 * c + slot] * scale
     pairs = jnp.concatenate([coef[2 * p] + coef[2 * p + 1] for p in range(HX)], axis=0)
@@ -192,11 +226,10 @@
 
 
 def fine_kernel(
-    material_ref,
     count_ref,
     where_ref,
     force_ref,
-    stiff_ref,
+    own_ref,
     below_ref,
     above_ref,
     index_ref,
@@ -218,12 +251,11 @@
 ):
     slab = lax.axis_index("space")
     slabs = lax.axis_size("space")
-    sh = Shifts((NY, NZ))
-    own = own_plane(material_ref)
+    sh = Shifts(4, True)
     has_below = slab > 0
     has_above = slab < slabs - 1
     for p in range(CX):
-        coef[3 + p] = stiff_ref[p] * own
+        coef[3 + p] = own_ref[p]
     for p in range(3):
         coef[p] = jnp.where(has_below, below_ref[9 + p], 0.0)
         coef[3 + CX + p] = jnp.where(has_above, above_ref[9 + p], 0.0)
@@ -238,7 +270,7 @@
 
     @pl.loop(1, FINE_PLANES - 1)
     def _(p):
-        d = diagonal(sh, coef[p - 1], coef[p], coef[p + 1])
+        d = plane(diagonal(sh, *[tiles(coef[p + o]) for o in (-1, 0, 1)]))
         place = slab * CX + p - 3
         valid = jnp.logical_and(place >= 0, place < slabs * CX)
         inv = jnp.where(valid, 1.0 / d, 0.0)
@@ -248,34 +280,38 @@
             first[c, p] = force[c, p] * inv * (1.0 / MIDPOINT)
 
     def remainder(src, p, base):
-        planes = [[src[c, p + o - base] for c in range(3)] for o in (-1, 0, 1)]
-        image = operate(sh, *planes, coef[p - 1], coef[p], coef[p + 1], diag[p])
-        return planes[1], [force[c, p] - image[c] for c in range(3)]
+        planes = [[tiles(src[c, p + o - base]) for c in range(3)] for o in (-1, 0, 1)]
+        factors = [tiles(coef[p + o]) for o in (-1, 0, 1)]
+        image = operate(sh, *planes, *factors, tiles(diag[p]))
+        return planes[1], [tiles(force[c, p]) - image[c] for c in range(3)]
 
     (keep_2, gain_2), (keep_3, gain_3) = step_factors(FINE_STEPS)
 
-    @pl.loop(1, FINE_PLANES - 1)
+    @pl.loop(1, FINE_PLANES - 1, unroll=UNROLL)
     def _(p):
         value, left = remainder(first, p, 0)
-        for c in range(3):
-            second[c, p] = (1.0 + keep_2) * value[c] + gain_2 * (left[c] * inverse[p])
-
-    @pl.loop(2, FINE_PLANES - 2)
+        inv = tiles(inverse[p])
+        for c in range(3):
+            second[c, p] = plane((1.0 + keep_2) * value[c] + gain_2 * (left[c] * inv))
+
+    @pl.loop(2, FINE_PLANES - 2, unroll=UNROLL)
     def _(p):
         value, left = remainder(second, p, 0)
-        for c in range(3):
-            step = keep_3 * (value[c] - first[c, p]) + gain_3 * (left[c] * inverse[p])
-            smooth_ref[c, p - 2] = value[c] + step
-
-    @pl.loop(3, FINE_PLANES - 3)
+        inv = tiles(inverse[p])
+        for c in range(3):
+            step = keep_3 * (value[c] - tiles(first[c, p])) + gain_3 * (left[c] * inv)
+            smooth_ref[c, p - 2] = plane(value[c] + step)
+
+    @pl.loop(3, FINE_PLANES - 3, unroll=UNROLL)
     def _(p):
         _, left = remainder(smooth_ref, p, 2)
         for c in range(3):
             row = pl.multiple_of(c * (CX * NY) + (p - 3) * NY, NY)
-            residual[pl.ds(row, NY), :] = left[c]
-            head = left[c].astype(BF16)
+            whole = plane(left[c])
+            residual[pl.ds(row, NY), :] = whole
+            head = whole.astype(BF16)
             table[pl.ds(row, NY), 0:NZ] = head
-            table[pl.ds(row, NY), NZ : 2 * NZ] = (left[c] - head.astype(F32)).astype(BF16)
+            table[pl.ds(row, NY), NZ : 2 * NZ] = (whole - head.astype(F32)).astype(BF16)
 
     for p in range(CX + 2):
         coef_out_ref[p] = coef[p + 2]
@@ -354,11 +390,11 @@
     one = jnp.ones((), BF16)
     zero = jnp.zeros((), BF16)
 
-    @pl.loop(0, slabs, step=4)
+    @pl.loop(0, slabs, step=BATCH)
     def _(s):
-        add = None
-        for u in range(4):
-            hot = jnp.where(column == column_ref[pl.ds(s + u, 1), :].astype(BF16), one, zero)
+        hots, lefts = [], []
+        for u in range(BATCH):
+            hots.append(jnp.where(column == column_ref[pl.ds(s + u, 1), :].astype(BF16), one, zero))
             chosen = line == line_ref[pl.ds(s + u, 1), :].astype(BF16)
             heads, tails = [], []
             for c in range(3):
@@ -367,14 +403,13 @@
                 tail = (value - head.astype(F32)).astype(BF16)
                 heads.append(jnp.where(chosen, head, zero))
                 tails.append(jnp.where(chosen, tail, zero))
-            part = lax.dot_general(
-                jnp.concatenate(heads + tails, axis=0),
-                hot,
-                (((1,), (1,)), ((), ())),
-                preferred_element_type=F32,
-            )
-            add = part if add is None else add + part
-        total[...] += add
+            lefts.append(jnp.concatenate(heads + tails, axis=0))
+        total[...] += lax.dot_general(
+            jnp.concatenate(lefts, axis=1),
+            jnp.concatenate(hots, axis=1),
+            (((1,), (1,)), ((), ())),
+            preferred_element_type=F32,
+        )
 
     count = 3 * lines
     source = (total[0:count, :] + total[count : 2 * count, :] + local_ref[...]).reshape(3, HX, HY, HZ)
@@ -382,10 +417,10 @@
     low_ref[...] = source
     high_ref[...] = source
     coef = coarse_extent(coef_below_ref, coef_ref, coef_above_ref, slab, slabs)
-    sh = Shifts((HY, HZ))
+    sh = Shifts(1, False)
     for ref, p in ((high_ref, 0), (low_ref, HX - 1)):
-        d = diagonal(sh, coef[HX + p - 1], coef[HX + p], coef[HX + p + 1])
-        scale = (1.0 / MIDPOINT) / d
+        d = diagonal(sh, *[coef[HX + p + o][None] for o in (-1, 0, 1)])
+        scale = (1.0 / MIDPOINT) / d[0]
         for c in range(3):
             ref[c, p] = source[c, p] * scale
 
@@ -404,7 +439,6 @@
     kept_ref,
     sent_1_ref,
     sent_2_ref,
-    sent_3_ref,
     rows,
     field,
     energy,
@@ -419,7 +453,7 @@
     count = 3 * HX - 2
     place = lax.broadcasted_iota(jnp.int32, (count, HY, HZ), 0) + (slab * HX - HX + 1)
     valid = jnp.logical_and(place >= 0, place < slabs * HX)
-    diag = diagonal(Shifts((count, HY, HZ)), coef[:-2], coef[1:-1], coef[2:])
+    diag = diagonal(Shifts(count, False), coef[:-2], coef[1:-1], coef[2:])
     inverse = jnp.where(valid, 1.0 / diag, 0.0)
     older = None
     value = []
@@ -433,7 +467,7 @@
         inside = slice(number, number + size)
         window = slice(number + 1, number + 1 + size)
         image = operate(
-            Shifts((size, HY, HZ)),
+            Shifts(size, False),
             [v[:-2] for v in value],
             [v[1:-1] for v in value],
             [v[2:] for v in value],
@@ -467,25 +501,23 @@
             if 0 < p <= CX:
                 moved_ref[0, c, p - 1] = moved
 
-    sh = Shifts((NY, NZ))
-
-    @pl.loop(1, CX + 1)
+    sh = Shifts(4, True)
+
+    @pl.loop(1, CX + 1, unroll=UNROLL)
     def _(p):
-        planes = [[field[c, p + o] for c in range(3)] for o in (-1, 0, 1)]
-        image = operate(
-            sh, *planes, coef_ref[p - 1], coef_ref[p], coef_ref[p + 1], diag_ref[p - 1]
-        )
+        planes = [[tiles(field[c, p + o]) for c in range(3)] for o in (-1, 0, 1)]
+        factors = [tiles(coef_ref[p + o]) for o in (-1, 0, 1)]
+        image = operate(sh, *planes, *factors, tiles(diag_ref[p - 1]))
         mid = planes[1]
-        energy[p - 1] = mid[0] * image[0] + mid[1] * image[1] + mid[2] * image[2]
+        energy[p - 1] = plane(mid[0] * image[0] + mid[1] * image[1] + mid[2] * image[2])
 
     part = NY // 4
     for q in range(4):
 
         @pl.when(mine == q)
         def _():
-            for k, ref in enumerate((kept_ref, sent_1_ref, sent_2_ref, sent_3_ref)):
-                y = ((q + k) % 4) * part
-                ref[...] = energy[:, y : y + part, :]
+            for ref, owner in ((kept_ref, q), (sent_1_ref, q ^ 1), (sent_2_ref.at[0], q ^ 2), (sent_2_ref.at[1], q ^ 3)):
+                ref[...] = energy[:, owner * part : owner * part + part, :]
 
 
 VMEM = pl.BlockSpec(memory_space=pltpu.VMEM)
@@ -502,11 +534,16 @@
     slabs = lax.axis_size("space")
     forward = [(i, (i + 1) % slabs) for i in range(slabs)]
     backward = [(target, origin) for origin, target in forward]
-    pack_low, pack_high, coarse_coef = pl.pallas_call(
+    pack_low, pack_high, coarse_coef, own_coef = pl.pallas_call(
         pack_kernel,
-        out_shape=(shaped(PACK, NY, NZ), shaped(PACK, NY, NZ), shaped(HX, HY, HZ)),
+        out_shape=(
+            shaped(PACK, NY, NZ),
+            shaped(PACK, NY, NZ),
+            shaped(HX, HY, HZ),
+            shaped(CX, NY, NZ),
+        ),
         in_specs=[HBM, HBM, HBM],
-        out_specs=(VMEM, VMEM, VMEM),
+        out_specs=(VMEM, VMEM, VMEM, VMEM),
         scratch_shapes=[
             pltpu.SMEM((1, NY // BY), jnp.int32),
             pltpu.VMEM((CX, NY, NZ), F32),
@@ -515,7 +552,9 @@
         ],
         compiler_params=PARAMS,
         name="pack",
-    )(material, load_force, stiffness)
+    )(*[
+        pltpu.with_memory_space_constraint(x, pltpu.HBM) for x in (material, load_force, stiffness)
+    ])
     below = lax.ppermute(pack_high, "space", forward)
     above = lax.ppermute(pack_low, "space", backward)
 
@@ -543,7 +582,7 @@
             shaped(3 * HX * HY, HZ),
             shaped(slabs, 3 * SLOTS),
         ),
-        in_specs=[SMEM, SMEM, SMEM, VMEM, VMEM, VMEM, VMEM, VMEM],
+        in_specs=[SMEM, SMEM, VMEM, VMEM, VMEM, VMEM, VMEM],
         out_specs=(VMEM, VMEM, VMEM, VMEM, VMEM),
         scratch_shapes=[
             pltpu.VMEM((COEF_PLANES, NY, NZ), F32),
@@ -559,7 +598,7 @@
         ],
         compiler_params=PARAMS,
         name="fine",
-    )(material, face_count, where, load_force, stiffness, below, above, index)
+    )(face_count, where, load_force, own_coef, below, above, index)
 
     arrived = lax.all_to_all(picked, "space", split_axis=0, concat_axis=0, tiled=True)
 
@@ -593,10 +632,10 @@
     source_above = lax.ppermute(send_low, "space", backward)
 
     part = (CX, NY // 4, NZ)
-    moved, kept, sent_1, sent_2, sent_3 = pl.pallas_call(
+    moved, kept, near, far = pl.pallas_call(
         coarse_kernel,
         grid=(1,),
-        out_shape=(shaped(1, 3, CX, NY, NZ),) + (shaped(*part),) * 4,
+        out_shape=(shaped(1, 3, CX, NY, NZ),) + (shaped(*part),) * 2 + (shaped(2, *part),),
         in_specs=[
             whole(*grid_shape),
             whole(*grid_shape),
@@ -608,7 +647,7 @@
             whole(CX + 2, NY, NZ),
             whole(CX, NY, NZ),
         ],
-        out_specs=(whole(1, 3, CX, NY, NZ),) + (whole(*part),) * 4,
+        out_specs=(whole(1, 3, CX, NY, NZ),) + (whole(*part),) * 2 + (whole(2, *part),),
         scratch_shapes=[
             pltpu.VMEM((3 * (HX + 2) * NY, HZ), F32),
             pltpu.VMEM((3, CX + 2, NY, NZ), F32),
@@ -617,16 +656,14 @@
         compiler_params=PARAMS,
         name="coarse",
     )(source, source_below, source_above, below, coarse_coef, above, smooth, coef, diag)
-    got = [
-        lax.ppermute(piece, "load", [(i, (i + k) % 4) for i in range(4)])
-        for k, piece in ((1, sent_1), (2, sent_2), (3, sent_3))
-    ]
+    got = lax.ppermute(far, "load", [(i, i ^ 2) for i in range(4)])
+    last = lax.ppermute(near + got[1], "load", [(i, i ^ 1) for i in range(4)])
     mine = lax.axis_index("load")
     ident = jnp.where(mine < 2, material[0, 0], material[0, 1])
     base = np.array(MODULI, np.float32)
     factors = jnp.asarray((base[None, :] - base[:, None]) / base[:, None])
     scale = jnp.where(ident == 0, factors[0], jnp.where(ident == 1, factors[1], factors[2]))
-    total = kept + got[0] + got[1] + got[2]
+    total = (kept + got[0]) + last
     sensitivity = scale[:, None, None, None] * total[None]
     return moved, sensitivity
 

time: 86.4 us -> 75.7 us (0.88)
  waiting for transfers between devices: 6.89 us -> 2.99 us
  Pallas kernels: 27.1 us -> 23.4 us
  local copies, waits for them, and re-layouts: 4.49 us -> 0.84 us
  starting transfers between devices: 27.3 us -> 28.2 us
    ppermute x3 -> x2, waiting for transfers between devices: 6.88 us -> 1.5 us  [the longest x1 0.84 us: body(): last = lax.ppermute(near + got[1], 'load', [(i, i ^ 1) for i in range(4)])]
    unnamed x23 -> x17, local copies, waits for them, and re-layouts: 3.7 us -> 0.05 us
    pallas_call x1, Pallas kernels: 4.61 us -> 2.09 us  [body(): pl.pallas_call(gather_kernel, grid=(1,), out_shape=(shaped(*grid_shape),...]
    ppermute x1, waiting for transfers between devices: 0.01 us -> 1.47 us  [body(): source_below = lax.ppermute(send_high, 'space', forward)]
    pallas_call x1, Pallas kernels: 12.3 us -> 11.3 us  [body(): pl.pallas_call(fine_kernel, out_shape=(shaped(3, CX + 2, NY, NZ), shaped(...]
    ppermute x3 -> x2, starting transfers between devices: 9.74 us -> 10.7 us  [the longest x1 5.78 us: body(): got = lax.ppermute(far, 'load', [(i, i ^ 2) for i in range(4)])]
  transfers between devices with their start and end apart: 7 -> 6, of which waited for: 2 -> 3; matrix products, arithmetic and copies ran while one was open for 1% -> 1% of each run, Pallas kernels for 7% -> 8%
where the time goes in v3:
time: 75.7 us; the launch traced here: 75.4 us
  starting transfers between devices  28.2 us (37%)
  Pallas kernels  23.4 us (31%)
  blocking collectives  17 us (22%)
  waiting for transfers between devices  2.99 us (4%)
  between operations  2.1 us (3%)
  local copies, waits for them, and re-layouts  0.84 us (1%)
    all_to_all x1, blocking collectives, body(): lax.all_to_all(picked, 'space', split_axis=0, concat_axis=0, tiled=True)  17 us
    pallas_call x1, Pallas kernels, body(): pl.pallas_call(fine_kernel, out_shape=(shaped(3, CX + 2, NY, NZ), shaped(...  11.3 us
    ppermute x1, starting transfers between devices, body(): above = lax.ppermute(pack_low, 'space', backward)  7.44 us
    ppermute x1, starting transfers between devices, body(): source_above = lax.ppermute(send_low, 'space', backward)  7.06 us
    pallas_call x1, Pallas kernels, body(): pl.pallas_call(plan_kernel, out_shape=(shaped(slabs, SLOTS), shaped(slabs...  6.06 us
    ppermute x1, starting transfers between devices, body(): got = lax.ppermute(far, 'load', [(i, i ^ 2) for i in range(4)])  5.78 us
    ppermute x1, starting transfers between devices, body(): last = lax.ppermute(near + got[1], 'load', [(i, i ^ 1) for i in range(4)])  4.91 us
    pallas_call x1, Pallas kernels, body(): pl.pallas_call(coarse_kernel, grid=(1,), out_shape=(shaped(1, 3, CX, NY,...  2.6 us
  transfers between devices with their start and end apart: 6, of which 3 were waited for; matrix products, arithmetic and copies ran while one was open for 1% of the time, Pallas kernels for 8%

profile of v3, /device:TPU:1, one launch (start us, length us, event | category | flops | bytes accessed | tf_op | source)
XLA Modules:
  0.0 75.4 jit_solution(15668489139995700303)
XLA Ops:
  0.7 1.4 %pack.1 = (f32[13,16,256]{2,1,0:T(8,128)S(1)}, f32[13,16,256]{2,1,0:T(8,128)S(1)}, f32[4,8,128]{2,1,0:T(8,128)S(1)}, f32[8,16,256]{2,1,0:T(8,128)S(1)}) custom-call(s32[1,2]{1,0:T(1,128)} %material_hbm.1, f32[1,3,8,16,256]{4,3,2,1,0:T(8,128)} %force_ref.1, f32[8,16,256]{2,1,0:T(8,128)} %stiff_hbm.1), custom_call_target="tpu_custom_call" | custom-call | tf_op jit(solution)/shard_map/pack/pallas_call | solution.py:537
  2.0 0.0 copy-start.3
  2.0 2.5 %collective-permute-start = (f32[13,16,256]{2,1,0:T(8,128)S(1)}, f32[13,16,256]{2,1,0:T(8,128)S(1)}, u32[]{:S(2)}, u32[]{:S(2)}) collective-permute-start(f32[13,16,256]{2,1,0:T(8,128)S(1)} %get-tuple-element.24), channel_id=1, source_target_pairs={{0,4},{4,8},{8,12},{12,16},{16,20},{20,24},{24,28},{28,32},{32,36}... | collective-permute-start | bytes 638984 | tf_op jit(solution)/shard_map/ppermute | solution.py:558
  4.6 7.4 %collective-permute-start.1 = (f32[13,16,256]{2,1,0:T(8,128)S(1)}, f32[13,16,256]{2,1,0:T(8,128)S(1)}, u32[]{:S(2)}, u32[]{:S(2)}) collective-permute-start(f32[13,16,256]{2,1,0:T(8,128)S(1)} %get-tuple-element.25), channel_id=1, source_target_pairs={{4,0},{8,4},{12,8},{16,12},{20,16},{24,20},{28,24},{32,28},{36,32}... | collective-permute-start | bytes 638984 | tf_op jit(solution)/shard_map/ppermute | solution.py:559
  12.0 0.0 copy-done.1
  12.0 6.1 %plan.1 = (f32[64,256]{1,0:T(8,128)S(1)}, f32[64,256]{1,0:T(8,128)S(1)}, s32[65]{0:T(128)S(1)}, s32[72,256]{1,0:T(8,128)S(1)}) custom-call(s32[1,64]{1,0:T(1,128)S(1)} %copy-done.3, s32[1,64,256]{2,1,0:T(8,128)S(1)} %copy-done.1, s32[1,64,256]{2,1,0:T(8,128)S(1)} %copy-done.2), custom_call_target="tpu_custom_call" | custom-call | tf_op jit(solution)/shard_map/plan/pallas_call | solution.py:562
  18.1 0.0 collective-permute-done.below_ref.coef_below_ref
  18.1 0.0 collective-permute-done.1.above_ref.coef_above_ref
  18.1 0.0 copy-done
  18.1 11.3 %fine.1 = (f32[3,10,16,256]{3,2,1,0:T(8,128)S(1)}, f32[10,16,256]{2,1,0:T(8,128)S(1)}, f32[8,16,256]{2,1,0:T(8,128)S(1)}, f32[96,128]{1,0:T(8,128)S(1)}, f32[64,768]{1,0:T(8,128)S(1)}) custom-call(s32[1,64]{1,0:T(1,128)S(1)} %copy-done.3, s32[65]{0:T(128)S(1)} %get-tuple-element.22.where_ref, f32[1,3,8,16,256]{4,3,2,1,0:T(8,128)S(1)} %copy-done, ...), custom_call_target="tpu_custom_call" | custom-call | tf_op jit(solution)/shard_map/fine/pallas_call | solution.py:576
  29.4 0.2 copy.9
  29.7 17.0 %all_to_all.11 = f32[64,1,768]{2,1,0:T(1,128)S(1)} all-to-all(f32[64,1,768]{2,1,0:T(1,128)S(1)} %copy.9), channel_id=1, replica_groups=mesh['space'=64,'load'=4] {'space'}, dimensions={0} | all-to-all | bytes 393216 | tf_op jit(solution)/shard_map/all_to_all | solution.py:603
  46.7 2.1 %reflux.1 = (f32[3,4,8,128]{3,2,1,0:T(8,128)S(1)}, f32[3,4,8,128]{3,2,1,0:T(8,128)S(1)}, f32[3,4,8,128]{3,2,1,0:T(8,128)S(1)}) custom-call(f32[64,768]{1,0:T(8,128)S(1)} %bitcast.18, f32[64,256]{1,0:T(8,128)S(1)} %get-tuple-element.28.line_ref, f32[64,256]{1,0:T(8,128)S(1)} %get-tuple-element.29.column_ref, f32[96,128]{1,0:T(8,128)S(1)} %get-tuple-element.30.local_ref, ...), custom_call_target="tpu_custom_call" | custom-call | tf_op jit(solution)/shard_map/reflux/pallas_call | solution.py:611
  48.8 0.5 collective-permute-start.2
  49.3 7.1 %collective-permute-start.3 = (f32[3,4,8,128]{3,2,1,0:T(8,128)S(1)}, f32[3,4,8,128]{3,2,1,0:T(8,128)S(1)}, u32[]{:S(2)}, u32[]{:S(2)}) collective-permute-start(f32[3,4,8,128]{3,2,1,0:T(8,128)S(1)} %get-tuple-element.34), channel_id=1, source_target_pairs={{4,0},{8,4},{12,8},{16,12},{20,16},{24,20},{28,24},{32,28},{36,32}... | collective-permute-start | bytes 147464 | tf_op jit(solution)/shard_map/ppermute | solution.py:632
  56.4 1.5 %collective-permute-done.2.below_ref = f32[3,4,8,128]{3,2,1,0:T(8,128)S(1)} collective-permute-done((f32[3,4,8,128]{3,2,1,0:T(8,128)S(1)}, f32[3,4,8,128]{3,2,1,0:T(8,128)S(1)}, u32[]{:S(2)}, u32[]{:S(2)}) %collective-permute-start.2) | collective-permute-done | bytes 49184 | tf_op jit(solution)/shard_map/ppermute | solution.py:631
  57.9 0.0 collective-permute-done.3.above_ref
  57.9 2.6 %coarse.1 = (f32[1,3,8,16,256]{4,3,2,1,0:T(8,128)}, f32[8,4,256]{2,1,0:T(4,128)S(1)}, f32[8,4,256]{2,1,0:T(4,128)S(1)}, f32[2,8,4,256]{3,2,1,0:T(4,128)S(1)}) custom-call(f32[3,4,8,128]{3,2,1,0:T(8,128)S(1)} %get-tuple-element.32.source_ref, f32[3,4,8,128]{3,2,1,0:T(8,128)S(1)} %collective-permute-done.2.below_ref, ...), custom_call_target="tpu_custom_call" | custom-call | tf_op jit(solution)/shard_map/coarse/pallas_call | solution.py:635
  60.5 5.8 %collective-permute-start.4 = (f32[2,8,4,256]{3,2,1,0:T(4,128)S(1)}, f32[2,8,4,256]{3,2,1,0:T(4,128)S(1)}, u32[]{:S(2)}, u32[]{:S(2)}) collective-permute-start(f32[2,8,4,256]{3,2,1,0:T(4,128)S(1)} %get-tuple-element.40), channel_id=1, source_target_pairs={{0,2},{1,3},{2,0},{3,1},{4,6},{5,7},{6,4},{7,5},{8,10},{9,11},{10,... | collective-permute-start | bytes 196616 | tf_op jit(solution)/shard_map/ppermute | solution.py:659
  66.2 0.6 fusion.4
  68.2 0.7 collective-permute-done.4
  68.9 4.9 %collective-permute-start.5 = (f32[8,4,256]{2,1,0:T(4,128)S(1)}, f32[8,4,256]{2,1,0:T(4,128)S(1)}, u32[]{:S(2)}, u32[]{:S(2)}) collective-permute-start(f32[8,4,256]{2,1,0:T(4,128)S(1)} %fusion), channel_id=1, source_target_pairs={{0,1},{1,0},{2,3},{3,2},{4,5},{5,4},{6,7},{7,6},{8,9},{9,8},{10,11... | collective-permute-start | bytes 98312 | tf_op jit(solution)/shard_map/ppermute | solution.py:660
  73.8 0.8 %collective-permute-done.5 = f32[8,4,256]{2,1,0:T(4,128)S(1)} collective-permute-done((f32[8,4,256]{2,1,0:T(4,128)S(1)}, f32[8,4,256]{2,1,0:T(4,128)S(1)}, u32[]{:S(2)}, u32[]{:S(2)}) %collective-permute-start.5) | collective-permute-done | bytes 32800 | tf_op jit(solution)/shard_map/ppermute | solution.py:660
  74.6 0.7 broadcast_multiply_fusion
  (17 shorter events, 0.1 us)
Async XLA Ops:
  0.6 17.5 %copy-start = (f32[1,3,8,16,256]{4,3,2,1,0:T(8,128)S(1)}, f32[1,3,8,16,256]{4,3,2,1,0:T(8,128)}, u32[]{:S(2)}) copy-start(f32[1,3,8,16,256]{4,3,2,1,0:T(8,128)} %force_ref.1) | copy-start | bytes 1179652
  0.6 11.4 %copy-start.1 = (s32[1,64,256]{2,1,0:T(8,128)S(1)}, s32[1,64,256]{2,1,0:T(8,128)}, u32[]{:S(2)}) copy-start(s32[1,64,256]{2,1,0:T(8,128)} %source_ref.1) | copy-start | bytes 196612
  0.7 11.4 %copy-start.2 = (s32[1,64,256]{2,1,0:T(8,128)S(1)}, s32[1,64,256]{2,1,0:T(8,128)}, u32[]{:S(2)}) copy-start(s32[1,64,256]{2,1,0:T(8,128)} %target_ref.1) | copy-start | bytes 196612
  2.0 10.0 %copy-start.3 = (s32[1,64]{1,0:T(1,128)S(1)}, s32[1,64]{1,0:T(1,128)}, u32[]{:S(2)}) copy-start(s32[1,64]{1,0:T(1,128)} %count_ref.3) | copy-start | bytes 772
  2.0 16.1 %collective-permute-start = (f32[13,16,256]{2,1,0:T(8,128)S(1)}, f32[13,16,256]{2,1,0:T(8,128)S(1)}, u32[]{:S(2)}, u32[]{:S(2)}) collective-permute-start(f32[13,16,256]{2,1,0:T(8,128)S(1)} %get-tuple-element.24), channel_id=1, source_target_pairs={{0,4},{4,8},{8,12},{12,16},{16,20},{20,24},{24,28},{28,32},{32,36}... | collective-permute-start | bytes 638984 | tf_op jit(solution)/shard_map/ppermute | solution.py:558
  4.6 13.5 %collective-permute-start.1 = (f32[13,16,256]{2,1,0:T(8,128)S(1)}, f32[13,16,256]{2,1,0:T(8,128)S(1)}, u32[]{:S(2)}, u32[]{:S(2)}) collective-permute-start(f32[13,16,256]{2,1,0:T(8,128)S(1)} %get-tuple-element.25), channel_id=1, source_target_pairs={{4,0},{8,4},{12,8},{16,12},{20,16},{24,20},{28,24},{32,28},{36,32}... | collective-permute-start | bytes 638984 | tf_op jit(solution)/shard_map/ppermute | solution.py:559
  48.8 9.0 %collective-permute-start.2 = (f32[3,4,8,128]{3,2,1,0:T(8,128)S(1)}, f32[3,4,8,128]{3,2,1,0:T(8,128)S(1)}, u32[]{:S(2)}, u32[]{:S(2)}) collective-permute-start(f32[3,4,8,128]{3,2,1,0:T(8,128)S(1)} %get-tuple-element.33), channel_id=1, source_target_pairs={{0,4},{4,8},{8,12},{12,16},{16,20},{20,24},{24,28},{28,32},{32,36}... | collective-permute-start | bytes 147464 | tf_op jit(solution)/shard_map/ppermute | solution.py:631
  49.3 8.5 %collective-permute-start.3 = (f32[3,4,8,128]{3,2,1,0:T(8,128)S(1)}, f32[3,4,8,128]{3,2,1,0:T(8,128)S(1)}, u32[]{:S(2)}, u32[]{:S(2)}) collective-permute-start(f32[3,4,8,128]{3,2,1,0:T(8,128)S(1)} %get-tuple-element.34), channel_id=1, source_target_pairs={{4,0},{8,4},{12,8},{16,12},{20,16},{24,20},{28,24},{32,28},{36,32}... | collective-permute-start | bytes 147464 | tf_op jit(solution)/shard_map/ppermute | solution.py:632
  60.5 5.8 %copy-start.4 = (s32[1,2]{1,0:T(1,128)S(1)}, s32[1,2]{1,0:T(1,128)}, u32[]{:S(2)}) copy-start(s32[1,2]{1,0:T(1,128)} %material_hbm.1) | copy-start | bytes 28
  60.5 8.4 %collective-permute-start.4 = (f32[2,8,4,256]{3,2,1,0:T(4,128)S(1)}, f32[2,8,4,256]{3,2,1,0:T(4,128)S(1)}, u32[]{:S(2)}, u32[]{:S(2)}) collective-permute-start(f32[2,8,4,256]{3,2,1,0:T(4,128)S(1)} %get-tuple-element.40), channel_id=1, source_target_pairs={{0,2},{1,3},{2,0},{3,1},{4,6},{5,7},{6,4},{7,5},{8,10},{9,11},{10,... | collective-permute-start | bytes 196616 | tf_op jit(solution)/shard_map/ppermute | solution.py:659
  68.8 4.9 %copy-start.5 = (f32[1,3]{1,0:T(1,128)S(1)}, f32[1,3]{1,0:T(1,128)}, u32[]{:S(2)}) copy-start(f32[1,3]{1,0:T(1,128)} %constant.19) | copy-start | bytes 40
  68.8 4.9 %copy-start.6 = (f32[1,3]{1,0:T(1,128)S(1)}, f32[1,3]{1,0:T(1,128)}, u32[]{:S(2)}) copy-start(f32[1,3]{1,0:T(1,128)} %constant.20) | copy-start | bytes 40
  68.8 4.9 %copy-start.7 = (f32[1,3]{1,0:T(1,128)S(1)}, f32[1,3]{1,0:T(1,128)}, u32[]{:S(2)}) copy-start(f32[1,3]{1,0:T(1,128)} %constant.21) | copy-start | bytes 40
  68.9 5.8 %collective-permute-start.5 = (f32[8,4,256]{2,1,0:T(4,128)S(1)}, f32[8,4,256]{2,1,0:T(4,128)S(1)}, u32[]{:S(2)}, u32[]{:S(2)}) collective-permute-start(f32[8,4,256]{2,1,0:T(4,128)S(1)} %fusion), channel_id=1, source_target_pairs={{0,1},{1,0},{2,3},{3,2},{4,5},{5,4},{6,7},{7,6},{8,9},{9,8},{10,11... | collective-permute-start | bytes 98312 | tf_op jit(solution)/shard_map/ppermute | solution.py:660

commit v4 on v3

--- a/solution.py
+++ b/solution.py
@@ -27,7 +27,7 @@
 COEF_PLANES = CX + 6
 PACK = 3 * 3 + 3 + 1
 BATCH = 32
-UNROLL = 2
+UNROLL = 4
 F32 = jnp.float32
 BF16 = jnp.bfloat16
 HIGHEST = lax.Precision.HIGHEST
@@ -197,25 +197,73 @@
         high_ref[PACK - 1, y : y + HY, z : z + HZ] = coarse[p]
 
 
-def plan_kernel(count_ref, source_ref, target_ref, line_ref, column_ref, where_ref, index_ref):
+def plan_kernel(
+    count_ref,
+    source_ref,
+    target_ref,
+    force_ref,
+    coef_ref,
+    line_ref,
+    column_ref,
+    where_ref,
+    index_ref,
+    diag_ref,
+    first_ref,
+    second_ref,
+    third_ref,
+):
     slabs = count_ref.shape[1]
     lane = lax.broadcasted_iota(jnp.int32, (1, SLOTS), 1)
     cells = target_ref[0]
     line_ref[...] = lax.shift_right_logical(cells, 7).astype(F32)
     column_ref[...] = (cells & (HZ - 1)).astype(F32)
 
-    def place(o, at):
+    def place(o, carry):
+        at, row = carry
         where_ref[o] = at
         tile = lax.shift_right_logical(at, 8)
         offset = at & (SLOTS - 1)
         turned = pltpu.roll(source_ref[0, pl.ds(o, 1), :], offset, 1)
-        index_ref[pl.ds(tile, 1), :] = jnp.where(
-            lane >= offset, turned, index_ref[pl.ds(tile, 1), :]
-        )
+        row = jnp.where(lane >= offset, turned, row)
+        index_ref[pl.ds(tile, 1), :] = row
         index_ref[pl.ds(tile + 1, 1), :] = turned
-        return at + count_ref[0, o]
-
-    where_ref[slabs] = lax.fori_loop(0, slabs, place, jnp.int32(0))
+        after = at + count_ref[0, o]
+        crossed = lax.shift_right_logical(after, 8) != tile
+        return after, jnp.where(crossed, turned, row)
+
+    start = (jnp.int32(0), jnp.zeros((1, SLOTS), jnp.int32))
+    where_ref[slabs] = lax.fori_loop(0, slabs, place, start, unroll=8)[0]
+
+    sh = Shifts(4, True)
+    (keep_2, gain_2), (keep_3, gain_3) = step_factors(FINE_STEPS)
+
+    @pl.loop(1, CX - 1, unroll=2)
+    def _(p):
+        d = diagonal(sh, *[tiles(coef_ref[p + o]) for o in (-1, 0, 1)])
+        scale = (1.0 / MIDPOINT) / d
+        diag_ref[p] = plane(d)
+        for c in range(3):
+            first_ref[c, p] = plane(tiles(force_ref[0, c, p]) * scale)
+
+    def advance(src, p):
+        planes = [[tiles(src[c, p + o]) for c in range(3)] for o in (-1, 0, 1)]
+        factors = [tiles(coef_ref[p + o]) for o in (-1, 0, 1)]
+        d = tiles(diag_ref[p])
+        image = operate(sh, *planes, *factors, d)
+        return planes[1], [(tiles(force_ref[0, c, p]) - image[c]) / d for c in range(3)]
+
+    @pl.loop(2, CX - 2, unroll=2)
+    def _(p):
+        value, left = advance(first_ref, p)
+        for c in range(3):
+            second_ref[c, p] = plane((1.0 + keep_2) * value[c] + gain_2 * left[c])
+
+    @pl.loop(3, CX - 3, unroll=2)
+    def _(p):
+        value, left = advance(second_ref, p)
+        for c in range(3):
+            step = keep_3 * (value[c] - tiles(first_ref[c, p])) + gain_3 * left[c]
+            third_ref[c, p - 3] = plane(value[c] + step)
 
 
 def unpack_coarse(plane_ref):
@@ -233,6 +281,10 @@
     below_ref,
     above_ref,
     index_ref,
+    inner_diag_ref,
+    inner_first_ref,
+    inner_second_ref,
+    inner_third_ref,
     smooth_ref,
     coef_out_ref,
     diag_out_ref,
@@ -268,8 +320,21 @@
         for p in range(CX):
             force[c, 3 + p] = force_ref[0, c, p]
 
-    @pl.loop(1, FINE_PLANES - 1)
-    def _(p):
+    for p in range(1, CX - 1):
+        diag[p + 3] = inner_diag_ref[p]
+        for c in range(3):
+            first[c, p + 3] = inner_first_ref[c, p]
+    for p in (1, 2, CX - 3, CX - 2):
+        inverse[p + 3] = 1.0 / inner_diag_ref[p]
+    for c in range(3):
+        for p in range(2, CX - 2):
+            second[c, p + 3] = inner_second_ref[c, p]
+        for p in range(3, CX - 3):
+            smooth_ref[c, p + 1] = inner_third_ref[c, p - 3]
+
+    @pl.loop(0, 6, unroll=2)
+    def _(i):
+        p = 1 + i + jnp.where(i >= 3, CX - 2, 0)
         d = plane(diagonal(sh, *[tiles(coef[p + o]) for o in (-1, 0, 1)]))
         place = slab * CX + p - 3
         valid = jnp.logical_and(place >= 0, place < slabs * CX)
@@ -287,15 +352,17 @@
 
     (keep_2, gain_2), (keep_3, gain_3) = step_factors(FINE_STEPS)
 
-    @pl.loop(1, FINE_PLANES - 1, unroll=UNROLL)
-    def _(p):
+    @pl.loop(0, 8, unroll=UNROLL)
+    def _(i):
+        p = 1 + i + jnp.where(i >= 4, CX - 4, 0)
         value, left = remainder(first, p, 0)
         inv = tiles(inverse[p])
         for c in range(3):
             second[c, p] = plane((1.0 + keep_2) * value[c] + gain_2 * (left[c] * inv))
 
-    @pl.loop(2, FINE_PLANES - 2, unroll=UNROLL)
-    def _(p):
+    @pl.loop(0, 8, unroll=UNROLL)
+    def _(i):
+        p = 2 + i + jnp.where(i >= 4, CX - 6, 0)
         value, left = remainder(second, p, 0)
         inv = tiles(inverse[p])
         for c in range(3):
@@ -330,27 +397,50 @@
     one = jnp.ones((), BF16)
     zero = jnp.zeros((), BF16)
 
+    half_line = lax.broadcasted_iota(jnp.int32, (8, HZ), 0)
+
     def pick(t):
         index = index_ref[pl.ds(t, 1), :]
         group = lax.shift_right_logical(index, 11)
         inner = line == (lax.shift_right_logical(index, 8) & 7)
         hot = jnp.where(column == (index & (NZ - 1)).astype(F32).astype(BF16), one, zero)
-        both = jnp.dot(table[:, 0:NZ], hot, preferred_element_type=F32) + jnp.dot(
-            table[:, NZ : 2 * NZ], hot, preferred_element_type=F32
+        amount = 2 * plane_rows
+        both = jnp.dot(table[0:amount, 0:NZ], hot, preferred_element_type=F32) + jnp.dot(
+            table[0:amount, NZ : 2 * NZ], hot, preferred_element_type=F32
         )
-        for c in range(3):
+        for c in range(2):
             held = both[c * plane_rows : c * plane_rows + 8, :]
             for g in range(1, groups):
                 at = c * plane_rows + 8 * g
                 held = jnp.where(group == g, both[at : at + 8, :], held)
             found[t, c : c + 1, :] = jnp.sum(jnp.where(inner, held, 0.0), axis=0, keepdims=True)
-
-    @pl.loop(0, lax.shift_right_logical(where_ref[slabs] + 2 * SLOTS - 1, 9))
-    def _(pair):
-        pick(2 * pair)
-        pick(2 * pair + 1)
-
-    @pl.loop(0, slabs, unroll=4)
+        for c in range(2, 3):
+            halves = []
+            for h in range(2):
+                part = index[:, h * HZ : (h + 1) * HZ]
+                lane_of = jnp.broadcast_to(part & (HZ - 1), (8, HZ))
+                right = (part & HZ) != 0
+                group_h = group[:, h * HZ : (h + 1) * HZ]
+                held = None
+                for g in range(groups):
+                    at = c * plane_rows + 8 * g
+                    rows8 = residual[at : at + 8, :]
+                    got = jnp.where(
+                        right,
+                        jnp.take_along_axis(rows8[:, HZ:], lane_of, axis=1, mode="promise_in_bounds"),
+                        jnp.take_along_axis(rows8[:, :HZ], lane_of, axis=1, mode="promise_in_bounds"),
+                    )
+                    held = got if held is None else jnp.where(group_h == g, got, held)
+                halves.append(held)
+            held = jnp.concatenate(halves, axis=1)
+            found[t, c : c + 1, :] = jnp.sum(jnp.where(inner, held, 0.0), axis=0, keepdims=True)
+
+    @pl.loop(0, lax.shift_right_logical(where_ref[slabs] + 4 * SLOTS - 1, 10))
+    def _(quad):
+        for u in range(4):
+            pick(4 * quad + u)
+
+    @pl.loop(0, slabs, unroll=16)
     def _(o):
         at = where_ref[o]
         tile = lax.shift_right_logical(at, 8)
@@ -559,19 +649,23 @@
     above = lax.ppermute(pack_low, "space", backward)
 
     rows_kept = slabs + 8
-    line, column, where, index = pl.pallas_call(
+    line, column, where, index, *inner = pl.pallas_call(
         plan_kernel,
         out_shape=(
             shaped(slabs, SLOTS),
             shaped(slabs, SLOTS),
             jax.ShapeDtypeStruct((slabs + 1,), jnp.int32),
             jax.ShapeDtypeStruct((rows_kept, SLOTS), jnp.int32),
+            shaped(CX, NY, NZ),
+            shaped(3, CX, NY, NZ),
+            shaped(3, CX, NY, NZ),
+            shaped(3, CX - 6, NY, NZ),
         ),
-        in_specs=[SMEM, VMEM, VMEM],
-        out_specs=(VMEM, VMEM, SMEM, VMEM),
+        in_specs=[SMEM, VMEM, VMEM, VMEM, VMEM],
+        out_specs=(VMEM, VMEM, SMEM, VMEM, VMEM, VMEM, VMEM, VMEM),
         compiler_params=PARAMS,
         name="plan",
-    )(face_count, face_src, face_dst)
+    )(face_count, face_src, face_dst, load_force, own_coef)
 
     smooth, coef, diag, local, picked = pl.pallas_call(
         fine_kernel,
@@ -582,7 +676,7 @@
             shaped(3 * HX * HY, HZ),
             shaped(slabs, 3 * SLOTS),
         ),
-        in_specs=[SMEM, SMEM, VMEM, VMEM, VMEM, VMEM, VMEM],
+        in_specs=[SMEM, SMEM] + [VMEM] * 9,
         out_specs=(VMEM, VMEM, VMEM, VMEM, VMEM),
         scratch_shapes=[
             pltpu.VMEM((COEF_PLANES, NY, NZ), F32),
@@ -598,7 +692,7 @@
         ],
         compiler_params=PARAMS,
         name="fine",
-    )(face_count, where, load_force, own_coef, below, above, index)
+    )(face_count, where, load_force, own_coef, below, above, index, *inner)
 
     arrived = lax.all_to_all(picked, "space", split_axis=0, concat_axis=0, tiled=True)
 

time: 75.7 us -> 71.3 us (0.942)
  Pallas kernels: 23.4 us -> 15.2 us
  blocking collectives: 17 us -> 19.2 us
  waiting for transfers between devices: 2.99 us -> 4.84 us
    pallas_call x1, Pallas kernels: 11.3 us -> 6.69 us  [body(): pl.pallas_call(fine_kernel, out_shape=(shaped(3, CX + 2, NY, NZ), shaped(...]
    pallas_call x1, Pallas kernels: 6.06 us -> 2.51 us  [body(): pl.pallas_call(plan_kernel, out_shape=(shaped(slabs, SLOTS), shaped(slabs...]
    all_to_all x1, blocking collectives: 17 us -> 19.2 us  [body(): lax.all_to_all(picked, 'space', split_axis=0, concat_axis=0, tiled=True)]
    ppermute x1, waiting for transfers between devices: 0.01 us -> 1.81 us  [body(): below = lax.ppermute(pack_high, 'space', forward)]
  transfers between devices with their start and end apart: 6 -> 6, of which waited for: 3 -> 4; matrix products, arithmetic and copies ran while one was open for 1% -> 1% of each run, Pallas kernels for 8% -> 4%
where the time goes in v4:
time: 71.3 us; the launch traced here: 70.9 us
  starting transfers between devices  28 us (39%)
  blocking collectives  19.2 us (27%)
  Pallas kernels  15.2 us (21%)
  waiting for transfers between devices  4.84 us (7%)
  between operations  2.07 us (3%)
  local copies, waits for them, and re-layouts  0.84 us (1%)
  other arithmetic  0.75 us (1%)
    all_to_all x1, blocking collectives, body(): lax.all_to_all(picked, 'space', split_axis=0, concat_axis=0, tiled=True)  19.2 us
    ppermute x1, starting transfers between devices, body(): above = lax.ppermute(pack_low, 'space', backward)  7.45 us
    ppermute x1, starting transfers between devices, body(): source_above = lax.ppermute(send_low, 'space', backward)  7.05 us
    pallas_call x1, Pallas kernels, body(): pl.pallas_call(fine_kernel, out_shape=(shaped(3, CX + 2, NY, NZ), shaped(...  6.69 us
    ppermute x1, starting transfers between devices, body(): got = lax.ppermute(far, 'load', [(i, i ^ 2) for i in range(4)])  5.57 us
    ppermute x1, starting transfers between devices, body(): last = lax.ppermute(near + got[1], 'load', [(i, i ^ 1) for i in range(4)])  4.89 us
    ppermute x1, starting transfers between devices, body(): below = lax.ppermute(pack_high, 'space', forward)  2.54 us
    pallas_call x1, Pallas kernels, body(): pl.pallas_call(coarse_kernel, grid=(1,), out_shape=(shaped(1, 3, CX, NY,...  2.52 us
  transfers between devices with their start and end apart: 6, of which 4 were waited for; matrix products, arithmetic and copies ran while one was open for 1% of the time, Pallas kernels for 4%

profile of v4, /device:TPU:1, one launch (start us, length us, event | category | flops | bytes accessed | tf_op | source)
XLA Modules:
  0.0 70.9 jit_solution(9270649439597061283)
XLA Ops:
  0.6 0.0 copy-start
  0.7 1.4 %pack.1 = (f32[13,16,256]{2,1,0:T(8,128)S(1)}, f32[13,16,256]{2,1,0:T(8,128)S(1)}, f32[4,8,128]{2,1,0:T(8,128)S(1)}, f32[8,16,256]{2,1,0:T(8,128)S(1)}) custom-call(s32[1,2]{1,0:T(1,128)} %material_hbm.1, f32[1,3,8,16,256]{4,3,2,1,0:T(8,128)} %force_ref.3, f32[8,16,256]{2,1,0:T(8,128)} %stiff_hbm.1), custom_call_target="tpu_custom_call" | custom-call | tf_op jit(solution)/shard_map/pack/pallas_call | solution.py:627
  2.0 2.5 %collective-permute-start = (f32[13,16,256]{2,1,0:T(8,128)S(1)}, f32[13,16,256]{2,1,0:T(8,128)S(1)}, u32[]{:S(2)}, u32[]{:S(2)}) collective-permute-start(f32[13,16,256]{2,1,0:T(8,128)S(1)} %get-tuple-element.28), channel_id=1, source_target_pairs={{0,4},{4,8},{8,12},{12,16},{16,20},{20,24},{24,28},{28,32},{32,36}... | collective-permute-start | bytes 638984 | tf_op jit(solution)/shard_map/ppermute | solution.py:648
  4.6 7.5 %collective-permute-start.1 = (f32[13,16,256]{2,1,0:T(8,128)S(1)}, f32[13,16,256]{2,1,0:T(8,128)S(1)}, u32[]{:S(2)}, u32[]{:S(2)}) collective-permute-start(f32[13,16,256]{2,1,0:T(8,128)S(1)} %get-tuple-element.29), channel_id=1, source_target_pairs={{4,0},{8,4},{12,8},{16,12},{20,16},{24,20},{28,24},{32,28},{36,32}... | collective-permute-start | bytes 638984 | tf_op jit(solution)/shard_map/ppermute | solution.py:649
  12.0 0.0 copy-done.2
  12.0 2.5 %plan.1 = (f32[64,256]{1,0:T(8,128)S(1)}, f32[64,256]{1,0:T(8,128)S(1)}, s32[65]{0:T(128)S(1)}, s32[72,256]{1,0:T(8,128)S(1)}, f32[8,16,256]{2,1,0:T(8,128)S(1)}...) custom-call(s32[1,64]{1,0:T(1,128)S(1)} %copy-done.3, ...), custom_call_target="tpu_custom_call" | custom-call | tf_op jit(solution)/shard_map/plan/pallas_call | solution.py:652
  14.6 1.8 %collective-permute-done.below_ref.coef_below_ref = f32[13,16,256]{2,1,0:T(8,128)S(1)} collective-permute-done((f32[13,16,256]{2,1,0:T(8,128)S(1)}, f32[13,16,256]{2,1,0:T(8,128)S(1)}, u32[]{:S(2)}, u32[]{:S(2)}) %collective-permute-start) | collective-permute-done | bytes 213024 | tf_op jit(solution)/shard_map/ppermute | solution.py:648
  16.4 0.0 collective-permute-done.1.above_ref.coef_above_ref
  16.4 6.7 %fine.1 = (f32[3,10,16,256]{3,2,1,0:T(8,128)S(1)}, f32[10,16,256]{2,1,0:T(8,128)S(1)}, f32[8,16,256]{2,1,0:T(8,128)S(1)}, f32[96,128]{1,0:T(8,128)S(1)}, f32[64,768]{1,0:T(8,128)S(1)}) custom-call(s32[1,64]{1,0:T(1,128)S(1)} %copy-done.3, s32[65]{0:T(128)S(1)} %get-tuple-element.27.where_ref, f32[1,3,8,16,256]{4,3,2,1,0:T(8,128)S(1)} %copy-done, ...), custom_call_target="tpu_custom_call" | custom-call | tf_op jit(solution)/shard_map/fine/pallas_call | solution.py:670
  23.1 0.2 copy.9
  23.3 19.2 %all_to_all.11 = f32[64,1,768]{2,1,0:T(1,128)S(1)} all-to-all(f32[64,1,768]{2,1,0:T(1,128)S(1)} %copy.9), channel_id=1, replica_groups=mesh['space'=64,'load'=4] {'space'}, dimensions={0} | all-to-all | bytes 393216 | tf_op jit(solution)/shard_map/all_to_all | solution.py:697
  42.5 2.1 %reflux.1 = (f32[3,4,8,128]{3,2,1,0:T(8,128)S(1)}, f32[3,4,8,128]{3,2,1,0:T(8,128)S(1)}, f32[3,4,8,128]{3,2,1,0:T(8,128)S(1)}) custom-call(f32[64,768]{1,0:T(8,128)S(1)} %bitcast.18, f32[64,256]{1,0:T(8,128)S(1)} %get-tuple-element.36.line_ref, f32[64,256]{1,0:T(8,128)S(1)} %get-tuple-element.37.column_ref, f32[96,128]{1,0:T(8,128)S(1)} %get-tuple-element.38.local_ref, ...), custom_call_target="tpu_custom_call" | custom-call | tf_op jit(solution)/shard_map/reflux/pallas_call | solution.py:705
  44.6 0.5 collective-permute-start.2
  45.1 7.1 %collective-permute-start.3 = (f32[3,4,8,128]{3,2,1,0:T(8,128)S(1)}, f32[3,4,8,128]{3,2,1,0:T(8,128)S(1)}, u32[]{:S(2)}, u32[]{:S(2)}) collective-permute-start(f32[3,4,8,128]{3,2,1,0:T(8,128)S(1)} %get-tuple-element.42), channel_id=1, source_target_pairs={{4,0},{8,4},{12,8},{16,12},{20,16},{24,20},{28,24},{32,28},{36,32}... | collective-permute-start | bytes 147464 | tf_op jit(solution)/shard_map/ppermute | solution.py:726
  52.2 1.5 %collective-permute-done.2.below_ref = f32[3,4,8,128]{3,2,1,0:T(8,128)S(1)} collective-permute-done((f32[3,4,8,128]{3,2,1,0:T(8,128)S(1)}, f32[3,4,8,128]{3,2,1,0:T(8,128)S(1)}, u32[]{:S(2)}, u32[]{:S(2)}) %collective-permute-start.2) | collective-permute-done | bytes 49184 | tf_op jit(solution)/shard_map/ppermute | solution.py:725
  53.6 0.0 collective-permute-done.3.above_ref
  53.6 2.5 %coarse.1 = (f32[1,3,8,16,256]{4,3,2,1,0:T(8,128)}, f32[8,4,256]{2,1,0:T(4,128)S(1)}, f32[8,4,256]{2,1,0:T(4,128)S(1)}, f32[2,8,4,256]{3,2,1,0:T(4,128)S(1)}) custom-call(f32[3,4,8,128]{3,2,1,0:T(8,128)S(1)} %get-tuple-element.40.source_ref, f32[3,4,8,128]{3,2,1,0:T(8,128)S(1)} %collective-permute-done.2.below_ref, ...), custom_call_target="tpu_custom_call" | custom-call | tf_op jit(solution)/shard_map/coarse/pallas_call | solution.py:729
  56.2 5.6 %collective-permute-start.4 = (f32[2,8,4,256]{3,2,1,0:T(4,128)S(1)}, f32[2,8,4,256]{3,2,1,0:T(4,128)S(1)}, u32[]{:S(2)}, u32[]{:S(2)}) collective-permute-start(f32[2,8,4,256]{3,2,1,0:T(4,128)S(1)} %get-tuple-element.48), channel_id=1, source_target_pairs={{0,2},{1,3},{2,0},{3,1},{4,6},{5,7},{6,4},{7,5},{8,10},{9,11},{10,... | collective-permute-start | bytes 196616 | tf_op jit(solution)/shard_map/ppermute | solution.py:753
  61.7 0.6 fusion.4
  63.7 0.7 %collective-permute-done.4 = f32[2,8,4,256]{3,2,1,0:T(4,128)S(1)} collective-permute-done((f32[2,8,4,256]{3,2,1,0:T(4,128)S(1)}, f32[2,8,4,256]{3,2,1,0:T(4,128)S(1)}, u32[]{:S(2)}, u32[]{:S(2)}) %collective-permute-start.4) | collective-permute-done | bytes 65568 | tf_op jit(solution)/shard_map/ppermute | solution.py:753
  64.4 4.9 %collective-permute-start.5 = (f32[8,4,256]{2,1,0:T(4,128)S(1)}, f32[8,4,256]{2,1,0:T(4,128)S(1)}, u32[]{:S(2)}, u32[]{:S(2)}) collective-permute-start(f32[8,4,256]{2,1,0:T(4,128)S(1)} %fusion), channel_id=1, source_target_pairs={{0,1},{1,0},{2,3},{3,2},{4,5},{5,4},{6,7},{7,6},{8,9},{9,8},{10,11... | collective-permute-start | bytes 98312 | tf_op jit(solution)/shard_map/ppermute | solution.py:754
  69.3 0.0 copy-done.5
  69.3 0.8 %collective-permute-done.5 = f32[8,4,256]{2,1,0:T(4,128)S(1)} collective-permute-done((f32[8,4,256]{2,1,0:T(4,128)S(1)}, f32[8,4,256]{2,1,0:T(4,128)S(1)}, u32[]{:S(2)}, u32[]{:S(2)}) %collective-permute-start.5) | collective-permute-done | bytes 32800 | tf_op jit(solution)/shard_map/ppermute | solution.py:754
  70.2 0.7 %broadcast_multiply_fusion = f32[3,8,4,256]{3,2,1,0:T(4,128)} fusion(f32[8,4,256]{2,1,0:T(4,128)S(1)} %fusion.2, f32[3]{0:T(128)S(1)} %fusion.3), kind=kLoop, calls=%fused_computation.1 | loop fusion | flops 24576 | bytes 131084 | tf_op jit(solution)/shard_map/mul | solution.py:761
  (17 shorter events, 0.1 us)
Async XLA Ops:
  0.6 11.4 %copy-start = (f32[1,3,8,16,256]{4,3,2,1,0:T(8,128)S(1)}, f32[1,3,8,16,256]{4,3,2,1,0:T(8,128)}, u32[]{:S(2)}) copy-start(f32[1,3,8,16,256]{4,3,2,1,0:T(8,128)} %force_ref.3) | copy-start | bytes 1179652
  0.6 11.4 %copy-start.1 = (s32[1,64,256]{2,1,0:T(8,128)S(1)}, s32[1,64,256]{2,1,0:T(8,128)}, u32[]{:S(2)}) copy-start(s32[1,64,256]{2,1,0:T(8,128)} %source_ref.1) | copy-start | bytes 196612
  0.7 11.4 %copy-start.2 = (s32[1,64,256]{2,1,0:T(8,128)S(1)}, s32[1,64,256]{2,1,0:T(8,128)}, u32[]{:S(2)}) copy-start(s32[1,64,256]{2,1,0:T(8,128)} %target_ref.1) | copy-start | bytes 196612
  2.0 14.3 %collective-permute-start = (f32[13,16,256]{2,1,0:T(8,128)S(1)}, f32[13,16,256]{2,1,0:T(8,128)S(1)}, u32[]{:S(2)}, u32[]{:S(2)}) collective-permute-start(f32[13,16,256]{2,1,0:T(8,128)S(1)} %get-tuple-element.28), channel_id=1, source_target_pairs={{0,4},{4,8},{8,12},{12,16},{16,20},{20,24},{24,28},{28,32},{32,36}... | collective-permute-start | bytes 638984 | tf_op jit(solution)/shard_map/ppermute | solution.py:648
  4.6 7.5 %copy-start.3 = (s32[1,64]{1,0:T(1,128)S(1)}, s32[1,64]{1,0:T(1,128)}, u32[]{:S(2)}) copy-start(s32[1,64]{1,0:T(1,128)} %count_ref.3) | copy-start | bytes 772
  4.6 11.8 %collective-permute-start.1 = (f32[13,16,256]{2,1,0:T(8,128)S(1)}, f32[13,16,256]{2,1,0:T(8,128)S(1)}, u32[]{:S(2)}, u32[]{:S(2)}) collective-permute-start(f32[13,16,256]{2,1,0:T(8,128)S(1)} %get-tuple-element.29), channel_id=1, source_target_pairs={{4,0},{8,4},{12,8},{16,12},{20,16},{24,20},{28,24},{32,28},{36,32}... | collective-permute-start | bytes 638984 | tf_op jit(solution)/shard_map/ppermute | solution.py:649
  44.6 9.0 %collective-permute-start.2 = (f32[3,4,8,128]{3,2,1,0:T(8,128)S(1)}, f32[3,4,8,128]{3,2,1,0:T(8,128)S(1)}, u32[]{:S(2)}, u32[]{:S(2)}) collective-permute-start(f32[3,4,8,128]{3,2,1,0:T(8,128)S(1)} %get-tuple-element.41), channel_id=1, source_target_pairs={{0,4},{4,8},{8,12},{12,16},{16,20},{20,24},{24,28},{28,32},{32,36}... | collective-permute-start | bytes 147464 | tf_op jit(solution)/shard_map/ppermute | solution.py:725
  45.1 8.5 %collective-permute-start.3 = (f32[3,4,8,128]{3,2,1,0:T(8,128)S(1)}, f32[3,4,8,128]{3,2,1,0:T(8,128)S(1)}, u32[]{:S(2)}, u32[]{:S(2)}) collective-permute-start(f32[3,4,8,128]{3,2,1,0:T(8,128)S(1)} %get-tuple-element.42), channel_id=1, source_target_pairs={{4,0},{8,4},{12,8},{16,12},{20,16},{24,20},{28,24},{32,28},{36,32}... | collective-permute-start | bytes 147464 | tf_op jit(solution)/shard_map/ppermute | solution.py:726
  56.2 5.6 %copy-start.4 = (s32[1,2]{1,0:T(1,128)S(1)}, s32[1,2]{1,0:T(1,128)}, u32[]{:S(2)}) copy-start(s32[1,2]{1,0:T(1,128)} %material_hbm.1) | copy-start | bytes 28
  56.2 8.2 %collective-permute-start.4 = (f32[2,8,4,256]{3,2,1,0:T(4,128)S(1)}, f32[2,8,4,256]{3,2,1,0:T(4,128)S(1)}, u32[]{:S(2)}, u32[]{:S(2)}) collective-permute-start(f32[2,8,4,256]{3,2,1,0:T(4,128)S(1)} %get-tuple-element.48), channel_id=1, source_target_pairs={{0,2},{1,3},{2,0},{3,1},{4,6},{5,7},{6,4},{7,5},{8,10},{9,11},{10,... | collective-permute-start | bytes 196616 | tf_op jit(solution)/shard_map/ppermute | solution.py:753
  64.4 4.9 %copy-start.5 = (f32[1,3]{1,0:T(1,128)S(1)}, f32[1,3]{1,0:T(1,128)}, u32[]{:S(2)}) copy-start(f32[1,3]{1,0:T(1,128)} %constant.19) | copy-start | bytes 40
  64.4 4.9 %copy-start.6 = (f32[1,3]{1,0:T(1,128)S(1)}, f32[1,3]{1,0:T(1,128)}, u32[]{:S(2)}) copy-start(f32[1,3]{1,0:T(1,128)} %constant.20) | copy-start | bytes 40
  64.4 4.9 %copy-start.7 = (f32[1,3]{1,0:T(1,128)S(1)}, f32[1,3]{1,0:T(1,128)}, u32[]{:S(2)}) copy-start(f32[1,3]{1,0:T(1,128)} %constant.21) | copy-start | bytes 40
  64.4 5.8 %collective-permute-start.5 = (f32[8,4,256]{2,1,0:T(4,128)S(1)}, f32[8,4,256]{2,1,0:T(4,128)S(1)}, u32[]{:S(2)}, u32[]{:S(2)}) collective-permute-start(f32[8,4,256]{2,1,0:T(4,128)S(1)} %fusion), channel_id=1, source_target_pairs={{0,1},{1,0},{2,3},{3,2},{4,5},{5,4},{6,7},{7,6},{8,9},{9,8},{10,11... | collective-permute-start | bytes 98312 | tf_op jit(solution)/shard_map/ppermute | solution.py:754

commit v5 on v4

--- a/solution.py
+++ b/solution.py
@@ -435,10 +435,10 @@
             held = jnp.concatenate(halves, axis=1)
             found[t, c : c + 1, :] = jnp.sum(jnp.where(inner, held, 0.0), axis=0, keepdims=True)
 
-    @pl.loop(0, lax.shift_right_logical(where_ref[slabs] + 4 * SLOTS - 1, 10))
-    def _(quad):
-        for u in range(4):
-            pick(4 * quad + u)
+    @pl.loop(0, lax.div(where_ref[slabs] + (6 * SLOTS - 1), jnp.int32(6 * SLOTS)))
+    def _(trip):
+        for u in range(6):
+            pick(6 * trip + u)
 
     @pl.loop(0, slabs, unroll=16)
     def _(o):
@@ -467,8 +467,8 @@
     coef_ref,
     coef_above_ref,
     source_ref,
-    low_ref,
-    high_ref,
+    first_ref,
+    second_ref,
     total,
 ):
     slab = lax.axis_index("space")
@@ -504,21 +504,25 @@
     count = 3 * lines
     source = (total[0:count, :] + total[count : 2 * count, :] + local_ref[...]).reshape(3, HX, HY, HZ)
     source_ref[...] = source
-    low_ref[...] = source
-    high_ref[...] = source
+    first_ref[...] = source
+    second_ref[...] = source
     coef = coarse_extent(coef_below_ref, coef_ref, coef_above_ref, slab, slabs)
     sh = Shifts(1, False)
-    for ref, p in ((high_ref, 0), (low_ref, HX - 1)):
+    even = (slab & 1) == 0
+    for p, upward in ((0, True), (HX - 1, False)):
         d = diagonal(sh, *[coef[HX + p + o][None] for o in (-1, 0, 1)])
         scale = (1.0 / MIDPOINT) / d[0]
-        for c in range(3):
-            ref[c, p] = source[c, p] * scale
+        to_first = even if upward else jnp.logical_not(even)
+        for c in range(3):
+            plain, scaled = source[c, p], source[c, p] * scale
+            first_ref[c, p] = jnp.where(to_first, scaled, plain)
+            second_ref[c, p] = jnp.where(to_first, plain, scaled)
 
 
 def coarse_kernel(
     source_ref,
-    below_ref,
-    above_ref,
+    first_ref,
+    second_ref,
     coef_below_ref,
     coarse_coef_ref,
     coef_above_ref,
@@ -537,9 +541,12 @@
     slabs = lax.axis_size("space")
     mine = lax.axis_index("load")
     coef = jnp.stack(coarse_extent(coef_below_ref, coarse_coef_ref, coef_above_ref, slab, slabs))
-    source = [
-        jnp.concatenate([below_ref[c], source_ref[c], above_ref[c]], axis=0) for c in range(3)
-    ]
+    even = (slab & 1) == 0
+    source = []
+    for c in range(3):
+        below = jnp.where(even, second_ref[c], first_ref[c])
+        above = jnp.where(even, first_ref[c], second_ref[c])
+        source.append(jnp.concatenate([below, source_ref[c], above], axis=0))
     count = 3 * HX - 2
     place = lax.broadcasted_iota(jnp.int32, (count, HY, HZ), 0) + (slab * HX - HX + 1)
     valid = jnp.logical_and(place >= 0, place < slabs * HX)
@@ -624,6 +631,8 @@
     slabs = lax.axis_size("space")
     forward = [(i, (i + 1) % slabs) for i in range(slabs)]
     backward = [(target, origin) for origin, target in forward]
+    first_pairs = [(i, i ^ 1) for i in range(slabs)]
+    second_pairs = [(i, min(max(((i + 1) ^ 1) - 1, 0), slabs - 1)) for i in range(slabs)]
     pack_low, pack_high, coarse_coef, own_coef = pl.pallas_call(
         pack_kernel,
         out_shape=(
@@ -702,7 +711,7 @@
         return pl.BlockSpec(shape, lambda i: (0,) * len(shape))
 
     grid_shape = (3, HX, HY, HZ)
-    source, send_low, send_high = pl.pallas_call(
+    source, send_first, send_second = pl.pallas_call(
         gather_kernel,
         grid=(1,),
         out_shape=(shaped(*grid_shape), shaped(*grid_shape), shaped(*grid_shape)),
@@ -722,8 +731,8 @@
         compiler_params=PARAMS,
         name="reflux",
     )(arrived, line, column, local, below, coarse_coef, above)
-    source_below = lax.ppermute(send_high, "space", forward)
-    source_above = lax.ppermute(send_low, "space", backward)
+    met_second = lax.ppermute(send_second, "space", second_pairs)
+    met_first = lax.ppermute(send_first, "space", first_pairs)
 
     part = (CX, NY // 4, NZ)
     moved, kept, near, far = pl.pallas_call(
@@ -749,7 +758,7 @@
         ],
         compiler_params=PARAMS,
         name="coarse",
-    )(source, source_below, source_above, below, coarse_coef, above, smooth, coef, diag)
+    )(source, met_first, met_second, below, coarse_coef, above, smooth, coef, diag)
     got = lax.ppermute(far, "load", [(i, i ^ 2) for i in range(4)])
     last = lax.ppermute(near + got[1], "load", [(i, i ^ 1) for i in range(4)])
     mine = lax.axis_index("load")

time: 71.3 us -> 70.5 us (0.989)
  the two profiles are of different devices: /device:TPU:1 before, /device:TPU:3 now
where the time goes in v5:
time: 70.5 us; the launch traced here: 70.3 us
  starting transfers between devices  22.9 us (32%)
  blocking collectives  19.2 us (27%)
  Pallas kernels  15.3 us (22%)
  waiting for transfers between devices  9.15 us (13%)
  between operations  2.12 us (3%)
  local copies, waits for them, and re-layouts  0.85 us (1%)
  other arithmetic  0.75 us (1%)
    all_to_all x1, blocking collectives, body(): lax.all_to_all(picked, 'space', split_axis=0, concat_axis=0, tiled=True)  19.2 us
    pallas_call x1, Pallas kernels, body(): pl.pallas_call(fine_kernel, out_shape=(shaped(3, CX + 2, NY, NZ), shaped(...  6.82 us
    ppermute x1, starting transfers between devices, body(): last = lax.ppermute(near + got[1], 'load', [(i, i ^ 1) for i in range(4)])  5.69 us
    ppermute x1, starting transfers between devices, body(): got = lax.ppermute(far, 'load', [(i, i ^ 2) for i in range(4)])  5.45 us
    ppermute x1, waiting for transfers between devices, body(): met_second = lax.ppermute(send_second, 'space', second_pairs)  5.26 us
    ppermute x1, starting transfers between devices, body(): above = lax.ppermute(pack_low, 'space', backward)  5.23 us
    ppermute x1, starting transfers between devices, body(): met_second = lax.ppermute(send_second, 'space', second_pairs)  4.35 us
    pallas_call x1, Pallas kernels, body(): pl.pallas_call(coarse_kernel, grid=(1,), out_shape=(shaped(1, 3, CX, NY,...  2.52 us
  transfers between devices with their start and end apart: 6, of which 4 were waited for; matrix products, arithmetic and copies ran while one was open for 1% of the time, Pallas kernels for 4%

profile of v5, /device:TPU:3, one launch (start us, length us, event | category | flops | bytes accessed | tf_op | source)
XLA Modules:
  0.0 70.3 jit_solution(11112485600627571558)
XLA Ops:
  0.7 1.4 %pack.1 = (f32[13,16,256]{2,1,0:T(8,128)S(1)}, f32[13,16,256]{2,1,0:T(8,128)S(1)}, f32[4,8,128]{2,1,0:T(8,128)S(1)}, f32[8,16,256]{2,1,0:T(8,128)S(1)}) custom-call(s32[1,2]{1,0:T(1,128)} %material_hbm.1, f32[1,3,8,16,256]{4,3,2,1,0:T(8,128)} %force_ref.3, f32[8,16,256]{2,1,0:T(8,128)} %stiff_hbm.1), custom_call_target="tpu_custom_call" | custom-call | tf_op jit(solution)/shard_map/pack/pallas_call | solution.py:636
  2.0 1.7 %collective-permute-start = (f32[13,16,256]{2,1,0:T(8,128)S(1)}, f32[13,16,256]{2,1,0:T(8,128)S(1)}, u32[]{:S(2)}, u32[]{:S(2)}) collective-permute-start(f32[13,16,256]{2,1,0:T(8,128)S(1)} %get-tuple-element.28), channel_id=1, source_target_pairs={{0,4},{4,8},{8,12},{12,16},{16,20},{20,24},{24,28},{28,32},{32,36}... | collective-permute-start | bytes 638984 | tf_op jit(solution)/shard_map/ppermute | solution.py:657
  3.7 5.2 %collective-permute-start.1 = (f32[13,16,256]{2,1,0:T(8,128)S(1)}, f32[13,16,256]{2,1,0:T(8,128)S(1)}, u32[]{:S(2)}, u32[]{:S(2)}) collective-permute-start(f32[13,16,256]{2,1,0:T(8,128)S(1)} %get-tuple-element.29), channel_id=1, source_target_pairs={{4,0},{8,4},{12,8},{16,12},{20,16},{24,20},{28,24},{32,28},{36,32}... | collective-permute-start | bytes 638984 | tf_op jit(solution)/shard_map/ppermute | solution.py:658
  9.0 2.5 %plan.1 = (f32[64,256]{1,0:T(8,128)S(1)}, f32[64,256]{1,0:T(8,128)S(1)}, s32[65]{0:T(128)S(1)}, s32[72,256]{1,0:T(8,128)S(1)}, f32[8,16,256]{2,1,0:T(8,128)S(1)}...) custom-call(s32[1,64]{1,0:T(1,128)S(1)} %copy-done.3, ...), custom_call_target="tpu_custom_call" | custom-call | tf_op jit(solution)/shard_map/plan/pallas_call | solution.py:661
  11.5 2.4 %collective-permute-done.below_ref.coef_below_ref = f32[13,16,256]{2,1,0:T(8,128)S(1)} collective-permute-done((f32[13,16,256]{2,1,0:T(8,128)S(1)}, f32[13,16,256]{2,1,0:T(8,128)S(1)}, u32[]{:S(2)}, u32[]{:S(2)}) %collective-permute-start) | collective-permute-done | bytes 213024 | tf_op jit(solution)/shard_map/ppermute | solution.py:657
  13.9 0.7 collective-permute-done.1.above_ref.coef_above_ref
  14.5 6.8 %fine.1 = (f32[3,10,16,256]{3,2,1,0:T(8,128)S(1)}, f32[10,16,256]{2,1,0:T(8,128)S(1)}, f32[8,16,256]{2,1,0:T(8,128)S(1)}, f32[96,128]{1,0:T(8,128)S(1)}, f32[64,768]{1,0:T(8,128)S(1)}) custom-call(s32[1,64]{1,0:T(1,128)S(1)} %copy-done.3, s32[65]{0:T(128)S(1)} %get-tuple-element.27.where_ref, f32[1,3,8,16,256]{4,3,2,1,0:T(8,128)S(1)} %copy-done, ...), custom_call_target="tpu_custom_call" | custom-call | tf_op jit(solution)/shard_map/fine/pallas_call | solution.py:679
  21.4 0.2 copy.9
  21.6 19.2 %all_to_all.11 = f32[64,1,768]{2,1,0:T(1,128)S(1)} all-to-all(f32[64,1,768]{2,1,0:T(1,128)S(1)} %copy.9), channel_id=1, replica_groups=mesh['space'=64,'load'=4] {'space'}, dimensions={0} | all-to-all | bytes 393216 | tf_op jit(solution)/shard_map/all_to_all | solution.py:706
  40.8 2.1 %reflux.1 = (f32[3,4,8,128]{3,2,1,0:T(8,128)S(1)}, f32[3,4,8,128]{3,2,1,0:T(8,128)S(1)}, f32[3,4,8,128]{3,2,1,0:T(8,128)S(1)}) custom-call(f32[64,768]{1,0:T(8,128)S(1)} %bitcast.18, f32[64,256]{1,0:T(8,128)S(1)} %get-tuple-element.36.line_ref, f32[64,256]{1,0:T(8,128)S(1)} %get-tuple-element.37.column_ref, f32[96,128]{1,0:T(8,128)S(1)} %get-tuple-element.38.local_ref, ...), custom_call_target="tpu_custom_call" | custom-call | tf_op jit(solution)/shard_map/reflux/pallas_call | solution.py:714
  42.9 0.5 collective-permute-start.2
  43.4 4.3 %collective-permute-start.3 = (f32[3,4,8,128]{3,2,1,0:T(8,128)S(1)}, f32[3,4,8,128]{3,2,1,0:T(8,128)S(1)}, u32[]{:S(2)}, u32[]{:S(2)}) collective-permute-start(f32[3,4,8,128]{3,2,1,0:T(8,128)S(1)} %get-tuple-element.42), channel_id=1, source_target_pairs={{0,0},{4,8},{8,4},{12,16},{16,12},{20,24},{24,20},{28,32},{32,28},... | collective-permute-start | bytes 147464 | tf_op jit(solution)/shard_map/ppermute | solution.py:734
  47.8 0.0 collective-permute-done.2.first_ref
  47.8 5.3 %collective-permute-done.3.second_ref = f32[3,4,8,128]{3,2,1,0:T(8,128)S(1)} collective-permute-done((f32[3,4,8,128]{3,2,1,0:T(8,128)S(1)}, f32[3,4,8,128]{3,2,1,0:T(8,128)S(1)}, u32[]{:S(2)}, u32[]{:S(2)}) %collective-permute-start.3) | collective-permute-done | bytes 49184 | tf_op jit(solution)/shard_map/ppermute | solution.py:734
  53.1 2.5 %coarse.1 = (f32[1,3,8,16,256]{4,3,2,1,0:T(8,128)}, f32[8,4,256]{2,1,0:T(4,128)S(1)}, f32[8,4,256]{2,1,0:T(4,128)S(1)}, f32[2,8,4,256]{3,2,1,0:T(4,128)S(1)}) custom-call(f32[3,4,8,128]{3,2,1,0:T(8,128)S(1)} %get-tuple-element.40.source_ref, f32[3,4,8,128]{3,2,1,0:T(8,128)S(1)} %collective-permute-done.2.first_ref, ...), custom_call_target="tpu_custom_call" | custom-call | tf_op jit(solution)/shard_map/coarse/pallas_call | solution.py:738
  55.6 5.4 %collective-permute-start.4 = (f32[2,8,4,256]{3,2,1,0:T(4,128)S(1)}, f32[2,8,4,256]{3,2,1,0:T(4,128)S(1)}, u32[]{:S(2)}, u32[]{:S(2)}) collective-permute-start(f32[2,8,4,256]{3,2,1,0:T(4,128)S(1)} %get-tuple-element.48), channel_id=1, source_target_pairs={{0,2},{1,3},{2,0},{3,1},{4,6},{5,7},{6,4},{7,5},{8,10},{9,11},{10,... | collective-permute-start | bytes 196616 | tf_op jit(solution)/shard_map/ppermute | solution.py:762
  61.0 0.6 fusion.4
  63.0 0.0 collective-permute-done.4
  63.0 0.0 copy-start.5
  63.0 0.0 copy-start.6
  63.0 0.0 copy-start.7
  63.0 5.7 %collective-permute-start.5 = (f32[8,4,256]{2,1,0:T(4,128)S(1)}, f32[8,4,256]{2,1,0:T(4,128)S(1)}, u32[]{:S(2)}, u32[]{:S(2)}) collective-permute-start(f32[8,4,256]{2,1,0:T(4,128)S(1)} %fusion), channel_id=1, source_target_pairs={{0,1},{1,0},{2,3},{3,2},{4,5},{5,4},{6,7},{7,6},{8,9},{9,8},{10,11... | collective-permute-start | bytes 98312 | tf_op jit(solution)/shard_map/ppermute | solution.py:763
  68.7 0.8 %collective-permute-done.5 = f32[8,4,256]{2,1,0:T(4,128)S(1)} collective-permute-done((f32[8,4,256]{2,1,0:T(4,128)S(1)}, f32[8,4,256]{2,1,0:T(4,128)S(1)}, u32[]{:S(2)}, u32[]{:S(2)}) %collective-permute-start.5) | collective-permute-done | bytes 32800 | tf_op jit(solution)/shard_map/ppermute | solution.py:763
  69.6 0.7 %broadcast_multiply_fusion = f32[3,8,4,256]{3,2,1,0:T(4,128)} fusion(f32[8,4,256]{2,1,0:T(4,128)S(1)} %fusion.2, f32[3]{0:T(128)S(1)} %fusion.3), kind=kLoop, calls=%fused_computation.1 | loop fusion | flops 24576 | bytes 131084 | tf_op jit(solution)/shard_map/mul | solution.py:770
  (17 shorter events, 0.1 us)
Async XLA Ops:
  0.6 8.3 %copy-start = (f32[1,3,8,16,256]{4,3,2,1,0:T(8,128)S(1)}, f32[1,3,8,16,256]{4,3,2,1,0:T(8,128)}, u32[]{:S(2)}) copy-start(f32[1,3,8,16,256]{4,3,2,1,0:T(8,128)} %force_ref.3) | copy-start | bytes 1179652
  0.6 8.3 %copy-start.1 = (s32[1,64,256]{2,1,0:T(8,128)S(1)}, s32[1,64,256]{2,1,0:T(8,128)}, u32[]{:S(2)}) copy-start(s32[1,64,256]{2,1,0:T(8,128)} %source_ref.1) | copy-start | bytes 196612
  0.7 8.3 %copy-start.2 = (s32[1,64,256]{2,1,0:T(8,128)S(1)}, s32[1,64,256]{2,1,0:T(8,128)}, u32[]{:S(2)}) copy-start(s32[1,64,256]{2,1,0:T(8,128)} %target_ref.1) | copy-start | bytes 196612
  2.0 11.9 %collective-permute-start = (f32[13,16,256]{2,1,0:T(8,128)S(1)}, f32[13,16,256]{2,1,0:T(8,128)S(1)}, u32[]{:S(2)}, u32[]{:S(2)}) collective-permute-start(f32[13,16,256]{2,1,0:T(8,128)S(1)} %get-tuple-element.28), channel_id=1, source_target_pairs={{0,4},{4,8},{8,12},{12,16},{16,20},{20,24},{24,28},{28,32},{32,36}... | collective-permute-start | bytes 638984 | tf_op jit(solution)/shard_map/ppermute | solution.py:657
  3.7 5.2 %copy-start.3 = (s32[1,64]{1,0:T(1,128)S(1)}, s32[1,64]{1,0:T(1,128)}, u32[]{:S(2)}) copy-start(s32[1,64]{1,0:T(1,128)} %count_ref.3) | copy-start | bytes 772
  3.7 10.8 %collective-permute-start.1 = (f32[13,16,256]{2,1,0:T(8,128)S(1)}, f32[13,16,256]{2,1,0:T(8,128)S(1)}, u32[]{:S(2)}, u32[]{:S(2)}) collective-permute-start(f32[13,16,256]{2,1,0:T(8,128)S(1)} %get-tuple-element.29), channel_id=1, source_target_pairs={{4,0},{8,4},{12,8},{16,12},{20,16},{24,20},{28,24},{32,28},{36,32}... | collective-permute-start | bytes 638984 | tf_op jit(solution)/shard_map/ppermute | solution.py:658
  42.9 4.9 %collective-permute-start.2 = (f32[3,4,8,128]{3,2,1,0:T(8,128)S(1)}, f32[3,4,8,128]{3,2,1,0:T(8,128)S(1)}, u32[]{:S(2)}, u32[]{:S(2)}) collective-permute-start(f32[3,4,8,128]{3,2,1,0:T(8,128)S(1)} %get-tuple-element.41), channel_id=1, source_target_pairs={{0,4},{4,0},{8,12},{12,8},{16,20},{20,16},{24,28},{28,24},{32,36},... | collective-permute-start | bytes 147464 | tf_op jit(solution)/shard_map/ppermute | solution.py:735
  43.4 9.6 %collective-permute-start.3 = (f32[3,4,8,128]{3,2,1,0:T(8,128)S(1)}, f32[3,4,8,128]{3,2,1,0:T(8,128)S(1)}, u32[]{:S(2)}, u32[]{:S(2)}) collective-permute-start(f32[3,4,8,128]{3,2,1,0:T(8,128)S(1)} %get-tuple-element.42), channel_id=1, source_target_pairs={{0,0},{4,8},{8,4},{12,16},{16,12},{20,24},{24,20},{28,32},{32,28},... | collective-permute-start | bytes 147464 | tf_op jit(solution)/shard_map/ppermute | solution.py:734
  55.6 5.5 %copy-start.4 = (s32[1,2]{1,0:T(1,128)S(1)}, s32[1,2]{1,0:T(1,128)}, u32[]{:S(2)}) copy-start(s32[1,2]{1,0:T(1,128)} %material_hbm.1) | copy-start | bytes 28
  55.6 7.4 %collective-permute-start.4 = (f32[2,8,4,256]{3,2,1,0:T(4,128)S(1)}, f32[2,8,4,256]{3,2,1,0:T(4,128)S(1)}, u32[]{:S(2)}, u32[]{:S(2)}) collective-permute-start(f32[2,8,4,256]{3,2,1,0:T(4,128)S(1)} %get-tuple-element.48), channel_id=1, source_target_pairs={{0,2},{1,3},{2,0},{3,1},{4,6},{5,7},{6,4},{7,5},{8,10},{9,11},{10,... | collective-permute-start | bytes 196616 | tf_op jit(solution)/shard_map/ppermute | solution.py:762
  63.0 5.8 %copy-start.5 = (f32[1,3]{1,0:T(1,128)S(1)}, f32[1,3]{1,0:T(1,128)}, u32[]{:S(2)}) copy-start(f32[1,3]{1,0:T(1,128)} %constant.19) | copy-start | bytes 40
  63.0 5.7 %copy-start.6 = (f32[1,3]{1,0:T(1,128)S(1)}, f32[1,3]{1,0:T(1,128)}, u32[]{:S(2)}) copy-start(f32[1,3]{1,0:T(1,128)} %constant.20) | copy-start | bytes 40
  63.0 5.7 %copy-start.7 = (f32[1,3]{1,0:T(1,128)S(1)}, f32[1,3]{1,0:T(1,128)}, u32[]{:S(2)}) copy-start(f32[1,3]{1,0:T(1,128)} %constant.21) | copy-start | bytes 40
  63.0 6.6 %collective-permute-start.5 = (f32[8,4,256]{2,1,0:T(4,128)S(1)}, f32[8,4,256]{2,1,0:T(4,128)S(1)}, u32[]{:S(2)}, u32[]{:S(2)}) collective-permute-start(f32[8,4,256]{2,1,0:T(4,128)S(1)} %fusion), channel_id=1, source_target_pairs={{0,1},{1,0},{2,3},{3,2},{4,5},{5,4},{6,7},{7,6},{8,9},{9,8},{10,11... | collective-permute-start | bytes 98312 | tf_op jit(solution)/shard_map/ppermute | solution.py:763

commit v6 on v5

--- a/solution.py
+++ b/solution.py
@@ -26,7 +26,7 @@
 FINE_PLANES = CX + 6
 COEF_PLANES = CX + 6
 PACK = 3 * 3 + 3 + 1
-BATCH = 32
+BATCH = 64
 UNROLL = 4
 F32 = jnp.float32
 BF16 = jnp.bfloat16
@@ -440,7 +440,7 @@
         for u in range(6):
             pick(6 * trip + u)
 
-    @pl.loop(0, slabs, unroll=16)
+    @pl.loop(0, slabs, unroll=32)
     def _(o):
         at = where_ref[o]
         tile = lax.shift_right_logical(at, 8)

time: 70.5 us -> 70.2 us (level)
  no operation moved by 1% of the time
where the time goes in v6:
time: 70.2 us; the launch traced here: 70 us
  starting transfers between devices  22.9 us (33%)
  blocking collectives  19.2 us (27%)
  Pallas kernels  14.9 us (21%)
  waiting for transfers between devices  9.16 us (13%)
  between operations  2.13 us (3%)
  local copies, waits for them, and re-layouts  0.85 us (1%)
  other arithmetic  0.75 us (1%)
    all_to_all x1, blocking collectives, body(): lax.all_to_all(picked, 'space', split_axis=0, concat_axis=0, tiled=True)  19.2 us
    pallas_call x1, Pallas kernels, body(): pl.pallas_call(fine_kernel, out_shape=(shaped(3, CX + 2, NY, NZ), shaped(...  6.71 us
    ppermute x1, starting transfers between devices, body(): last = lax.ppermute(near + got[1], 'load', [(i, i ^ 1) for i in range(4)])  5.69 us
    ppermute x1, starting transfers between devices, body(): got = lax.ppermute(far, 'load', [(i, i ^ 2) for i in range(4)])  5.44 us
    ppermute x1, waiting for transfers between devices, body(): met_second = lax.ppermute(send_second, 'space', second_pairs)  5.27 us
    ppermute x1, starting transfers between devices, body(): above = lax.ppermute(pack_low, 'space', backward)  5.23 us
    ppermute x1, starting transfers between devices, body(): met_second = lax.ppermute(send_second, 'space', second_pairs)  4.33 us
    pallas_call x1, Pallas kernels, body(): pl.pallas_call(coarse_kernel, grid=(1,), out_shape=(shaped(1, 3, CX, NY,...  2.52 us
  transfers between devices with their start and end apart: 6, of which 4 were waited for; matrix products, arithmetic and copies ran while one was open for 1% of the time, Pallas kernels for 4%

profile of v6, /device:TPU:3, one launch (start us, length us, event | category | flops | bytes accessed | tf_op | source)
XLA Modules:
  0.0 70.0 jit_solution(15635362727159182731)
XLA Ops:
  0.7 1.4 %pack.1 = (f32[13,16,256]{2,1,0:T(8,128)S(1)}, f32[13,16,256]{2,1,0:T(8,128)S(1)}, f32[4,8,128]{2,1,0:T(8,128)S(1)}, f32[8,16,256]{2,1,0:T(8,128)S(1)}) custom-call(s32[1,2]{1,0:T(1,128)} %material_hbm.1, f32[1,3,8,16,256]{4,3,2,1,0:T(8,128)} %force_ref.3, f32[8,16,256]{2,1,0:T(8,128)} %stiff_hbm.1), custom_call_target="tpu_custom_call" | custom-call | tf_op jit(solution)/shard_map/pack/pallas_call | solution.py:636
  2.0 1.7 %collective-permute-start = (f32[13,16,256]{2,1,0:T(8,128)S(1)}, f32[13,16,256]{2,1,0:T(8,128)S(1)}, u32[]{:S(2)}, u32[]{:S(2)}) collective-permute-start(f32[13,16,256]{2,1,0:T(8,128)S(1)} %get-tuple-element.28), channel_id=1, source_target_pairs={{0,4},{4,8},{8,12},{12,16},{16,20},{20,24},{24,28},{28,32},{32,36}... | collective-permute-start | bytes 638984 | tf_op jit(solution)/shard_map/ppermute | solution.py:657
  3.7 5.2 %collective-permute-start.1 = (f32[13,16,256]{2,1,0:T(8,128)S(1)}, f32[13,16,256]{2,1,0:T(8,128)S(1)}, u32[]{:S(2)}, u32[]{:S(2)}) collective-permute-start(f32[13,16,256]{2,1,0:T(8,128)S(1)} %get-tuple-element.29), channel_id=1, source_target_pairs={{4,0},{8,4},{12,8},{16,12},{20,16},{24,20},{28,24},{32,28},{36,32}... | collective-permute-start | bytes 638984 | tf_op jit(solution)/shard_map/ppermute | solution.py:658
  9.0 2.5 %plan.1 = (f32[64,256]{1,0:T(8,128)S(1)}, f32[64,256]{1,0:T(8,128)S(1)}, s32[65]{0:T(128)S(1)}, s32[72,256]{1,0:T(8,128)S(1)}, f32[8,16,256]{2,1,0:T(8,128)S(1)}...) custom-call(s32[1,64]{1,0:T(1,128)S(1)} %copy-done.3, ...), custom_call_target="tpu_custom_call" | custom-call | tf_op jit(solution)/shard_map/plan/pallas_call | solution.py:661
  11.5 2.4 %collective-permute-done.below_ref.coef_below_ref = f32[13,16,256]{2,1,0:T(8,128)S(1)} collective-permute-done((f32[13,16,256]{2,1,0:T(8,128)S(1)}, f32[13,16,256]{2,1,0:T(8,128)S(1)}, u32[]{:S(2)}, u32[]{:S(2)}) %collective-permute-start) | collective-permute-done | bytes 213024 | tf_op jit(solution)/shard_map/ppermute | solution.py:657
  13.9 0.7 collective-permute-done.1.above_ref.coef_above_ref
  14.5 6.7 %fine.1 = (f32[3,10,16,256]{3,2,1,0:T(8,128)S(1)}, f32[10,16,256]{2,1,0:T(8,128)S(1)}, f32[8,16,256]{2,1,0:T(8,128)S(1)}, f32[96,128]{1,0:T(8,128)S(1)}, f32[64,768]{1,0:T(8,128)S(1)}) custom-call(s32[1,64]{1,0:T(1,128)S(1)} %copy-done.3, s32[65]{0:T(128)S(1)} %get-tuple-element.27.where_ref, f32[1,3,8,16,256]{4,3,2,1,0:T(8,128)S(1)} %copy-done, ...), custom_call_target="tpu_custom_call" | custom-call | tf_op jit(solution)/shard_map/fine/pallas_call | solution.py:679
  21.3 0.2 copy.9
  21.5 19.2 %all_to_all.11 = f32[64,1,768]{2,1,0:T(1,128)S(1)} all-to-all(f32[64,1,768]{2,1,0:T(1,128)S(1)} %copy.9), channel_id=1, replica_groups=mesh['space'=64,'load'=4] {'space'}, dimensions={0} | all-to-all | bytes 393216 | tf_op jit(solution)/shard_map/all_to_all | solution.py:706
  40.7 1.8 %reflux.1 = (f32[3,4,8,128]{3,2,1,0:T(8,128)S(1)}, f32[3,4,8,128]{3,2,1,0:T(8,128)S(1)}, f32[3,4,8,128]{3,2,1,0:T(8,128)S(1)}) custom-call(f32[64,768]{1,0:T(8,128)S(1)} %bitcast.18, f32[64,256]{1,0:T(8,128)S(1)} %get-tuple-element.36.line_ref, f32[64,256]{1,0:T(8,128)S(1)} %get-tuple-element.37.column_ref, f32[96,128]{1,0:T(8,128)S(1)} %get-tuple-element.38.local_ref, ...), custom_call_target="tpu_custom_call" | custom-call | tf_op jit(solution)/shard_map/reflux/pallas_call | solution.py:714
  42.6 0.5 collective-permute-start.2
  43.1 4.3 %collective-permute-start.3 = (f32[3,4,8,128]{3,2,1,0:T(8,128)S(1)}, f32[3,4,8,128]{3,2,1,0:T(8,128)S(1)}, u32[]{:S(2)}, u32[]{:S(2)}) collective-permute-start(f32[3,4,8,128]{3,2,1,0:T(8,128)S(1)} %get-tuple-element.42), channel_id=1, source_target_pairs={{0,0},{4,8},{8,4},{12,16},{16,12},{20,24},{24,20},{28,32},{32,28},... | collective-permute-start | bytes 147464 | tf_op jit(solution)/shard_map/ppermute | solution.py:734
  47.4 0.0 collective-permute-done.2.first_ref
  47.4 5.3 %collective-permute-done.3.second_ref = f32[3,4,8,128]{3,2,1,0:T(8,128)S(1)} collective-permute-done((f32[3,4,8,128]{3,2,1,0:T(8,128)S(1)}, f32[3,4,8,128]{3,2,1,0:T(8,128)S(1)}, u32[]{:S(2)}, u32[]{:S(2)}) %collective-permute-start.3) | collective-permute-done | bytes 49184 | tf_op jit(solution)/shard_map/ppermute | solution.py:734
  52.7 2.5 %coarse.1 = (f32[1,3,8,16,256]{4,3,2,1,0:T(8,128)}, f32[8,4,256]{2,1,0:T(4,128)S(1)}, f32[8,4,256]{2,1,0:T(4,128)S(1)}, f32[2,8,4,256]{3,2,1,0:T(4,128)S(1)}) custom-call(f32[3,4,8,128]{3,2,1,0:T(8,128)S(1)} %get-tuple-element.40.source_ref, f32[3,4,8,128]{3,2,1,0:T(8,128)S(1)} %collective-permute-done.2.first_ref, ...), custom_call_target="tpu_custom_call" | custom-call | tf_op jit(solution)/shard_map/coarse/pallas_call | solution.py:738
  55.2 5.4 %collective-permute-start.4 = (f32[2,8,4,256]{3,2,1,0:T(4,128)S(1)}, f32[2,8,4,256]{3,2,1,0:T(4,128)S(1)}, u32[]{:S(2)}, u32[]{:S(2)}) collective-permute-start(f32[2,8,4,256]{3,2,1,0:T(4,128)S(1)} %get-tuple-element.48), channel_id=1, source_target_pairs={{0,2},{1,3},{2,0},{3,1},{4,6},{5,7},{6,4},{7,5},{8,10},{9,11},{10,... | collective-permute-start | bytes 196616 | tf_op jit(solution)/shard_map/ppermute | solution.py:762
  60.7 0.6 fusion.4
  62.6 0.0 collective-permute-done.4
  62.6 0.0 copy-start.5
  62.6 0.0 copy-start.6
  62.6 0.0 copy-start.7
  62.7 5.7 %collective-permute-start.5 = (f32[8,4,256]{2,1,0:T(4,128)S(1)}, f32[8,4,256]{2,1,0:T(4,128)S(1)}, u32[]{:S(2)}, u32[]{:S(2)}) collective-permute-start(f32[8,4,256]{2,1,0:T(4,128)S(1)} %fusion), channel_id=1, source_target_pairs={{0,1},{1,0},{2,3},{3,2},{4,5},{5,4},{6,7},{7,6},{8,9},{9,8},{10,11... | collective-permute-start | bytes 98312 | tf_op jit(solution)/shard_map/ppermute | solution.py:763
  68.4 0.8 %collective-permute-done.5 = f32[8,4,256]{2,1,0:T(4,128)S(1)} collective-permute-done((f32[8,4,256]{2,1,0:T(4,128)S(1)}, f32[8,4,256]{2,1,0:T(4,128)S(1)}, u32[]{:S(2)}, u32[]{:S(2)}) %collective-permute-start.5) | collective-permute-done | bytes 32800 | tf_op jit(solution)/shard_map/ppermute | solution.py:763
  69.2 0.7 %broadcast_multiply_fusion = f32[3,8,4,256]{3,2,1,0:T(4,128)} fusion(f32[8,4,256]{2,1,0:T(4,128)S(1)} %fusion.2, f32[3]{0:T(128)S(1)} %fusion.3), kind=kLoop, calls=%fused_computation.1 | loop fusion | flops 24576 | bytes 131084 | tf_op jit(solution)/shard_map/mul | solution.py:770
  (17 shorter events, 0.1 us)
Async XLA Ops:
  0.6 8.3 %copy-start = (f32[1,3,8,16,256]{4,3,2,1,0:T(8,128)S(1)}, f32[1,3,8,16,256]{4,3,2,1,0:T(8,128)}, u32[]{:S(2)}) copy-start(f32[1,3,8,16,256]{4,3,2,1,0:T(8,128)} %force_ref.3) | copy-start | bytes 1179652
  0.6 8.3 %copy-start.1 = (s32[1,64,256]{2,1,0:T(8,128)S(1)}, s32[1,64,256]{2,1,0:T(8,128)}, u32[]{:S(2)}) copy-start(s32[1,64,256]{2,1,0:T(8,128)} %source_ref.1) | copy-start | bytes 196612
  0.7 8.3 %copy-start.2 = (s32[1,64,256]{2,1,0:T(8,128)S(1)}, s32[1,64,256]{2,1,0:T(8,128)}, u32[]{:S(2)}) copy-start(s32[1,64,256]{2,1,0:T(8,128)} %target_ref.1) | copy-start | bytes 196612
  2.0 11.9 %collective-permute-start = (f32[13,16,256]{2,1,0:T(8,128)S(1)}, f32[13,16,256]{2,1,0:T(8,128)S(1)}, u32[]{:S(2)}, u32[]{:S(2)}) collective-permute-start(f32[13,16,256]{2,1,0:T(8,128)S(1)} %get-tuple-element.28), channel_id=1, source_target_pairs={{0,4},{4,8},{8,12},{12,16},{16,20},{20,24},{24,28},{28,32},{32,36}... | collective-permute-start | bytes 638984 | tf_op jit(solution)/shard_map/ppermute | solution.py:657
  3.7 5.2 %copy-start.3 = (s32[1,64]{1,0:T(1,128)S(1)}, s32[1,64]{1,0:T(1,128)}, u32[]{:S(2)}) copy-start(s32[1,64]{1,0:T(1,128)} %count_ref.3) | copy-start | bytes 772
  3.7 10.8 %collective-permute-start.1 = (f32[13,16,256]{2,1,0:T(8,128)S(1)}, f32[13,16,256]{2,1,0:T(8,128)S(1)}, u32[]{:S(2)}, u32[]{:S(2)}) collective-permute-start(f32[13,16,256]{2,1,0:T(8,128)S(1)} %get-tuple-element.29), channel_id=1, source_target_pairs={{4,0},{8,4},{12,8},{16,12},{20,16},{24,20},{28,24},{32,28},{36,32}... | collective-permute-start | bytes 638984 | tf_op jit(solution)/shard_map/ppermute | solution.py:658
  42.6 4.8 %collective-permute-start.2 = (f32[3,4,8,128]{3,2,1,0:T(8,128)S(1)}, f32[3,4,8,128]{3,2,1,0:T(8,128)S(1)}, u32[]{:S(2)}, u32[]{:S(2)}) collective-permute-start(f32[3,4,8,128]{3,2,1,0:T(8,128)S(1)} %get-tuple-element.41), channel_id=1, source_target_pairs={{0,4},{4,0},{8,12},{12,8},{16,20},{20,16},{24,28},{28,24},{32,36},... | collective-permute-start | bytes 147464 | tf_op jit(solution)/shard_map/ppermute | solution.py:735
  43.1 9.6 %collective-permute-start.3 = (f32[3,4,8,128]{3,2,1,0:T(8,128)S(1)}, f32[3,4,8,128]{3,2,1,0:T(8,128)S(1)}, u32[]{:S(2)}, u32[]{:S(2)}) collective-permute-start(f32[3,4,8,128]{3,2,1,0:T(8,128)S(1)} %get-tuple-element.42), channel_id=1, source_target_pairs={{0,0},{4,8},{8,4},{12,16},{16,12},{20,24},{24,20},{28,32},{32,28},... | collective-permute-start | bytes 147464 | tf_op jit(solution)/shard_map/ppermute | solution.py:734
  55.2 5.4 %copy-start.4 = (s32[1,2]{1,0:T(1,128)S(1)}, s32[1,2]{1,0:T(1,128)}, u32[]{:S(2)}) copy-start(s32[1,2]{1,0:T(1,128)} %material_hbm.1) | copy-start | bytes 28
  55.2 7.4 %collective-permute-start.4 = (f32[2,8,4,256]{3,2,1,0:T(4,128)S(1)}, f32[2,8,4,256]{3,2,1,0:T(4,128)S(1)}, u32[]{:S(2)}, u32[]{:S(2)}) collective-permute-start(f32[2,8,4,256]{3,2,1,0:T(4,128)S(1)} %get-tuple-element.48), channel_id=1, source_target_pairs={{0,2},{1,3},{2,0},{3,1},{4,6},{5,7},{6,4},{7,5},{8,10},{9,11},{10,... | collective-permute-start | bytes 196616 | tf_op jit(solution)/shard_map/ppermute | solution.py:762
  62.6 5.7 %copy-start.5 = (f32[1,3]{1,0:T(1,128)S(1)}, f32[1,3]{1,0:T(1,128)}, u32[]{:S(2)}) copy-start(f32[1,3]{1,0:T(1,128)} %constant.19) | copy-start | bytes 40
  62.6 5.7 %copy-start.6 = (f32[1,3]{1,0:T(1,128)S(1)}, f32[1,3]{1,0:T(1,128)}, u32[]{:S(2)}) copy-start(f32[1,3]{1,0:T(1,128)} %constant.20) | copy-start | bytes 40
  62.6 5.7 %copy-start.7 = (f32[1,3]{1,0:T(1,128)S(1)}, f32[1,3]{1,0:T(1,128)}, u32[]{:S(2)}) copy-start(f32[1,3]{1,0:T(1,128)} %constant.21) | copy-start | bytes 40
  62.7 6.5 %collective-permute-start.5 = (f32[8,4,256]{2,1,0:T(4,128)S(1)}, f32[8,4,256]{2,1,0:T(4,128)S(1)}, u32[]{:S(2)}, u32[]{:S(2)}) collective-permute-start(f32[8,4,256]{2,1,0:T(4,128)S(1)} %fusion), channel_id=1, source_target_pairs={{0,1},{1,0},{2,3},{3,2},{4,5},{5,4},{6,7},{7,6},{8,9},{9,8},{10,11... | collective-permute-start | bytes 98312 | tf_op jit(solution)/shard_map/ppermute | solution.py:763

commit v7 on v6

--- a/solution.py
+++ b/solution.py
@@ -332,7 +332,7 @@
         for p in range(3, CX - 3):
             smooth_ref[c, p + 1] = inner_third_ref[c, p - 3]
 
-    @pl.loop(0, 6, unroll=2)
+    @pl.loop(0, 6, unroll=6)
     def _(i):
         p = 1 + i + jnp.where(i >= 3, CX - 2, 0)
         d = plane(diagonal(sh, *[tiles(coef[p + o]) for o in (-1, 0, 1)]))
@@ -600,7 +600,7 @@
 
     sh = Shifts(4, True)
 
-    @pl.loop(1, CX + 1, unroll=UNROLL)
+    @pl.loop(1, CX + 1, unroll=8)
     def _(p):
         planes = [[tiles(field[c, p + o]) for c in range(3)] for o in (-1, 0, 1)]
         factors = [tiles(coef_ref[p + o]) for o in (-1, 0, 1)]

time: 70.2 us -> 69.9 us (level)
  no operation moved by 1% of the time
where the time goes in v7:
time: 69.9 us; the launch traced here: 69.7 us
  starting transfers between devices  22.9 us (33%)
  blocking collectives  19.2 us (27%)
  Pallas kernels  14.7 us (21%)
  waiting for transfers between devices  9.17 us (13%)
  between operations  2.13 us (3%)
  local copies, waits for them, and re-layouts  0.85 us (1%)
  other arithmetic  0.75 us (1%)
    all_to_all x1, blocking collectives, body(): lax.all_to_all(picked, 'space', split_axis=0, concat_axis=0, tiled=True)  19.2 us
    pallas_call x1, Pallas kernels, body(): pl.pallas_call(fine_kernel, out_shape=(shaped(3, CX + 2, NY, NZ), shaped(...  6.46 us
    ppermute x1, starting transfers between devices, body(): last = lax.ppermute(near + got[1], 'load', [(i, i ^ 1) for i in range(4)])  5.66 us
    ppermute x1, starting transfers between devices, body(): got = lax.ppermute(far, 'load', [(i, i ^ 2) for i in range(4)])  5.46 us
    ppermute x1, waiting for transfers between devices, body(): met_second = lax.ppermute(send_second, 'space', second_pairs)  5.28 us
    ppermute x1, starting transfers between devices, body(): above = lax.ppermute(pack_low, 'space', backward)  5.23 us
    ppermute x1, starting transfers between devices, body(): met_second = lax.ppermute(send_second, 'space', second_pairs)  4.33 us
    pallas_call x1, Pallas kernels, body(): pl.pallas_call(coarse_kernel, grid=(1,), out_shape=(shaped(1, 3, CX, NY,...  2.52 us
  transfers between devices with their start and end apart: 6, of which 4 were waited for; matrix products, arithmetic and copies ran while one was open for 1% of the time, Pallas kernels for 4%

profile of v7, /device:TPU:3, one launch (start us, length us, event | category | flops | bytes accessed | tf_op | source)
XLA Modules:
  0.0 69.7 jit_solution(9694625451584721058)
XLA Ops:
  0.7 1.4 %pack.1 = (f32[13,16,256]{2,1,0:T(8,128)S(1)}, f32[13,16,256]{2,1,0:T(8,128)S(1)}, f32[4,8,128]{2,1,0:T(8,128)S(1)}, f32[8,16,256]{2,1,0:T(8,128)S(1)}) custom-call(s32[1,2]{1,0:T(1,128)} %material_hbm.1, f32[1,3,8,16,256]{4,3,2,1,0:T(8,128)} %force_ref.3, f32[8,16,256]{2,1,0:T(8,128)} %stiff_hbm.1), custom_call_target="tpu_custom_call" | custom-call | tf_op jit(solution)/shard_map/pack/pallas_call | solution.py:636
  2.0 1.7 %collective-permute-start = (f32[13,16,256]{2,1,0:T(8,128)S(1)}, f32[13,16,256]{2,1,0:T(8,128)S(1)}, u32[]{:S(2)}, u32[]{:S(2)}) collective-permute-start(f32[13,16,256]{2,1,0:T(8,128)S(1)} %get-tuple-element.28), channel_id=1, source_target_pairs={{0,4},{4,8},{8,12},{12,16},{16,20},{20,24},{24,28},{28,32},{32,36}... | collective-permute-start | bytes 638984 | tf_op jit(solution)/shard_map/ppermute | solution.py:657
  3.7 5.2 %collective-permute-start.1 = (f32[13,16,256]{2,1,0:T(8,128)S(1)}, f32[13,16,256]{2,1,0:T(8,128)S(1)}, u32[]{:S(2)}, u32[]{:S(2)}) collective-permute-start(f32[13,16,256]{2,1,0:T(8,128)S(1)} %get-tuple-element.29), channel_id=1, source_target_pairs={{4,0},{8,4},{12,8},{16,12},{20,16},{24,20},{28,24},{32,28},{36,32}... | collective-permute-start | bytes 638984 | tf_op jit(solution)/shard_map/ppermute | solution.py:658
  9.0 2.5 %plan.1 = (f32[64,256]{1,0:T(8,128)S(1)}, f32[64,256]{1,0:T(8,128)S(1)}, s32[65]{0:T(128)S(1)}, s32[72,256]{1,0:T(8,128)S(1)}, f32[8,16,256]{2,1,0:T(8,128)S(1)}...) custom-call(s32[1,64]{1,0:T(1,128)S(1)} %copy-done.3, ...), custom_call_target="tpu_custom_call" | custom-call | tf_op jit(solution)/shard_map/plan/pallas_call | solution.py:661
  11.5 2.4 %collective-permute-done.below_ref.coef_below_ref = f32[13,16,256]{2,1,0:T(8,128)S(1)} collective-permute-done((f32[13,16,256]{2,1,0:T(8,128)S(1)}, f32[13,16,256]{2,1,0:T(8,128)S(1)}, u32[]{:S(2)}, u32[]{:S(2)}) %collective-permute-start) | collective-permute-done | bytes 213024 | tf_op jit(solution)/shard_map/ppermute | solution.py:657
  13.9 0.7 collective-permute-done.1.above_ref.coef_above_ref
  14.5 6.5 %fine.1 = (f32[3,10,16,256]{3,2,1,0:T(8,128)S(1)}, f32[10,16,256]{2,1,0:T(8,128)S(1)}, f32[8,16,256]{2,1,0:T(8,128)S(1)}, f32[96,128]{1,0:T(8,128)S(1)}, f32[64,768]{1,0:T(8,128)S(1)}) custom-call(s32[1,64]{1,0:T(1,128)S(1)} %copy-done.3, s32[65]{0:T(128)S(1)} %get-tuple-element.27.where_ref, f32[1,3,8,16,256]{4,3,2,1,0:T(8,128)S(1)} %copy-done, ...), custom_call_target="tpu_custom_call" | custom-call | tf_op jit(solution)/shard_map/fine/pallas_call | solution.py:679
  21.0 0.2 copy.9
  21.2 19.2 %all_to_all.11 = f32[64,1,768]{2,1,0:T(1,128)S(1)} all-to-all(f32[64,1,768]{2,1,0:T(1,128)S(1)} %copy.9), channel_id=1, replica_groups=mesh['space'=64,'load'=4] {'space'}, dimensions={0} | all-to-all | bytes 393216 | tf_op jit(solution)/shard_map/all_to_all | solution.py:706
  40.5 1.8 %reflux.1 = (f32[3,4,8,128]{3,2,1,0:T(8,128)S(1)}, f32[3,4,8,128]{3,2,1,0:T(8,128)S(1)}, f32[3,4,8,128]{3,2,1,0:T(8,128)S(1)}) custom-call(f32[64,768]{1,0:T(8,128)S(1)} %bitcast.18, f32[64,256]{1,0:T(8,128)S(1)} %get-tuple-element.36.line_ref, f32[64,256]{1,0:T(8,128)S(1)} %get-tuple-element.37.column_ref, f32[96,128]{1,0:T(8,128)S(1)} %get-tuple-element.38.local_ref, ...), custom_call_target="tpu_custom_call" | custom-call | tf_op jit(solution)/shard_map/reflux/pallas_call | solution.py:714
  42.3 0.5 collective-permute-start.2
  42.8 4.3 %collective-permute-start.3 = (f32[3,4,8,128]{3,2,1,0:T(8,128)S(1)}, f32[3,4,8,128]{3,2,1,0:T(8,128)S(1)}, u32[]{:S(2)}, u32[]{:S(2)}) collective-permute-start(f32[3,4,8,128]{3,2,1,0:T(8,128)S(1)} %get-tuple-element.42), channel_id=1, source_target_pairs={{0,0},{4,8},{8,4},{12,16},{16,12},{20,24},{24,20},{28,32},{32,28},... | collective-permute-start | bytes 147464 | tf_op jit(solution)/shard_map/ppermute | solution.py:734
  47.1 0.0 collective-permute-done.2.first_ref
  47.2 5.3 %collective-permute-done.3.second_ref = f32[3,4,8,128]{3,2,1,0:T(8,128)S(1)} collective-permute-done((f32[3,4,8,128]{3,2,1,0:T(8,128)S(1)}, f32[3,4,8,128]{3,2,1,0:T(8,128)S(1)}, u32[]{:S(2)}, u32[]{:S(2)}) %collective-permute-start.3) | collective-permute-done | bytes 49184 | tf_op jit(solution)/shard_map/ppermute | solution.py:734
  52.4 2.5 %coarse.1 = (f32[1,3,8,16,256]{4,3,2,1,0:T(8,128)}, f32[8,4,256]{2,1,0:T(4,128)S(1)}, f32[8,4,256]{2,1,0:T(4,128)S(1)}, f32[2,8,4,256]{3,2,1,0:T(4,128)S(1)}) custom-call(f32[3,4,8,128]{3,2,1,0:T(8,128)S(1)} %get-tuple-element.40.source_ref, f32[3,4,8,128]{3,2,1,0:T(8,128)S(1)} %collective-permute-done.2.first_ref, ...), custom_call_target="tpu_custom_call" | custom-call | tf_op jit(solution)/shard_map/coarse/pallas_call | solution.py:738
  54.9 5.5 %collective-permute-start.4 = (f32[2,8,4,256]{3,2,1,0:T(4,128)S(1)}, f32[2,8,4,256]{3,2,1,0:T(4,128)S(1)}, u32[]{:S(2)}, u32[]{:S(2)}) collective-permute-start(f32[2,8,4,256]{3,2,1,0:T(4,128)S(1)} %get-tuple-element.48), channel_id=1, source_target_pairs={{0,2},{1,3},{2,0},{3,1},{4,6},{5,7},{6,4},{7,5},{8,10},{9,11},{10,... | collective-permute-start | bytes 196616 | tf_op jit(solution)/shard_map/ppermute | solution.py:762
  60.4 0.6 fusion.4
  62.3 0.0 collective-permute-done.4
  62.4 0.0 copy-start.5
  62.4 0.0 copy-start.6
  62.4 0.0 copy-start.7
  62.4 5.7 %collective-permute-start.5 = (f32[8,4,256]{2,1,0:T(4,128)S(1)}, f32[8,4,256]{2,1,0:T(4,128)S(1)}, u32[]{:S(2)}, u32[]{:S(2)}) collective-permute-start(f32[8,4,256]{2,1,0:T(4,128)S(1)} %fusion), channel_id=1, source_target_pairs={{0,1},{1,0},{2,3},{3,2},{4,5},{5,4},{6,7},{7,6},{8,9},{9,8},{10,11... | collective-permute-start | bytes 98312 | tf_op jit(solution)/shard_map/ppermute | solution.py:763
  68.1 0.8 %collective-permute-done.5 = f32[8,4,256]{2,1,0:T(4,128)S(1)} collective-permute-done((f32[8,4,256]{2,1,0:T(4,128)S(1)}, f32[8,4,256]{2,1,0:T(4,128)S(1)}, u32[]{:S(2)}, u32[]{:S(2)}) %collective-permute-start.5) | collective-permute-done | bytes 32800 | tf_op jit(solution)/shard_map/ppermute | solution.py:763
  69.0 0.7 %broadcast_multiply_fusion = f32[3,8,4,256]{3,2,1,0:T(4,128)} fusion(f32[8,4,256]{2,1,0:T(4,128)S(1)} %fusion.2, f32[3]{0:T(128)S(1)} %fusion.3), kind=kLoop, calls=%fused_computation.1 | loop fusion | flops 24576 | bytes 131084 | tf_op jit(solution)/shard_map/mul | solution.py:770
  (17 shorter events, 0.1 us)
Async XLA Ops:
  0.6 8.3 %copy-start = (f32[1,3,8,16,256]{4,3,2,1,0:T(8,128)S(1)}, f32[1,3,8,16,256]{4,3,2,1,0:T(8,128)}, u32[]{:S(2)}) copy-start(f32[1,3,8,16,256]{4,3,2,1,0:T(8,128)} %force_ref.3) | copy-start | bytes 1179652
  0.6 8.3 %copy-start.1 = (s32[1,64,256]{2,1,0:T(8,128)S(1)}, s32[1,64,256]{2,1,0:T(8,128)}, u32[]{:S(2)}) copy-start(s32[1,64,256]{2,1,0:T(8,128)} %source_ref.1) | copy-start | bytes 196612
  0.7 8.3 %copy-start.2 = (s32[1,64,256]{2,1,0:T(8,128)S(1)}, s32[1,64,256]{2,1,0:T(8,128)}, u32[]{:S(2)}) copy-start(s32[1,64,256]{2,1,0:T(8,128)} %target_ref.1) | copy-start | bytes 196612
  2.0 11.9 %collective-permute-start = (f32[13,16,256]{2,1,0:T(8,128)S(1)}, f32[13,16,256]{2,1,0:T(8,128)S(1)}, u32[]{:S(2)}, u32[]{:S(2)}) collective-permute-start(f32[13,16,256]{2,1,0:T(8,128)S(1)} %get-tuple-element.28), channel_id=1, source_target_pairs={{0,4},{4,8},{8,12},{12,16},{16,20},{20,24},{24,28},{28,32},{32,36}... | collective-permute-start | bytes 638984 | tf_op jit(solution)/shard_map/ppermute | solution.py:657
  3.7 5.2 %copy-start.3 = (s32[1,64]{1,0:T(1,128)S(1)}, s32[1,64]{1,0:T(1,128)}, u32[]{:S(2)}) copy-start(s32[1,64]{1,0:T(1,128)} %count_ref.3) | copy-start | bytes 772
  3.7 10.8 %collective-permute-start.1 = (f32[13,16,256]{2,1,0:T(8,128)S(1)}, f32[13,16,256]{2,1,0:T(8,128)S(1)}, u32[]{:S(2)}, u32[]{:S(2)}) collective-permute-start(f32[13,16,256]{2,1,0:T(8,128)S(1)} %get-tuple-element.29), channel_id=1, source_target_pairs={{4,0},{8,4},{12,8},{16,12},{20,16},{24,20},{28,24},{32,28},{36,32}... | collective-permute-start | bytes 638984 | tf_op jit(solution)/shard_map/ppermute | solution.py:658
  42.3 4.9 %collective-permute-start.2 = (f32[3,4,8,128]{3,2,1,0:T(8,128)S(1)}, f32[3,4,8,128]{3,2,1,0:T(8,128)S(1)}, u32[]{:S(2)}, u32[]{:S(2)}) collective-permute-start(f32[3,4,8,128]{3,2,1,0:T(8,128)S(1)} %get-tuple-element.41), channel_id=1, source_target_pairs={{0,4},{4,0},{8,12},{12,8},{16,20},{20,16},{24,28},{28,24},{32,36},... | collective-permute-start | bytes 147464 | tf_op jit(solution)/shard_map/ppermute | solution.py:735
  42.8 9.6 %collective-permute-start.3 = (f32[3,4,8,128]{3,2,1,0:T(8,128)S(1)}, f32[3,4,8,128]{3,2,1,0:T(8,128)S(1)}, u32[]{:S(2)}, u32[]{:S(2)}) collective-permute-start(f32[3,4,8,128]{3,2,1,0:T(8,128)S(1)} %get-tuple-element.42), channel_id=1, source_target_pairs={{0,0},{4,8},{8,4},{12,16},{16,12},{20,24},{24,20},{28,32},{32,28},... | collective-permute-start | bytes 147464 | tf_op jit(solution)/shard_map/ppermute | solution.py:734
  54.9 5.5 %copy-start.4 = (s32[1,2]{1,0:T(1,128)S(1)}, s32[1,2]{1,0:T(1,128)}, u32[]{:S(2)}) copy-start(s32[1,2]{1,0:T(1,128)} %material_hbm.1) | copy-start | bytes 28
  54.9 7.4 %collective-permute-start.4 = (f32[2,8,4,256]{3,2,1,0:T(4,128)S(1)}, f32[2,8,4,256]{3,2,1,0:T(4,128)S(1)}, u32[]{:S(2)}, u32[]{:S(2)}) collective-permute-start(f32[2,8,4,256]{3,2,1,0:T(4,128)S(1)} %get-tuple-element.48), channel_id=1, source_target_pairs={{0,2},{1,3},{2,0},{3,1},{4,6},{5,7},{6,4},{7,5},{8,10},{9,11},{10,... | collective-permute-start | bytes 196616 | tf_op jit(solution)/shard_map/ppermute | solution.py:762
  62.4 5.7 %copy-start.5 = (f32[1,3]{1,0:T(1,128)S(1)}, f32[1,3]{1,0:T(1,128)}, u32[]{:S(2)}) copy-start(f32[1,3]{1,0:T(1,128)} %constant.19) | copy-start | bytes 40
  62.4 5.7 %copy-start.6 = (f32[1,3]{1,0:T(1,128)S(1)}, f32[1,3]{1,0:T(1,128)}, u32[]{:S(2)}) copy-start(f32[1,3]{1,0:T(1,128)} %constant.20) | copy-start | bytes 40
  62.4 5.7 %copy-start.7 = (f32[1,3]{1,0:T(1,128)S(1)}, f32[1,3]{1,0:T(1,128)}, u32[]{:S(2)}) copy-start(f32[1,3]{1,0:T(1,128)} %constant.21) | copy-start | bytes 40
  62.4 6.5 %collective-permute-start.5 = (f32[8,4,256]{2,1,0:T(4,128)S(1)}, f32[8,4,256]{2,1,0:T(4,128)S(1)}, u32[]{:S(2)}, u32[]{:S(2)}) collective-permute-start(f32[8,4,256]{2,1,0:T(4,128)S(1)} %fusion), channel_id=1, source_target_pairs={{0,1},{1,0},{2,3},{3,2},{4,5},{5,4},{6,7},{7,6},{8,9},{9,8},{10,11... | collective-permute-start | bytes 98312 | tf_op jit(solution)/shard_map/ppermute | solution.py:763
